TPU v7x, 32 devices: a whole 2x2x4 slice. The times are simulated.
32 devices in a mesh: ctx: 8 (over z, x), fsdp: 4 (over y, core).
Axes of the slice: x: 2, y: 2, z: 4, core: 2. Of those that a mesh axis runs over, the one named last changes fastest.
Arguments:
- inputs: bfloat16 [8, 1024, 768], P('fsdp', 'ctx'), may hold values from -6 to 6
- cotangent: bfloat16 [8, 1024, 768], P('fsdp', 'ctx'), may hold values from -6 to 6
- lengths: int32 [8], P('fsdp'), may hold values from 256 to 1024, as said below
- w_query: bfloat16 [768, 768], P('fsdp'), may hold values from -0.21875 to 0.21875
- b_query: bfloat16 [768], P('fsdp'), may hold values from -3 to 3
- w_key: bfloat16 [768, 768], P('fsdp'), may hold values from -0.21875 to 0.21875
- w_value: bfloat16 [768, 768], P('fsdp'), may hold values from -0.21875 to 0.21875
- b_value: bfloat16 [768], P('fsdp'), may hold values from -0.119628906 to 0.119628906
- w_output: bfloat16 [768, 768], P('fsdp'), may hold values from -3.5 to 3.5
- b_output: bfloat16 [768], P('fsdp'), may hold values from -2 to 2
- gain_one: bfloat16 [768], P('fsdp'), may hold values from 0.5 to 1.5
- bias_one: bfloat16 [768], P('fsdp'), may hold values from -1.1953125 to 1.1953125
- w_inner: bfloat16 [768, 3072], P('fsdp'), may hold values from -0.21875 to 0.21875
- b_inner: bfloat16 [3072], P('fsdp'), may hold values from -3 to 3
- w_outer: bfloat16 [3072, 768], P('fsdp'), may hold values from -0.109375 to 0.109375
- b_outer: bfloat16 [768], P('fsdp'), may hold values from -2 to 2
- gain_two: bfloat16 [768], P('fsdp'), may hold values from 0.5 to 1.5
- bias_two: bfloat16 [768], P('fsdp'), may hold values from -1.1953125 to 1.1953125
Outputs:
- outputs: bfloat16 [8, 1024, 768], P('fsdp', 'ctx')
- input_grad: float32 [8, 1024, 768], P('fsdp', 'ctx')
- grad_w_query: float32 [768, 768], P('fsdp')
- grad_b_query: float32 [768], P('fsdp')
- grad_w_key: float32 [768, 768], P('fsdp')
- grad_w_value: float32 [768, 768], P('fsdp')
- grad_b_value: float32 [768], P('fsdp')
- grad_w_output: float32 [768, 768], P('fsdp')
- grad_b_output: float32 [768], P('fsdp')
- grad_gain_one: float32 [768], P('fsdp')
- grad_bias_one: float32 [768], P('fsdp')
- grad_w_inner: float32 [768, 3072], P('fsdp')
- grad_b_inner: float32 [3072], P('fsdp')
- grad_w_outer: float32 [3072, 768], P('fsdp')
- grad_b_outer: float32 [768], P('fsdp')
- grad_gain_two: float32 [768], P('fsdp')
- grad_bias_two: float32 [768], P('fsdp')
Inputs may be any that keep to these rules, and one draw needn't show every extreme that they name: Slot s has 1024 positions, of which the first lengths[s] are real tokens; in every draw some slot is full.
All inputs are finite; a program needn't handle non-finite values.
Results may differ from a plain program's by a relative error of at most 0.024.
Values may be sent and summed in bfloat16 or wider, within the bound.
No kernel may reach another device: no remote copies, remote signals or barrier semaphores. Data moves between devices by JAX's collectives and lax.ppermute only.
A program may use at most 192 MiB of HBM per device.

v0:
```python
from functools import partial

import jax
import jax.numpy as jnp
from jax import lax
from jax.sharding import PartitionSpec as P

D = 768
H = 12
HD = 64
SEQ_MB = 1
MICRO = 2


EPSILON = 1e-05
NEG_FILL = -1e30
SCALE = 0.125
ROOT_HALF = 0.7071067811865476
INV_ROOT_TAU = 0.3989422804014327
key_block = 512


def matmul(left_side, right_side):
    return jnp.dot(left_side, right_side, preferred_element_type=jnp.float32)


def left_product(left_side, right_side):
    return lax.dot_general(
        left_side, right_side, (((0,), (0,)), ((), ())), preferred_element_type=jnp.float32
    )


def right_product(left_side, right_side):
    return lax.dot_general(
        left_side, right_side, (((1,), (1,)), ((), ())), preferred_element_type=jnp.float32
    )


def split_heads(token_rows):
    return token_rows.reshape(token_rows.shape[0], token_rows.shape[1], H, HD)


def head_scores(query_rows, key_rows):
    return (
        jnp.einsum(
            "bqhd,bkhd->bhqk",
            split_heads(query_rows),
            split_heads(key_rows),
            preferred_element_type=jnp.float32,
        )
        * SCALE
    )


def live_mask(seq_lens, first_pos, num_rows):
    return (first_pos + lax.iota(jnp.int32, num_rows))[None, :] < seq_lens[:, None]


def layer_norm(resid, norm_gain, norm_bias):
    row_mean = jnp.mean(resid, axis=-1, keepdims=True)
    centered = resid - row_mean
    inv_std = lax.rsqrt(jnp.mean(centered * centered, axis=-1, keepdims=True) + EPSILON)
    normed = centered * inv_std
    return (normed * norm_gain + norm_bias, normed, inv_std)


def norm_back(grad_out, normed, inv_std, norm_gain):
    grad_norm = grad_out * norm_gain
    grad_in = inv_std * (
        grad_norm
        - jnp.mean(grad_norm, axis=-1, keepdims=True)
        - normed * jnp.mean(grad_norm * normed, axis=-1, keepdims=True)
    )
    return (grad_in, jnp.sum(grad_out * normed, axis=0), jnp.sum(grad_out, axis=0))


def gelu_exact(pre_act):
    return 0.5 * pre_act * (1.0 + lax.erf(pre_act * ROOT_HALF))


def gelu_slope(pre_act):
    return 0.5 * (1.0 + lax.erf(pre_act * ROOT_HALF)) + pre_act * INV_ROOT_TAU * jnp.exp(
        -0.5 * pre_act * pre_act
    )


def in_blocks(step_fn, running, pieces):
    num_rows = pieces[0].shape[1]

    def advance(block_index, current):
        offset = block_index * key_block
        sliced = tuple(
            (lax.dynamic_slice_in_dim(member, offset, key_block, 1) for member in pieces)
        )
        return step_fn(current, sliced, offset)

    return lax.fori_loop(0, num_rows // key_block, advance, running)


def attend_step(running, sliced, first_pos, queries, seq_lens, skip_empty):
    key_rows, value_rows = sliced
    live_keys = live_mask(seq_lens, first_pos, key_rows.shape[1])
    run_max, run_sum, run_out = running
    key_mask = live_keys[:, None, None, :]
    scores = jnp.where(key_mask, head_scores(queries, key_rows), NEG_FILL)
    new_max = jnp.maximum(run_max, jnp.max(scores, axis=-1))
    weights = jnp.where(key_mask, jnp.exp(scores - new_max[..., None]), 0.0)
    rescale = jnp.exp(run_max - new_max)
    new_sum = run_sum * rescale + jnp.sum(weights, axis=-1)
    new_out = run_out * rescale[..., None] + jnp.einsum(
        "bhqk,bkhd->bhqd",
        weights.astype(jnp.bfloat16),
        split_heads(value_rows),
        preferred_element_type=jnp.float32,
    )
    return (new_max, new_sum, new_out)


def query_grad_step(
    running,
    sliced,
    first_pos,
    queries,
    grad_context,
    log_total,
    row_delta,
    seq_lens,
    live_queries,
    skip_empty,
):
    key_rows, value_rows = sliced
    live_keys = live_mask(seq_lens, first_pos, key_rows.shape[1])
    key_mask = live_keys[:, None, None, :]
    probabilities = jnp.where(
        key_mask, jnp.exp(head_scores(queries, key_rows) - log_total[..., None]), 0.0
    )
    grad_probs = jnp.einsum(
        "bqhd,bkhd->bhqk",
        split_heads(grad_context),
        split_heads(value_rows),
        preferred_element_type=jnp.float32,
    )
    grad_scores = (probabilities * (grad_probs - row_delta[..., None])).astype(jnp.bfloat16)
    return running + jnp.einsum(
        "bhqk,bkhd->bqhd", grad_scores, split_heads(key_rows), preferred_element_type=jnp.float32
    )


def key_grad_step(
    running,
    sliced,
    first_pos,
    key_rows,
    value_rows,
    stat_total,
    stat_delta,
    seq_lens,
    live_keys,
    skip_empty,
):
    query_rows, grad_rows = sliced
    num_rows = query_rows.shape[1]
    grad_k, grad_v = running
    log_total = lax.dynamic_slice_in_dim(stat_total, first_pos, num_rows, 1).transpose(0, 2, 1)
    row_delta = lax.dynamic_slice_in_dim(stat_delta, first_pos, num_rows, 1).transpose(0, 2, 1)
    key_mask = live_keys[:, None, None, :]
    probabilities = jnp.where(
        key_mask, jnp.exp(head_scores(query_rows, key_rows) - log_total[..., None]), 0.0
    )
    grad_probs = jnp.einsum(
        "bqhd,bkhd->bhqk",
        split_heads(grad_rows),
        split_heads(value_rows),
        preferred_element_type=jnp.float32,
    )
    grad_scores = (probabilities * (grad_probs - row_delta[..., None])).astype(jnp.bfloat16)
    grad_v = grad_v + jnp.einsum(
        "bhqk,bqhd->bkhd",
        probabilities.astype(jnp.bfloat16),
        split_heads(grad_rows),
        preferred_element_type=jnp.float32,
    )
    grad_k = grad_k + jnp.einsum(
        "bhqk,bqhd->bkhd", grad_scores, split_heads(query_rows), preferred_element_type=jnp.float32
    )
    return (grad_k, grad_v)


def body(
    inputs,
    cotangent,
    lengths,
    w_query,
    b_query,
    w_key,
    w_value,
    b_value,
    w_output,
    b_output,
    gain_one,
    bias_one,
    w_inner,
    b_inner,
    w_outer,
    b_outer,
    gain_two,
    bias_two,
):
    gathered = (
        lax.all_gather(w_query, "fsdp", axis=0, tiled=True),
        lax.all_gather(b_query, "fsdp", axis=0, tiled=True),
        lax.all_gather(w_key, "fsdp", axis=0, tiled=True),
        lax.all_gather(w_value, "fsdp", axis=0, tiled=True),
        lax.all_gather(b_value, "fsdp", axis=0, tiled=True),
        lax.all_gather(w_output, "fsdp", axis=0, tiled=True),
        lax.all_gather(b_output, "fsdp", axis=0, tiled=True),
        lax.all_gather(gain_one, "fsdp", axis=0, tiled=True),
        lax.all_gather(bias_one, "fsdp", axis=0, tiled=True),
        lax.all_gather(w_inner, "fsdp", axis=0, tiled=True),
        lax.all_gather(b_inner, "fsdp", axis=0, tiled=True),
        lax.all_gather(w_outer, "fsdp", axis=0, tiled=True),
        lax.all_gather(b_outer, "fsdp", axis=0, tiled=True),
        lax.all_gather(gain_two, "fsdp", axis=0, tiled=True),
        lax.all_gather(bias_two, "fsdp", axis=0, tiled=True),
    )
    (
        query_weight,
        query_bias,
        key_weight,
        value_weight,
        value_bias,
        out_weight,
        out_bias,
        gain_first,
        shift_first,
        inner_weight,
        inner_bias,
        outer_weight,
        outer_bias,
        gain_second,
        shift_second,
    ) = gathered
    joint_weight = jnp.concatenate([query_weight, key_weight, value_weight], axis=1)
    joint_bias = jnp.concatenate(
        [
            query_bias.astype(jnp.float32),
            jnp.zeros((D,), jnp.float32),
            value_bias.astype(jnp.float32),
        ]
    )
    out_bias_f = out_bias.astype(jnp.float32)
    inner_bias_f = inner_bias.astype(jnp.float32)
    outer_bias_f = outer_bias.astype(jnp.float32)
    gain_first_f = gain_first.astype(jnp.float32)
    shift_first_f = shift_first.astype(jnp.float32)
    gain_second_f = gain_second.astype(jnp.float32)
    shift_second_f = shift_second.astype(jnp.float32)
    seq_dev = inputs.shape[1]
    row_count = SEQ_MB * seq_dev
    positions = lax.axis_index("ctx") * seq_dev + lax.iota(jnp.int32, seq_dev)
    accum = None
    out_list = []
    grad_list = []
    for micro_index in range(MICRO):
        first_seq = micro_index * SEQ_MB
        seq_lens = lengths[first_seq : first_seq + SEQ_MB]
        token_rows = inputs[first_seq : first_seq + SEQ_MB].reshape(row_count, D)
        grad_rows = (
            cotangent[first_seq : first_seq + SEQ_MB].reshape(row_count, D).astype(jnp.float32)
        )
        query_ok = positions[None, :] < seq_lens[:, None]
        row_keep = query_ok.reshape(row_count, 1).astype(jnp.float32)
        projected = (matmul(token_rows, joint_weight) + joint_bias).astype(jnp.bfloat16)
        queries = projected[:, :D].reshape(SEQ_MB, seq_dev, D)
        keys_local = projected[:, D : 2 * D].reshape(SEQ_MB, seq_dev, D)
        values_local = projected[:, 2 * D :].reshape(SEQ_MB, seq_dev, D)
        start_state = (
            jnp.full((SEQ_MB, H, seq_dev), NEG_FILL, jnp.float32),
            jnp.zeros((SEQ_MB, H, seq_dev), jnp.float32),
            jnp.zeros((SEQ_MB, H, seq_dev, HD), jnp.float32),
        )
        attend_fn = partial(attend_step, queries=queries, seq_lens=seq_lens, skip_empty=False)
        run_max, run_sum, run_out = in_blocks(
            attend_fn,
            start_state,
            (
                lax.all_gather(keys_local, "ctx", axis=1, tiled=True),
                lax.all_gather(values_local, "ctx", axis=1, tiled=True),
            ),
        )
        attended = run_out / run_sum[..., None]
        log_total = run_max + jnp.log(run_sum)
        context = attended.transpose(0, 2, 1, 3).reshape(row_count, D).astype(jnp.bfloat16)
        first_sum = token_rows.astype(jnp.float32) + matmul(context, out_weight) + out_bias_f
        hidden, normed_one, inv_one = layer_norm(first_sum, gain_first_f, shift_first_f)
        hidden_low = hidden.astype(jnp.bfloat16)
        inner_pre = matmul(hidden_low, inner_weight) + inner_bias_f
        activated = gelu_exact(inner_pre).astype(jnp.bfloat16)
        outer_out = matmul(activated, outer_weight) + outer_bias_f
        result, normed_two, inv_two = layer_norm(hidden + outer_out, gain_second_f, shift_second_f)
        out_list.append(result.astype(jnp.bfloat16).reshape(SEQ_MB, seq_dev, D))
        grad_out = grad_rows * row_keep
        grad_second, grad_gain_b, grad_shift_b = norm_back(
            grad_out, normed_two, inv_two, gain_second_f
        )
        grad_outer = grad_second.astype(jnp.bfloat16)
        grad_outer_w = left_product(activated, grad_outer)
        grad_outer_b = jnp.sum(grad_outer.astype(jnp.float32), axis=0)
        grad_inner = (right_product(grad_outer, outer_weight) * gelu_slope(inner_pre)).astype(
            jnp.bfloat16
        )
        grad_inner_w = left_product(hidden_low, grad_inner)
        grad_inner_b = jnp.sum(grad_inner.astype(jnp.float32), axis=0)
        grad_hidden = grad_second + right_product(grad_inner, inner_weight)
        grad_first, grad_gain_a, grad_shift_a = norm_back(
            grad_hidden, normed_one, inv_one, gain_first_f
        )
        grad_branch = grad_first.astype(jnp.bfloat16)
        grad_out_w = left_product(context, grad_branch)
        grad_out_b = jnp.sum(grad_branch.astype(jnp.float32), axis=0)
        grad_context = (
            right_product(grad_branch, out_weight).astype(jnp.bfloat16).reshape(SEQ_MB, seq_dev, D)
        )
        row_delta = jnp.einsum(
            "bqhd,bhqd->bhq", split_heads(grad_context).astype(jnp.float32), attended
        )
        stat_total, stat_delta = (
            lax.all_gather(log_total.transpose(0, 2, 1), "ctx", axis=1, tiled=True),
            lax.all_gather(row_delta.transpose(0, 2, 1), "ctx", axis=1, tiled=True),
        )
        query_fn = partial(
            query_grad_step,
            queries=queries,
            grad_context=grad_context,
            log_total=log_total,
            row_delta=row_delta,
            seq_lens=seq_lens,
            live_queries=query_ok,
            skip_empty=False,
        )
        key_fn = partial(
            key_grad_step,
            key_rows=keys_local,
            value_rows=values_local,
            stat_total=stat_total,
            stat_delta=stat_delta,
            seq_lens=seq_lens,
            live_keys=query_ok,
            skip_empty=False,
        )
        grad_zero = jnp.zeros((SEQ_MB, seq_dev, H, HD), jnp.float32)
        grad_q = in_blocks(
            query_fn,
            grad_zero,
            (
                lax.all_gather(keys_local, "ctx", axis=1, tiled=True),
                lax.all_gather(values_local, "ctx", axis=1, tiled=True),
            ),
        )
        grad_k, grad_v = in_blocks(
            key_fn,
            (grad_zero, grad_zero),
            (
                lax.all_gather(queries, "ctx", axis=1, tiled=True),
                lax.all_gather(grad_context, "ctx", axis=1, tiled=True),
            ),
        )
        joint_grad = jnp.concatenate(
            [
                (grad_q * SCALE).reshape(row_count, D).astype(jnp.bfloat16),
                (grad_k * SCALE).reshape(row_count, D).astype(jnp.bfloat16),
                grad_v.reshape(row_count, D).astype(jnp.bfloat16),
            ],
            axis=1,
        )
        grad_joint_w = left_product(token_rows, joint_grad)
        grad_joint_b = jnp.sum(joint_grad.astype(jnp.float32), axis=0)
        input_rows = grad_first + right_product(joint_grad, joint_weight)
        grad_list.append(input_rows.reshape(SEQ_MB, seq_dev, D))
        micro_grads = (
            grad_joint_w,
            grad_joint_b,
            grad_out_w,
            grad_out_b,
            grad_gain_a,
            grad_shift_a,
            grad_inner_w,
            grad_inner_b,
            grad_outer_w,
            grad_outer_b,
            grad_gain_b,
            grad_shift_b,
        )
        if accum is None:
            accum = micro_grads
        else:
            accum = tuple((held + fresh for held, fresh in zip(accum, micro_grads)))
    (
        joint_w,
        joint_b,
        out_w,
        out_b,
        gain_a,
        shift_a,
        inner_w,
        inner_b,
        outer_w,
        outer_b,
        gain_b,
        shift_b,
    ) = accum
    grad_set = (
        joint_w[:, :D],
        joint_b[:D],
        joint_w[:, D : 2 * D],
        joint_w[:, 2 * D :],
        joint_b[2 * D :],
        out_w,
        out_b,
        gain_a,
        shift_a,
        inner_w,
        inner_b,
        outer_w,
        outer_b,
        gain_b,
        shift_b,
    )
    shard_grads = (
        lax.psum_scatter(
            grad_set[0].astype(jnp.bfloat16), "fsdp", scatter_dimension=0, tiled=True
        ).astype(jnp.float32),
        lax.psum_scatter(
            grad_set[1].astype(jnp.bfloat16), "fsdp", scatter_dimension=0, tiled=True
        ).astype(jnp.float32),
        lax.psum_scatter(
            grad_set[2].astype(jnp.bfloat16), "fsdp", scatter_dimension=0, tiled=True
        ).astype(jnp.float32),
        lax.psum_scatter(
            grad_set[3].astype(jnp.bfloat16), "fsdp", scatter_dimension=0, tiled=True
        ).astype(jnp.float32),
        lax.psum_scatter(
            grad_set[4].astype(jnp.bfloat16), "fsdp", scatter_dimension=0, tiled=True
        ).astype(jnp.float32),
        lax.psum_scatter(
            grad_set[5].astype(jnp.bfloat16), "fsdp", scatter_dimension=0, tiled=True
        ).astype(jnp.float32),
        lax.psum_scatter(
            grad_set[6].astype(jnp.bfloat16), "fsdp", scatter_dimension=0, tiled=True
        ).astype(jnp.float32),
        lax.psum_scatter(
            grad_set[7].astype(jnp.bfloat16), "fsdp", scatter_dimension=0, tiled=True
        ).astype(jnp.float32),
        lax.psum_scatter(
            grad_set[8].astype(jnp.bfloat16), "fsdp", scatter_dimension=0, tiled=True
        ).astype(jnp.float32),
        lax.psum_scatter(
            grad_set[9].astype(jnp.bfloat16), "fsdp", scatter_dimension=0, tiled=True
        ).astype(jnp.float32),
        lax.psum_scatter(
            grad_set[10].astype(jnp.bfloat16), "fsdp", scatter_dimension=0, tiled=True
        ).astype(jnp.float32),
        lax.psum_scatter(
            grad_set[11].astype(jnp.bfloat16), "fsdp", scatter_dimension=0, tiled=True
        ).astype(jnp.float32),
        lax.psum_scatter(
            grad_set[12].astype(jnp.bfloat16), "fsdp", scatter_dimension=0, tiled=True
        ).astype(jnp.float32),
        lax.psum_scatter(
            grad_set[13].astype(jnp.bfloat16), "fsdp", scatter_dimension=0, tiled=True
        ).astype(jnp.float32),
        lax.psum_scatter(
            grad_set[14].astype(jnp.bfloat16), "fsdp", scatter_dimension=0, tiled=True
        ).astype(jnp.float32),
    )
    summed = lax.psum(
        (
            shard_grads[0],
            shard_grads[1],
            shard_grads[2],
            shard_grads[3],
            shard_grads[4],
            shard_grads[5],
            shard_grads[6],
            shard_grads[7],
            shard_grads[8],
            shard_grads[9],
            shard_grads[10],
            shard_grads[11],
            shard_grads[12],
            shard_grads[13],
            shard_grads[14],
        ),
        "ctx",
    )
    outputs = jnp.concatenate(out_list, axis=0)
    input_grad = jnp.concatenate(grad_list, axis=0)
    return (outputs, input_grad) + tuple(summed)


def solution(mesh):
    placed = (
        P("fsdp", "ctx", None),
        P("fsdp", "ctx", None),
        P("fsdp"),
        P("fsdp", None),
        P("fsdp"),
        P("fsdp", None),
        P("fsdp", None),
        P("fsdp"),
        P("fsdp", None),
        P("fsdp"),
        P("fsdp"),
        P("fsdp"),
        P("fsdp", None),
        P("fsdp"),
        P("fsdp", None),
        P("fsdp"),
        P("fsdp"),
        P("fsdp"),
    )
    return jax.shard_map(
        body,
        mesh=mesh,
        in_specs=placed,
        out_specs=(
            P("fsdp", "ctx", None),
            P("fsdp", "ctx", None),
            P("fsdp", None),
            P("fsdp"),
            P("fsdp", None),
            P("fsdp", None),
            P("fsdp"),
            P("fsdp", None),
            P("fsdp"),
            P("fsdp"),
            P("fsdp"),
            P("fsdp", None),
            P("fsdp"),
            P("fsdp", None),
            P("fsdp"),
            P("fsdp"),
            P("fsdp"),
        ),
        check_vma=False,
    )
```

profile of v0, /device:TPU:0, one launch (start us, length us, event | category | flops | bytes accessed | tf_op | source)
XLA Modules:
  0.0 1116.4 jit_solution(8844355284658579773)
XLA Ops:
  17.3 13.5 %all-reduce.19 = (bf16[768]{0:T(1024)(128)(2,1)S(1)}, bf16[768]{0:T(1024)(128)(2,1)S(1)}, bf16[768]{0:T(1024)(128)(2,1)}, bf16[768]{0:T(1024)(128)(2,1)}, bf16[7...) all-reduce(bf16[768]{0:T(1024)(128)(2,1)S(1)} %dynamic-update-slice, ...), channel_id=1, replica_groups=mesh['ctx'=8,'fsdp'=4] {'fsdp'}, use_global_device_ids=true, to_apply=%add.1 | all-reduce | flops 5376 | bytes 21504
  32.2 16.8 %all-gather.26.cloned.1.call-done = bf16[768,768]{1,0:T(8,128)(2,1)} async-done(((bf16[192,768]{1,0:T(8,128)(2,1)}), bf16[768,768]{1,0:T(8,128)(2,1)}) %all-gather.26.cloned.1.call-update) | async-done | bytes 1179664 | tf_op jit(solution)/shard_map/all_gather | solution.py:212
  50.4 17.7 %all-gather.28.cloned.1.call-done = bf16[768,768]{1,0:T(8,128)(2,1)} async-done(((bf16[192,768]{1,0:T(8,128)(2,1)}), bf16[768,768]{1,0:T(8,128)(2,1)}) %all-gather.28.cloned.1.call-update) | async-done | bytes 1179664 | tf_op jit(solution)/shard_map/all_gather | solution.py:213
  91.0 27.3 %all-gather.36.cloned.1.call-done = bf16[1024,768]{0,1:T(8,128)(2,1)} async-done(((bf16[128,768]{0,1:T(8,128)(2,1)}), bf16[1024,768]{0,1:T(8,128)(2,1)}) %all-gather.36.cloned.1.call-update) | async-done | bytes 1572880 | tf_op jit(solution)/shard_map/all_gather | solution.py:287
  118.2 45.4 %all-gather.38.cloned.1.call-done = bf16[1024,768]{0,1:T(8,128)(2,1)} async-done(((bf16[128,768]{0,1:T(8,128)(2,1)}), bf16[1024,768]{0,1:T(8,128)(2,1)}) %all-gather.38.cloned.1.call-update) | async-done | bytes 1572880 | tf_op jit(solution)/shard_map/all_gather | solution.py:288
  163.7 18.6 %while.96 = (s32[]{:T(128)}, f32[1,12,128]{2,1,0:T(8,128)S(1)}, f32[1,12,128]{2,1,0:T(8,128)}, f32[1,12,128,64]{2,3,1,0:T(8,128)}, s32[1]{0:T(128)}, /*index=5*/...) while((s32[]{:T(128)}, f32[1,12,128]{2,1,0:T(8,128)S(1)}, ...), condition=%wide.region_3.4_spmd.clone, body=%wide.region_0.3_spmd.clone.sunk | while | flops 211855360 | bytes 21584264 | solution.py:97
  186.6 41.5 %all-gather.40.cloned.1.call-done = bf16[1024,768]{0,1:T(8,128)(2,1)} async-done(((bf16[128,768]{0,1:T(8,128)(2,1)}), bf16[1024,768]{0,1:T(8,128)(2,1)}) %all-gather.40.cloned.1.call-update) | async-done | bytes 1572880 | tf_op jit(solution)/shard_map/all_gather | solution.py:287
  228.1 45.6 %all-gather.42.cloned.1.call-done = bf16[1024,768]{0,1:T(8,128)(2,1)} async-done(((bf16[128,768]{0,1:T(8,128)(2,1)}), bf16[1024,768]{0,1:T(8,128)(2,1)}) %all-gather.42.cloned.1.call-update) | async-done | bytes 1572880 | tf_op jit(solution)/shard_map/all_gather | solution.py:288
  273.7 19.2 %while.97 = (s32[]{:T(128)}, f32[1,12,128]{2,1,0:T(8,128)S(1)}, f32[1,12,128]{2,1,0:T(8,128)}, f32[1,12,128,64]{2,3,1,0:T(8,128)}, s32[1]{0:T(128)}, /*index=5*/...) while((s32[]{:T(128)}, f32[1,12,128]{2,1,0:T(8,128)S(1)}, ...), condition=%wide.region_11.12_spmd.clone, body=%wide.region_8.11_spmd.clone.sunk | while | flops 211855360 | bytes 21584264 | solution.py:97
  296.2 14.8 %all-gather.32.cloned.1.call-done = bf16[768,3072]{1,0:T(8,128)(2,1)} async-done(((bf16[192,3072]{1,0:T(8,128)(2,1)}), bf16[768,3072]{1,0:T(8,128)(2,1)}) %all-gather.32.cloned.1.call-update) | async-done | bytes 4718608 | tf_op jit(solution)/shard_map/all_gather | solution.py:219
  314.3 35.6 %all-gather.34.cloned.1.call-done = bf16[3072,768]{1,0:T(8,128)(2,1)} async-done(((bf16[768,768]{1,0:T(8,128)(2,1)}), bf16[3072,768]{1,0:T(8,128)(2,1)}) %all-gather.34.cloned.1.call-update) | async-done | bytes 4718608 | tf_op jit(solution)/shard_map/all_gather | solution.py:221
  371.9 32.4 %all_gather.105 = f32[1,1024,12]{1,2,0:T(8,128)} all-gather(f32[1,128,12]{1,2,0:T(8,128)S(1)} %bitcast.529), channel_id=1, replica_groups=mesh['ctx'=8,'fsdp'=4] {'ctx'}, dimensions={1}, use_global_device_ids=true | all-gather | bytes 55296 | tf_op jit(solution)/shard_map/all_gather | solution.py:328
  404.3 32.9 %all_gather.109 = f32[1,1024,12]{1,2,0:T(8,128)} all-gather(f32[1,128,12]{1,2,0:T(8,128)S(1)} %bitcast.527), channel_id=1, replica_groups=mesh['ctx'=8,'fsdp'=4] {'ctx'}, dimensions={1}, use_global_device_ids=true | all-gather | bytes 55296 | tf_op jit(solution)/shard_map/all_gather | solution.py:328
  441.3 32.0 %all_gather.107 = f32[1,1024,12]{1,2,0:T(8,128)} all-gather(f32[1,128,12]{1,2,0:T(8,128)S(1)} %bitcast.521), channel_id=1, replica_groups=mesh['ctx'=8,'fsdp'=4] {'ctx'}, dimensions={1}, use_global_device_ids=true | all-gather | bytes 55296 | tf_op jit(solution)/shard_map/all_gather | solution.py:329
  473.3 17.9 %while.98 = (s32[]{:T(128)}, f32[1,128,12,64]{1,3,2,0:T(8,128)}, bf16[1,1024,768]{1,2,0:T(8,128)(2,1)}, s32[1]{0:T(128)}, bf16[128,768]{0,1:T(8,128)(2,1)S(1)}, ...) while((s32[]{:T(128)}, f32[1,128,12,64]{1,3,2,0:T(8,128)}, ...), condition=%wide.region_21.22_spmd.clone, body=%wide.region_20.21_spmd.clone.sunk | while | flops 306906112 | bytes 16135397 | solution.py:97
  494.1 32.3 %all_gather.111 = f32[1,1024,12]{1,2,0:T(8,128)} all-gather(f32[1,128,12]{1,2,0:T(8,128)S(1)} %bitcast.524), channel_id=1, replica_groups=mesh['ctx'=8,'fsdp'=4] {'ctx'}, dimensions={1}, use_global_device_ids=true | all-gather | bytes 55296 | tf_op jit(solution)/shard_map/all_gather | solution.py:329
  526.4 17.8 %while.100 = (s32[]{:T(128)}, f32[1,128,12,64]{1,3,2,0:T(8,128)}, bf16[1,1024,768]{1,2,0:T(8,128)(2,1)}, s32[1]{0:T(128)}, bf16[128,768]{0,1:T(8,128)(2,1)S(1)},...) while((s32[]{:T(128)}, f32[1,128,12,64]{1,3,2,0:T(8,128)}, ...), condition=%wide.region_29.30_spmd.clone, body=%wide.region_28.29_spmd.clone.sunk | while | flops 306906112 | bytes 16160001 | solution.py:97
  549.1 31.5 %while.99 = (s32[]{:T(128)}, f32[1,128,12,64]{1,3,2,0:T(8,128)}, f32[1,128,12,64]{1,3,2,0:T(8,128)}, bf16[1,1024,768]{1,2,0:T(8,128)(2,1)}, bf16[128,768]{0,1:T(...) while((s32[]{:T(128)}, f32[1,128,12,64]{1,3,2,0:T(8,128)}, ...), condition=%wide.region_23.24_spmd.clone, body=%wide.region_22.23_spmd.clone.sunk | while | flops 410910976 | bytes 41460404 | solution.py:97
  580.6 29.8 %while.101 = (s32[]{:T(128)}, f32[1,128,12,64]{1,3,2,0:T(8,128)}, f32[1,128,12,64]{1,3,2,0:T(8,128)}, bf16[1,1024,768]{1,2,0:T(8,128)(2,1)}, bf16[128,768]{0,1:T...) while((s32[]{:T(128)}, f32[1,128,12,64]{1,3,2,0:T(8,128)}, ...), condition=%wide.region_31.32_spmd.clone, body=%wide.region_30.31_spmd.clone.sunk | while | flops 410910976 | bytes 41853676 | solution.py:97
  651.3 11.5 %all-reduce.18 = (bf16[768]{0:T(1024)(128)(2,1)}, bf16[768]{0:T(1024)(128)(2,1)}, bf16[768]{0:T(1024)(128)(2,1)}, bf16[768]{0:T(1024)(128)(2,1)}, bf16[768]{0:T(...) all-reduce(bf16[768]{0:T(1024)(128)(2,1)} %dynamic-update-slice.7, ...), channel_id=1, replica_groups=mesh['ctx'=8,'fsdp'=4] {'fsdp'}, use_global_device_ids=true, to_apply=%add.7 | all-reduce | flops 9984 | bytes 39936
  682.9 21.1 %reduce-scatter.23.cloned.1.call-done = bf16[192,768]{1,0:T(8,128)(2,1)} async-done(((bf16[768,768]{1,0:T(8,128)(2,1)}), bf16[192,768]{1,0:T(8,128)(2,1)}) %reduce-scatter.23.cloned.1.call-update) | async-done | bytes 294928
  705.1 49.3 %reduce-scatter.15.cloned.1.call-done = bf16[192,3072]{1,0:T(8,128)(2,1)} async-done(((bf16[768,3072]{1,0:T(8,128)(2,1)}), bf16[192,3072]{1,0:T(8,128)(2,1)}) %reduce-scatter.15.cloned.1.call-update) | async-done | bytes 1179664 | tf_op jit(solution)/shard_map/reduce_scatter | solution.py:457
  754.4 50.4 %reduce-scatter.17.cloned.1.call-done = bf16[768,768]{1,0:T(8,128)(2,1)} async-done(((bf16[3072,768]{1,0:T(8,128)(2,1)}), bf16[768,768]{1,0:T(8,128)(2,1)}) %reduce-scatter.17.cloned.1.call-update) | async-done | bytes 1179664 | tf_op jit(solution)/shard_map/reduce_scatter | solution.py:463
  804.8 301.3 %all-reduce.21 = (f32[192,768]{0,1:T(8,128)S(1)}, f32[192]{0:T(256)}, f32[192,768]{0,1:T(8,128)S(1)}, f32[192,768]{0,1:T(8,128)S(1)}, f32[192]{0:T(256)}, /*inde...) all-reduce(bf16[192,768]{0,1:T(8,128)(2,1)S(1)} %copy.87, ...), channel_id=1, replica_groups=mesh['ctx'=8,'fsdp'=4] {'ctx'}, use_global_device_ids=true, to_apply=%region_33.34 | all-reduce | flops 1771776 | bytes 10635264 | tf_op jit(solution)/shard_map/psum | solution.py:476
  (565 shorter events, 275.6 us)
Async XLA Ops:
  7.2 23.7 %all-gather.24.cloned.1.call-start = ((), (), s32[]{:S(2)}) async-start(), calls=%async_computation.6 | async-start | bytes 1474560 | tf_op jit(solution)/shard_map/all_gather | solution.py:210
  7.9 41.1 %all-gather.26.cloned.1.call-start = ((), (), s32[]{:S(2)}) async-start(), calls=%async_computation.7 | async-start | bytes 1474560 | tf_op jit(solution)/shard_map/all_gather | solution.py:212
  8.7 59.4 %all-gather.28.cloned.1.call-start = ((), (), s32[]{:S(2)}) async-start(), calls=%async_computation.8 | async-start | bytes 1474560 | tf_op jit(solution)/shard_map/all_gather | solution.py:213
  9.4 108.8 %all-gather.36.cloned.1.call-start = ((), (), s32[]{:S(2)}) async-start(), calls=%async_computation.15 | async-start | bytes 1769472 | tf_op jit(solution)/shard_map/all_gather | solution.py:287
  72.8 90.9 %all-gather.38.cloned.1.call-start = ((), (), s32[]{:S(2)}) async-start(), calls=%async_computation.16 | async-start | bytes 1769472 | tf_op jit(solution)/shard_map/all_gather | solution.py:288
  73.4 110.0 %all-gather.30.cloned.1.call-start = ((), (), s32[]{:S(2)}) async-start(), calls=%async_computation.9 | async-start | bytes 1474560 | tf_op jit(solution)/shard_map/all_gather | solution.py:215
  74.0 154.2 %all-gather.40.cloned.1.call-start = ((), (), s32[]{:S(2)}) async-start(), calls=%async_computation.17 | async-start | bytes 1769472 | tf_op jit(solution)/shard_map/all_gather | solution.py:287
  76.3 87.3 %copy-start.9 = (bf16[128,768]{0,1:T(8,128)(2,1)S(1)}, bf16[128,768]{0,1:T(8,128)(2,1)}, u32[]{:S(2)}) copy-start(bf16[128,768]{0,1:T(8,128)(2,1)} %get-tuple-element.2059) | copy-start | bytes 589828
  77.2 196.5 %all-gather.42.cloned.1.call-start = ((), (), s32[]{:S(2)}) async-start(), calls=%async_computation.18 | async-start | bytes 1769472 | tf_op jit(solution)/shard_map/all_gather | solution.py:288
  78.0 233.0 %all-gather.32.cloned.1.call-start = ((), (), s32[]{:S(2)}) async-start(), calls=%async_computation.10 | async-start | bytes 5898240 | tf_op jit(solution)/shard_map/all_gather | solution.py:219
  78.7 271.2 %all-gather.34.cloned.1.call-start = ((), (), s32[]{:S(2)}) async-start(), calls=%async_computation.11 | async-start | bytes 5898240 | tf_op jit(solution)/shard_map/all_gather | solution.py:221
  79.3 469.8 %all-gather.44.cloned.1.call-start = ((), (), s32[]{:S(2)}) async-start(), calls=%async_computation.19 | async-start | bytes 1769472 | tf_op jit(solution)/shard_map/all_gather | solution.py:364
  90.6 458.5 %all-gather.46.cloned.1.call-start = ((), (), s32[]{:S(2)}) async-start(), calls=%async_computation.20 | async-start | bytes 1769472 | tf_op jit(solution)/shard_map/all_gather | solution.py:365
  183.3 90.4 %copy-start.55 = (bf16[1,12,128,64]{2,3,1,0:T(8,128)(2,1)}, bf16[1,12,128,64]{2,3,1,0:T(8,128)(2,1)S(1)}, u32[]{:S(2)}) copy-start(bf16[1,12,128,64]{2,3,1,0:T(8,128)(2,1)S(1)} %fusion.140) | copy-start | bytes 589828
  369.7 103.5 %copy-start.34 = (f32[128,768]{1,0:T(8,128)}, f32[128,768]{1,0:T(8,128)S(1)}, u32[]{:S(2)}) copy-start(f32[128,768]{1,0:T(8,128)S(1)} %get-tuple-element.1498) | copy-start | bytes 1179652
  371.0 209.6 %all-gather.48.cloned.1.call-start = ((), (), s32[]{:S(2)}) async-start(), calls=%async_computation.21 | async-start | bytes 1769472 | tf_op jit(solution)/shard_map/all_gather | solution.py:364
  371.8 208.8 %all-gather.50.cloned.1.call-start = ((), (), s32[]{:S(2)}) async-start(), calls=%async_computation.22 | async-start | bytes 1769472 | tf_op jit(solution)/shard_map/all_gather | solution.py:365
  492.9 155.2 %reduce-scatter.13.cloned.1.call-start = ((), (), s32[]{:S(2)}) async-start(), calls=%async_computation.12 | async-start | bytes 1474560 | tf_op jit(solution)/shard_map/reduce_scatter | solution.py:445
  549.0 131.7 %reduce-scatter.19.cloned.1.call-start = ((), (), s32[]{:S(2)}) async-start(), calls=%async_computation.23 | async-start | bytes 1474560
  621.7 60.1 %reduce-scatter.21.cloned.1.call-start = ((), (), s32[]{:S(2)}) async-start(), calls=%async_computation.24 | async-start | bytes 1474560
  623.3 80.7 %reduce-scatter.23.cloned.1.call-start = ((), (), s32[]{:S(2)}) async-start(), calls=%async_computation.25 | async-start | bytes 1474560
  624.8 129.6 %reduce-scatter.15.cloned.1.call-start = ((), (), s32[]{:S(2)}) async-start(), calls=%async_computation.13 | async-start | bytes 5898240 | tf_op jit(solution)/shard_map/reduce_scatter | solution.py:457
  630.5 174.4 %reduce-scatter.17.cloned.1.call-start = ((), (), s32[]{:S(2)}) async-start(), calls=%async_computation.14 | async-start | bytes 5898240 | tf_op jit(solution)/shard_map/reduce_scatter | solution.py:463
  678.4 126.5 %copy-start.114 = (f32[192]{0:T(256)S(1)}, f32[192]{0:T(256)}, u32[]{:S(2)}) copy-start(f32[192]{0:T(256)} %dynamic-slice_convert_fusion.6) | copy-start | bytes 2308
  (143 other events, 1454.6 us)
Sparse Core Ops, SparseCore 0:
  9.6 20.4 all-gather.23
  31.6 17.3 all-gather.25
  50.6 17.4 all-gather.27
  72.9 45.2 all-gather.35
  120.1 43.4 all-gather.37
  165.1 15.6 all-gather.29
  182.8 45.2 all-gather.39
  230.2 43.4 all-gather.41
  275.3 35.6 all-gather.31
  312.3 37.4 all-gather.33
  351.9 46.5 all-gather.43
  400.5 42.0 all-gather.45
  444.7 44.5 all-gather.47
  493.0 43.5 all-gather.49
  549.1 25.6 reduce-scatter.12
  621.8 25.6 reduce-scatter.18
  649.9 25.7 reduce-scatter.20
  678.3 25.7 reduce-scatter.22
  706.5 47.8 reduce-scatter.14
  757.0 47.8 reduce-scatter.16
where the time goes:
time: 1120 us
  blocking collectives  461 us (41%)
  waiting for transfers between devices  371 us (33%)
  matrix products  120 us (11%)
  local copies, waits for them, and re-layouts  76.2 us (7%)
  other arithmetic  67.4 us (6%)
  between operations  18.5 us (2%)
    psum x1, blocking collectives, body(): lax.psum((shard_grads[0], shard_grads[1], shard_grads[2], shard_grads[3],...  301 us
    all_gather x2, waiting for transfers between devices, body(): lax.all_gather(values_local, 'ctx', axis=1, tiled=True)  91 us
    all_gather x2, waiting for transfers between devices, body(): lax.all_gather(keys_local, 'ctx', axis=1, tiled=True)  68.8 us
    all_gather x2, blocking collectives, body(): lax.all_gather(log_total.transpose(0, 2, 1), 'ctx', axis=1, tiled=True)  65.3 us
    all_gather x2, blocking collectives, body(): lax.all_gather(row_delta.transpose(0, 2, 1), 'ctx', axis=1, tiled=True)  64.3 us
    reduce_scatter x1, waiting for transfers between devices, body(): lax.psum_scatter(grad_set[11].astype(jnp.bfloat16), 'fsdp', scatter_dimen...  50.4 us
    reduce_scatter x1, waiting for transfers between devices, body(): lax.psum_scatter(grad_set[9].astype(jnp.bfloat16), 'fsdp', scatter_dimens...  49.3 us
    all_gather x1, waiting for transfers between devices, body(): lax.all_gather(w_outer, 'fsdp', axis=0, tiled=True)  35.6 us
  transfers between devices with their start and end apart: 20, of which 11 were waited for; matrix products, arithmetic and copies ran while one was open for 22% of the time, Pallas kernels for 0%

commit v1 on v0

--- a/solution.py
+++ b/solution.py
@@ -3,6 +3,8 @@
 import jax
 import jax.numpy as jnp
 from jax import lax
+from jax.experimental import pallas as pl
+from jax.experimental.pallas import tpu as pltpu
 from jax.sharding import PartitionSpec as P
 
 D = 768
@@ -498,6 +500,731 @@
     return (outputs, input_grad) + tuple(summed)
 
 
+HALF = D // 2
+ROWS = 128
+
+
+def flat(z, x, y, k):
+    return (z * 2 + x) * 4 + y * 2 + k
+
+
+def table(move):
+    return [
+        (flat(z, x, y, k), flat(*move(z, x, y, k)))
+        for z in range(4)
+        for x in range(2)
+        for y in range(2)
+        for k in range(2)
+    ]
+
+
+def permute(move):
+    pairs = table(move)
+    return lambda block: lax.ppermute(block, ("ctx", "fsdp"), pairs)
+
+
+def permute_back(move):
+    pairs = [(b, a) for a, b in table(move)]
+    return lambda block: lax.ppermute(block, ("ctx", "fsdp"), pairs)
+
+
+def to_seq(turn):
+    return lambda z, x, y, k: (2 * k + (z // 2 + turn) % 2, x, y, z % 2)
+
+
+swap_core = permute(lambda z, x, y, k: (z, x, y, k ^ 1))
+swap_y = permute(lambda z, x, y, k: (z, x, y ^ 1, k))
+swap_x = permute(lambda z, x, y, k: (z, x ^ 1, y, k))
+swap_z1 = permute(lambda z, x, y, k: (z ^ 1, x, y, k))
+swap_z2 = permute(lambda z, x, y, k: (z ^ 2, x, y, k))
+seq_send = (permute(to_seq(0)), permute(to_seq(1)))
+seq_return = (permute_back(to_seq(0)), permute_back(to_seq(1)))
+
+
+def low(value):
+    return value.astype(jnp.bfloat16)
+
+
+def wide(value):
+    return value.astype(jnp.float32)
+
+
+def pick(array, index, axis=0):
+    return lax.dynamic_index_in_dim(array, index, axis, keepdims=False)
+
+
+def dot_nt(a, b):
+    return lax.dot_general(a, b, (((1,), (1,)), ((), ())), preferred_element_type=jnp.float32)
+
+
+def dot_tn(a, b):
+    return lax.dot_general(a, b, (((0,), (0,)), ((), ())), preferred_element_type=jnp.float32)
+
+
+def attend_kernel(
+    info, b0, b1, b2, b3, b4, b5, b6, b7, w0, w1, w2, w3, bias,
+    xs, ws, q_out, k_out, v_out, p_out, cu, cv, cxu, cxv, key_bias,
+):
+    step = pl.program_id(0)
+
+    @pl.when(step == 0)
+    def _():
+        for n, block in enumerate((b0, b1, b2, b3, b4, b5, b6, b7)):
+            xs[n * ROWS : (n + 1) * ROWS, :] = block[...]
+            place = info[n] + lax.broadcasted_iota(jnp.int32, (1, ROWS), 1)
+            key_bias[:, n * ROWS : (n + 1) * ROWS] = jnp.where(place < info[8], 0.0, NEG_FILL)
+        for n, piece in enumerate((w0, w1, w2, w3)):
+            ws[pl.ds(pl.multiple_of(info[9 + n], 64), 192), :] = piece[...]
+        q_out[...] = low(
+            wide(low(matmul(xs[: 4 * ROWS, :], ws[:, :HALF]) + bias[:, :HALF])) * SCALE
+        )
+        k_out[...] = low(matmul(xs[...], ws[:, HALF : 2 * HALF]))
+        v_out[...] = low(matmul(xs[...], ws[:, 2 * HALF :]) + bias[:, 2 * HALF :])
+
+    lanes = pl.ds(pl.multiple_of(step * 128, 128), 128)
+    first = lax.broadcasted_iota(jnp.int32, (1, 128), 1) < HD
+    queries = q_out[:, lanes]
+    keys = k_out[:, lanes]
+    values = v_out[:, lanes]
+    for part in range(2):
+        rows = slice(part * 256, part * 256 + 256)
+        found = []
+        for head in range(2):
+            mine = first if head == 0 else jnp.logical_not(first)
+            scores = dot_nt(jnp.where(mine, queries[rows], 0), keys) + key_bias[...]
+            top = jnp.max(scores, axis=1, keepdims=True)
+            weights = jnp.exp(scores - top)
+            total = jnp.sum(weights, axis=1, keepdims=True)
+            probs = low(weights * (1.0 / total))
+            p_out[head, rows, :] = probs
+            found.append(matmul(probs, values))
+        context = low(jnp.where(first, found[0], found[1]))
+        one, two = (cu, cv) if part == 0 else (cxu, cxv)
+        one[...] = context[:ROWS]
+        two[...] = context[ROWS:]
+
+
+def attend_back_kernel(
+    info, xs, ws, queries_ref, keys_ref, values_ref, probs_ref, gu, gv, gxu, gxv,
+    dx_own, dx_other, keep, send, dq, dk, dv, dw,
+):
+    step = pl.program_id(0)
+    lanes = pl.ds(pl.multiple_of(step * 128, 128), 128)
+    first = lax.broadcasted_iota(jnp.int32, (1, 128), 1) < HD
+    keys = keys_ref[:, lanes]
+    values = values_ref[:, lanes]
+    grad_k = jnp.zeros((8 * ROWS, 128), jnp.float32)
+    grad_v = jnp.zeros((8 * ROWS, 128), jnp.float32)
+    for part in range(2):
+        rows = slice(part * 256, part * 256 + 256)
+        one, two = (gu, gv) if part == 0 else (gxu, gxv)
+        grad_rows = jnp.concatenate([one[...], two[...]], axis=0)
+        queries = queries_ref[rows, lanes]
+        grad_q = jnp.zeros((256, 128), jnp.float32)
+        for head in range(2):
+            mine = first if head == 0 else jnp.logical_not(first)
+            grad_mine = jnp.where(mine, grad_rows, 0)
+            probs = probs_ref[head, rows, :]
+            grad_probs = dot_nt(grad_mine, values)
+            product = wide(probs) * grad_probs
+            delta = jnp.sum(product, axis=1, keepdims=True)
+            grad_scores = low(product - wide(probs) * delta)
+            grad_q = grad_q + matmul(grad_scores, jnp.where(mine, keys, 0))
+            grad_k = grad_k + dot_tn(grad_scores, jnp.where(mine, queries, 0))
+            grad_v = grad_v + dot_tn(probs, grad_mine)
+        dq[rows, lanes] = low(grad_q * SCALE)
+    dk[:, lanes] = low(grad_k)
+    dv[:, lanes] = low(grad_v)
+
+    @pl.when(step == pl.num_programs(0) - 1)
+    def _():
+        own = slice(0, 4 * ROWS)
+        other = slice(4 * ROWS, 8 * ROWS)
+        w_q, w_k, w_v = ws[:, :HALF], ws[:, HALF : 2 * HALF], ws[:, 2 * HALF :]
+        dx_other[...] = low(dot_nt(dk[other, :], w_k) + dot_nt(dv[other, :], w_v))
+        dx_own[...] = dot_nt(dq[...], w_q) + dot_nt(dk[own, :], w_k) + dot_nt(dv[own, :], w_v)
+        dw[:, :HALF] = low(dot_tn(xs[own, :], dq[...]))
+        dw[:, HALF : 2 * HALF] = low(dot_tn(xs[...], dk[...]))
+        dw[:, 2 * HALF :] = low(dot_tn(xs[...], dv[...]))
+        col_sums = jnp.concatenate(
+            [
+                jnp.sum(wide(dq[...]), axis=0, keepdims=True),
+                jnp.zeros((1, HALF), jnp.float32),
+                jnp.sum(wide(dv[...]), axis=0, keepdims=True),
+            ],
+            axis=1,
+        )
+        tail = low(jnp.where(lax.broadcasted_iota(jnp.int32, (16, 1), 0) == 0, col_sums, 0.0))
+        fsdp, z_bit = info[13], info[14]
+        for other_f in range(4):
+            place = send if other_f % 2 else keep
+            for half in range(2):
+                start = pl.multiple_of(192 * (fsdp ^ other_f) + 96 * half, 32)
+                place[other_f // 2, half ^ z_bit, :96, :] = dw[pl.ds(start, 96), :]
+                place[other_f // 2, half ^ z_bit, 96:, :] = tail if half == 0 else tail * 0
+
+
+def whole(shape):
+    return pl.BlockSpec(shape, lambda *_: (0,) * len(shape))
+
+
+def lane_block(rows):
+    return pl.BlockSpec((rows, 128), lambda step, *_: (0, step))
+
+
+VMEM_LIMIT = 56 * 1024 * 1024
+
+
+def attend(info, blocks, pieces, bias):
+    shape = jax.ShapeDtypeStruct
+    half = jnp.bfloat16
+    return pl.pallas_call(
+        attend_kernel,
+        out_shape=[
+            shape((8 * ROWS, D), half),
+            shape((D, 3 * HALF), half),
+            shape((4 * ROWS, HALF), half),
+            shape((8 * ROWS, HALF), half),
+            shape((8 * ROWS, HALF), half),
+            shape((6, 4 * ROWS, 8 * ROWS), half),
+        ]
+        + [shape((ROWS, HALF), half)] * 4,
+        grid_spec=pltpu.PrefetchScalarGridSpec(
+            num_scalar_prefetch=1,
+            grid=(3,),
+            in_specs=[whole((ROWS, D))] * 8 + [whole((192, 3 * HALF))] * 4 + [whole((1, 3 * HALF))],
+            out_specs=[
+                whole((8 * ROWS, D)),
+                whole((D, 3 * HALF)),
+                whole((4 * ROWS, HALF)),
+                whole((8 * ROWS, HALF)),
+                whole((8 * ROWS, HALF)),
+                pl.BlockSpec((2, 4 * ROWS, 8 * ROWS), lambda step, *_: (step, 0, 0)),
+            ]
+            + [lane_block(ROWS)] * 4,
+            scratch_shapes=[pltpu.VMEM((1, 8 * ROWS), jnp.float32)],
+        ),
+        compiler_params=pltpu.CompilerParams(
+            dimension_semantics=("arbitrary",), vmem_limit_bytes=VMEM_LIMIT
+        ),
+        cost_estimate=pl.CostEstimate(
+            flops=10_000_000_000, bytes_accessed=20_000_000, transcendentals=3_200_000
+        ),
+        name="attend",
+    )(info, *blocks, *pieces, bias)
+
+
+def attend_back(info, xs, ws, queries, keys, values, probs, grads):
+    shape = jax.ShapeDtypeStruct
+    half = jnp.bfloat16
+    joint = (2, 2, 112, 3 * HALF)
+    return pl.pallas_call(
+        attend_back_kernel,
+        out_shape=[
+            shape((4 * ROWS, D), jnp.float32),
+            shape((4 * ROWS, D), half),
+            shape(joint, half),
+            shape(joint, half),
+        ],
+        grid_spec=pltpu.PrefetchScalarGridSpec(
+            num_scalar_prefetch=1,
+            grid=(3,),
+            in_specs=[
+                whole((8 * ROWS, D)),
+                whole((D, 3 * HALF)),
+                whole((4 * ROWS, HALF)),
+                whole((8 * ROWS, HALF)),
+                whole((8 * ROWS, HALF)),
+                pl.BlockSpec((2, 4 * ROWS, 8 * ROWS), lambda step, *_: (step, 0, 0)),
+            ]
+            + [lane_block(ROWS)] * 4,
+            out_specs=[whole((4 * ROWS, D)), whole((4 * ROWS, D)), whole(joint), whole(joint)],
+            scratch_shapes=[
+                pltpu.VMEM((4 * ROWS, HALF), half),
+                pltpu.VMEM((8 * ROWS, HALF), half),
+                pltpu.VMEM((8 * ROWS, HALF), half),
+                pltpu.VMEM((D, 3 * HALF), half),
+            ],
+        ),
+        compiler_params=pltpu.CompilerParams(
+            dimension_semantics=("arbitrary",), vmem_limit_bytes=VMEM_LIMIT
+        ),
+        cost_estimate=pl.CostEstimate(
+            flops=14_000_000_000, bytes_accessed=20_000_000, transcendentals=0
+        ),
+        name="attend_back",
+    )(info, xs, ws, queries, keys, values, probs, *grads)
+
+
+def middle_one_kernel(
+    info, cm0, cm1, co0, co1, x0, x1, o0, o1, o2, o3, i0, i1, i2, i3, vec, bias,
+    hidden_out, normed_out, inv_out, act, slope, ctx, low_rows,
+):
+    step = pl.program_id(0)
+    f, x = info[0], info[1]
+
+    @pl.when(step == 0)
+    def _():
+        for side, (one, two) in enumerate(((cm0, cm1), (co0, co1))):
+            rows = jnp.concatenate([one[...], two[...]], axis=0)
+            for part in range(2):
+                ctx[2 * (x ^ side) + part] = rows[:, 192 * part : 192 * part + 192]
+        total = wide(jnp.concatenate([x0[...], x1[...]], axis=0)) + vec[0:1, :]
+        for n, piece in enumerate((o0, o1, o2, o3)):
+            total = total + matmul(ctx[f ^ n], piece[...])
+        hidden, normed, inv = layer_norm(total, vec[1:2, :], vec[2:3, :])
+        hidden_out[...] = hidden
+        normed_out[...] = normed
+        inv_out[...] = inv
+        rows = low(hidden)
+        for n in range(4):
+            low_rows[n] = rows[:, 192 * n : 192 * n + 192]
+
+    pre = bias[0]
+    for n, piece in enumerate((i0, i1, i2, i3)):
+        pre = pre + matmul(low_rows[f ^ n], piece[...])
+    bell = 0.5 * (1.0 + lax.erf(pre * ROOT_HALF))
+    act[0] = low(pre * bell)
+    slope[0] = low(bell + pre * INV_ROOT_TAU * jnp.exp(-0.5 * pre * pre))
+
+
+def middle_two_kernel(
+    info, act, slope, hidden, normed_one, inv_one, cot, vec,
+    o0, o1, o2, o3, i0, i1, i2, i3, w0, w1, w2, w3,
+    out, first_out, gm0, gm1, go0, go1, outer_out, inner_out, branch_out, sums,
+    o_all, i_all, w_all, spread, gc, o_sem, i_sem, w_sem,
+):
+    f, x = info[0], info[1]
+    copies = {}
+    for name, refs, held, sems in (
+        ("w", (w0, w1, w2, w3), w_all, w_sem),
+        ("i", (i0, i1, i2, i3), i_all, i_sem),
+        ("o", (o0, o1, o2, o3), o_all, o_sem),
+    ):
+        for n, ref in enumerate(refs):
+            copies[name, n] = pltpu.make_async_copy(ref, held.at[n], sems.at[n])
+            copies[name, n].start()
+    b_2, g_2, s_2, g_1 = vec[3:4, :], vec[4:5, :], vec[5:6, :], vec[1:2, :]
+    total = hidden[...] + b_2
+    for n in range(4):
+        copies["w", n].wait()
+        total = total + matmul(act[n], w_all[n])
+    result, normed, inv = layer_norm(total, g_2, s_2)
+    out[...] = low(result)
+    row = lax.broadcasted_iota(jnp.int32, (2 * ROWS, 1), 0)
+    end = jnp.where(row < ROWS, info[4], info[5] + ROWS)
+    grad = wide(cot[...]) * jnp.where(row + info[3] < end, 1.0, 0.0)
+    sums[...] = jnp.zeros_like(sums)
+
+    def put(index, value):
+        sums[index : index + 1, :] = jnp.sum(value, axis=0, keepdims=True)
+
+    def back(grad, normed, inv, gain):
+        scaled = grad * gain
+        return inv * (
+            scaled
+            - jnp.mean(scaled, axis=-1, keepdims=True)
+            - normed * jnp.mean(scaled * normed, axis=-1, keepdims=True)
+        )
+
+    put(4, grad * normed)
+    put(5, grad)
+    grad_second = back(grad, normed, inv, g_2)
+    grad_outer = low(grad_second)
+    outer_out[...] = grad_outer
+    put(3, wide(grad_outer))
+    for n in range(4):
+        copies["i", n].wait()
+    parts = [None] * 4
+    for e in range(4):
+        inner = low(dot_nt(grad_outer, w_all[e]) * wide(slope[e]))
+        inner_out[e] = inner
+        sums[pl.ds(8 + (f ^ e), 1), :] = jnp.sum(wide(inner), axis=0, keepdims=True)
+        columns = pl.ds(pl.multiple_of(D * (f ^ e), 128), D)
+        for n in range(4):
+            fresh = dot_nt(inner, i_all[n, :, columns])
+            parts[n] = fresh if e == 0 else parts[n] + fresh
+    for n in range(4):
+        spread[f ^ n] = parts[n]
+    grad_hidden = grad_second + jnp.concatenate([spread[n] for n in range(4)], axis=1)
+    normed = normed_one[...]
+    put(1, grad_hidden * normed)
+    put(2, grad_hidden)
+    grad_first = back(grad_hidden, normed, inv_one[...], g_1)
+    first_out[...] = grad_first
+    branch = low(grad_first)
+    branch_out[...] = branch
+    put(0, wide(branch))
+    for n in range(4):
+        copies["o", n].wait()
+        gc[f ^ n] = low(dot_nt(branch, o_all[n]))
+    for side, (one, two) in enumerate(((gm0, gm1), (go0, go1))):
+        rows = jnp.concatenate([gc[2 * (x ^ side)], gc[2 * (x ^ side) + 1]], axis=1)
+        one[...] = rows[:ROWS]
+        two[...] = rows[ROWS:]
+
+
+def middle_three_kernel(
+    info, act, inner, outer, hidden, branch, cm0, cm1, co0, co1, sums,
+    outer_keep, outer_send, inner_keep, inner_send, held, out_held, vec_held,
+):
+    step = pl.program_id(0)
+    f, x, spot = info[0], info[1], info[2]
+    block = f ^ step
+
+    @pl.when(step == 0)
+    def _():
+        for side, (one, two) in enumerate(((cm0, cm1), (co0, co1))):
+            rows = jnp.concatenate([one[...], two[...]], axis=0)
+            start = pl.multiple_of(HALF * (x ^ side), 128)
+            out_held[pl.ds(start, HALF), :] = low(dot_tn(rows, branch[...]))
+        vec_held[...] = jnp.zeros_like(vec_held)
+        top = lax.broadcasted_iota(jnp.int32, (16, 1), 0) == 0
+        for n in range(4):
+            cut = slice(192 * n, 192 * n + 192)
+            lines = (
+                sums[8 + n : 9 + n, :],
+                jnp.concatenate([sums[m : m + 1, cut] for m in range(4)], axis=1),
+                jnp.concatenate(
+                    [sums[4:5, cut], sums[5:6, cut], jnp.zeros((1, HALF), jnp.float32)], axis=1
+                ),
+            )
+            for m, line in enumerate(lines):
+                vec_held[m, n] = low(jnp.where(top, line, 0.0))
+
+    grad = low(dot_tn(act[0], outer[...]))
+    for place, wanted in ((outer_send, step < 2), (outer_keep, step >= 2)):
+
+        @pl.when(wanted)
+        def _(place=place):
+            for n in range(4):
+                place[0, n ^ spot] = grad[192 * n : 192 * n + 192]
+
+    held[...] = low(dot_tn(low(hidden[...]), inner[0]))
+    for n in range(4):
+        place = inner_send if n % 2 else inner_keep
+        start = 192 * (f ^ n)
+        place[n // 2, 0, :192, :] = held[pl.ds(pl.multiple_of(start, 64), 192), :]
+        place[n // 2, 0, 192:240, :] = out_held[pl.ds(pl.multiple_of(start + 48 * block, 16), 48), :]
+        place[n // 2, 0, 240:, :] = vec_held[block, f ^ n]
+
+
+MIDDLE = 2 * ROWS
+
+
+def middle_one(info, ctx, rows, out_pieces, inner_pieces, vec, bias):
+    shape = jax.ShapeDtypeStruct
+    return pl.pallas_call(
+        middle_one_kernel,
+        out_shape=[
+            shape((MIDDLE, D), jnp.float32),
+            shape((MIDDLE, D), jnp.float32),
+            shape((MIDDLE, 1), jnp.float32),
+            shape((4, MIDDLE, D), jnp.bfloat16),
+            shape((4, MIDDLE, D), jnp.bfloat16),
+        ],
+        grid_spec=pltpu.PrefetchScalarGridSpec(
+            num_scalar_prefetch=1,
+            grid=(4,),
+            in_specs=[whole((ROWS, HALF))] * 4
+            + [whole((ROWS, D))] * 2
+            + [whole((192, D))] * 4
+            + [pl.BlockSpec((192, D), lambda step, info: (0, info[0] ^ step))] * 4
+            + [whole((8, D)), pl.BlockSpec((1, 1, D), lambda step, info: (info[0] ^ step, 0, 0))],
+            out_specs=[whole((MIDDLE, D)), whole((MIDDLE, D)), whole((MIDDLE, 1))]
+            + [pl.BlockSpec((1, MIDDLE, D), lambda step, info: (step, 0, 0))] * 2,
+            scratch_shapes=[
+                pltpu.VMEM((4, MIDDLE, 192), jnp.bfloat16),
+                pltpu.VMEM((4, MIDDLE, 192), jnp.bfloat16),
+            ],
+        ),
+        compiler_params=pltpu.CompilerParams(
+            dimension_semantics=("arbitrary",), vmem_limit_bytes=VMEM_LIMIT
+        ),
+        cost_estimate=pl.CostEstimate(
+            flops=1_600_000_000, bytes_accessed=12_000_000, transcendentals=1_600_000
+        ),
+        name="middle_one",
+    )(info, *ctx, *rows, *out_pieces, *inner_pieces, vec, bias)
+
+
+def middle_two(info, act, slope, hidden, normed, inv, cot, vec, out_p, inner_p, outer_p):
+    shape = jax.ShapeDtypeStruct
+    half = jnp.bfloat16
+    return pl.pallas_call(
+        middle_two_kernel,
+        out_shape=[shape((MIDDLE, D), half), shape((MIDDLE, D), jnp.float32)]
+        + [shape((ROWS, HALF), half)] * 4
+        + [
+            shape((MIDDLE, D), half),
+            shape((4, MIDDLE, D), half),
+            shape((MIDDLE, D), half),
+            shape((16, D), jnp.float32),
+        ],
+        grid_spec=pltpu.PrefetchScalarGridSpec(
+            num_scalar_prefetch=1,
+            grid=(1,),
+            in_specs=[whole((4, MIDDLE, D))] * 2
+            + [whole((MIDDLE, D))] * 2
+            + [whole((MIDDLE, 1)), whole((MIDDLE, D)), whole((8, D))]
+            + [pl.BlockSpec(memory_space=pl.ANY)] * 12,
+            out_specs=[whole((MIDDLE, D))] * 2
+            + [whole((ROWS, HALF))] * 4
+            + [whole((MIDDLE, D)), whole((4, MIDDLE, D)), whole((MIDDLE, D)), whole((16, D))],
+            scratch_shapes=[
+                pltpu.VMEM((4, 192, D), half),
+                pltpu.VMEM((4, 192, 4 * D), half),
+                pltpu.VMEM((4, D, D), half),
+                pltpu.VMEM((4, MIDDLE, 192), jnp.float32),
+                pltpu.VMEM((4, MIDDLE, 192), half),
+                pltpu.SemaphoreType.DMA((4,)),
+                pltpu.SemaphoreType.DMA((4,)),
+                pltpu.SemaphoreType.DMA((4,)),
+            ],
+        ),
+        compiler_params=pltpu.CompilerParams(
+            dimension_semantics=("arbitrary",), vmem_limit_bytes=VMEM_LIMIT
+        ),
+        cost_estimate=pl.CostEstimate(
+            flops=4_000_000_000, bytes_accessed=20_000_000, transcendentals=0
+        ),
+        name="middle_two",
+    )(info, act, slope, hidden, normed, inv, cot, vec, *out_p, *inner_p, *outer_p)
+
+
+def middle_three(info, act, inner, outer, hidden, branch, ctx, sums):
+    shape = jax.ShapeDtypeStruct
+    half = jnp.bfloat16
+    return pl.pallas_call(
+        middle_three_kernel,
+        out_shape=[shape((2, 4, 192, D), half)] * 2 + [shape((2, 4, 256, D), half)] * 2,
+        grid_spec=pltpu.PrefetchScalarGridSpec(
+            num_scalar_prefetch=1,
+            grid=(4,),
+            in_specs=[
+                pl.BlockSpec(
+                    (1, MIDDLE, D),
+                    lambda step, info: (jnp.where(step < 2, 2 * step + 1, 2 * step - 4), 0, 0),
+                ),
+                pl.BlockSpec((1, MIDDLE, D), lambda step, info: (step, 0, 0)),
+            ]
+            + [whole((MIDDLE, D))] * 3
+            + [whole((ROWS, HALF))] * 4
+            + [whole((16, D))],
+            out_specs=[
+                pl.BlockSpec(
+                    (1, 4, 192, D), lambda step, info: (jnp.maximum(step - 2, 0), 0, 0, 0)
+                ),
+                pl.BlockSpec((1, 4, 192, D), lambda step, info: (jnp.minimum(step, 1), 0, 0, 0)),
+            ]
+            + [
+                pl.BlockSpec(
+                    (2, 1, 256, D), lambda step, info: (0, info[0] ^ step ^ info[2], 0, 0)
+                )
+            ]
+            * 2,
+            scratch_shapes=[
+                pltpu.VMEM((D, D), half),
+                pltpu.VMEM((D, D), half),
+                pltpu.VMEM((4, 4, 16, D), half),
+            ],
+        ),
+        compiler_params=pltpu.CompilerParams(
+            dimension_semantics=("arbitrary",), vmem_limit_bytes=VMEM_LIMIT
+        ),
+        cost_estimate=pl.CostEstimate(
+            flops=3_000_000_000, bytes_accessed=16_000_000, transcendentals=0
+        ),
+        name="middle_three",
+    )(info, act, inner, outer, hidden, branch, *ctx, sums)
+
+
+def place_outer_kernel(info, p0, p1, p2, p3, out):
+    for n, piece in enumerate((p0, p1, p2, p3)):
+        out[pl.ds(pl.multiple_of(192 * (n ^ info[2]), 64), 192), :] = wide(piece[...])
+
+
+def place_inner_kernel(info, p0, p1, p2, p3, inner, out, vec):
+    for n, piece in enumerate((p0, p1, p2, p3)):
+        at = n ^ info[2]
+        inner[:, pl.ds(pl.multiple_of(D * at, 128), D)] = wide(piece[:192, :])
+        out[pl.ds(pl.multiple_of(48 * at, 16), 48), :] = wide(piece[192:240, :])
+        vec[at] = wide(piece[240:, :])
+
+
+def place_joint_kernel(info, p0, p1, p2, p3, query, key, value, vec):
+    x, z_bit = info[1], info[2] % 2
+    for n, piece in enumerate((p0, p1, p2, p3)):
+        rows = pl.ds(pl.multiple_of(96 * (n % 2 ^ z_bit), 32), 96)
+        columns = pl.ds(pl.multiple_of(HALF * (n // 2 ^ x), 128), HALF)
+        for m, out in enumerate((query, key, value)):
+            out[rows, columns] = wide(piece[:96, HALF * m : HALF * m + HALF])
+        vec[n // 2 ^ x, n % 2 ^ z_bit] = wide(piece[96:, :])
+
+
+def placed(kernel, name, info, pieces, shapes):
+    return pl.pallas_call(
+        kernel,
+        out_shape=[jax.ShapeDtypeStruct(shape, jnp.float32) for shape in shapes],
+        grid_spec=pltpu.PrefetchScalarGridSpec(
+            num_scalar_prefetch=1,
+            grid=(1,),
+            in_specs=[whole(piece.shape) for piece in pieces],
+            out_specs=[whole(shape) for shape in shapes],
+        ),
+        compiler_params=pltpu.CompilerParams(
+            dimension_semantics=("arbitrary",), vmem_limit_bytes=VMEM_LIMIT
+        ),
+        name=name,
+    )(info, *pieces)
+
+
+def unshuffle(array, bit):
+    return jnp.where(bit == 0, array, array[::-1])
+
+
+def fsdp_sum(keep, send):
+    by_y = wide(keep) + wide(swap_core(send))
+    return by_y[0] + wide(swap_y(low(by_y[1])))
+
+
+def halved(shard, swap):
+    half = shard.shape[0] // 2
+    return shard[:half] + wide(swap(low(shard[half:])))
+
+
+def z_sum(pair):
+    one = low(halved(pair, swap_z1)[0])
+    one = low(wide(one) + wide(swap_z2(one)))
+    return [one, swap_z1(one)]
+
+
+def ctx_sum(shard):
+    pair = z_sum(halved(shard, swap_x))
+    return pair + [swap_x(one) for one in pair]
+
+
+def fast_body(
+    inputs, cotangent, lengths, w_query, b_query, w_key, w_value, b_value, w_output, b_output,
+    gain_one, bias_one, w_inner, b_inner, w_outer, b_outer, gain_two, bias_two,
+):
+    c, f = lax.axis_index("ctx"), lax.axis_index("fsdp")
+    z, x, y, k = c // 2, c % 2, f // 2, f % 2
+    zh = z // 2
+
+    turned = unshuffle(inputs, zh)
+    bu, bv = seq_send[0](turned[0]), seq_send[1](turned[1])
+    bxu, bxv = swap_x(bu), swap_x(bv)
+    blocks = [bu, bv, bxu, bxv]
+    blocks = blocks + [swap_core(b) for b in blocks]
+    z_low, z_high = 2 * (z % 2), 2 * (1 - z % 2)
+    spots = []
+    for kk in (k, 1 - k):
+        for xx in (x, 1 - x):
+            spots += [((z_low + kk) * 2 + xx) * ROWS, ((z_high + kk) * 2 + xx) * ROWS]
+
+    ends = jnp.stack([lengths // 128, lengths % 128]).reshape(4).astype(jnp.bfloat16)
+    small = jnp.concatenate(
+        [b_query, b_value, b_output, gain_one, bias_one, b_outer, gain_two, bias_two, b_inner, ends]
+        + [jnp.zeros((124,), jnp.bfloat16)]
+    ).reshape(19, 128)
+    small = jnp.stack([small, swap_y(small)])
+    small = jnp.stack([small, swap_core(small)], axis=1)
+    small = unshuffle(small, y)
+    small = jnp.where(k == 0, small, small[:, ::-1]).reshape(4, 19 * 128)
+    small = small.astype(jnp.float32)
+    vectors = [small[:, 192 * n : 192 * n + 192].reshape(D) for n in range(8)]
+    b_q, b_v, b_o, g_1, s_1, b_2, g_2, s_2 = vectors
+    b_1 = small[:, 1536:2304].reshape(4, 1, D)
+    ends = small[:, 2304:2308].astype(jnp.int32).reshape(4, 2, 2)
+    ends = (128 * ends[:, 0] + ends[:, 1]).reshape(8)
+    vec = jnp.stack([b_o, g_1, s_1, b_2, g_2, s_2, g_2, s_2])
+    info = jnp.stack(
+        spots + [pick(ends, 4 * y + z)] + [192 * (f ^ n) for n in range(4)] + [f, z % 2]
+    ).astype(jnp.int32)
+    turned_ends = unshuffle(lengths, zh)
+    spot = jnp.stack(
+        [f, x, 2 * x + z % 2, c * ROWS, turned_ends[0], turned_ends[1]]
+    ).astype(jnp.int32)
+    x_bias = jnp.concatenate(
+        [
+            lax.dynamic_slice_in_dim(b_q, x * HALF, HALF),
+            jnp.zeros((HALF,), jnp.float32),
+            lax.dynamic_slice_in_dim(b_v, x * HALF, HALF),
+        ]
+    )[None]
+    w_x = jnp.concatenate(
+        [lax.dynamic_slice_in_dim(w, x * HALF, HALF, 1) for w in (w_query, w_key, w_value)], axis=1
+    )
+
+    def gathered(shard, after=None):
+        if after is not None:
+            shard, after = lax.optimization_barrier((shard, after))
+        far = swap_y(shard)
+        return [shard, swap_core(shard), far, swap_core(far)]
+
+    qkv_p = gathered(w_x)
+    out_p = gathered(w_output, qkv_p[2])
+    inner_p = gathered(w_inner, out_p[2])
+    outer_p = gathered(w_outer, inner_p[2])
+
+    xs, ws, queries, keys, values, probs, cu, cv, cxu, cxv = attend(info, blocks, qkv_p, x_bias)
+
+    mine = [seq_return[0](cu), seq_return[1](cv)]
+    cxu, cxv = swap_x(cxu), swap_x(cxv)
+    ctx = mine + [seq_return[0](cxu), seq_return[1](cxv)]
+
+    hidden, normed, inv, act, slope = middle_one(
+        spot, ctx, [turned[0], turned[1]], out_p, inner_p, vec, b_1
+    )
+    cot = unshuffle(cotangent, zh).reshape(MIDDLE, D)
+    result, grad_first, gm0, gm1, go0, go1, outer, inner, branch, sums = middle_two(
+        spot, act, slope, hidden, normed, inv, cot, vec, out_p, inner_p, outer_p
+    )
+    outputs = unshuffle(result.reshape(2, ROWS, D), zh)
+    sent = [seq_send[0](go0), seq_send[1](go1)]
+    kept = [seq_send[0](gm0), seq_send[1](gm1)]
+    came = [swap_x(block) for block in sent]
+    outer_keep, outer_send, inner_keep, inner_send = middle_three(
+        spot, act, inner, outer, hidden, branch, ctx, sums
+    )
+    dx_own, dx_other, joint_keep, joint_send = attend_back(
+        info, xs, ws, queries, keys, values, probs, kept + came
+    )
+
+    dx = dx_own + wide(swap_core(dx_other))
+    dx = low(halved(dx, swap_x))
+    dx = jnp.concatenate([seq_return[n](dx[n * ROWS : (n + 1) * ROWS]) for n in range(2)], axis=0)
+    input_grad = unshuffle((grad_first + wide(dx)).reshape(2, ROWS, D), zh)
+
+    outer_blocks = ctx_sum(fsdp_sum(outer_keep, outer_send))
+    inner_blocks = ctx_sum(fsdp_sum(inner_keep, inner_send))
+    joint = z_sum(fsdp_sum(joint_keep, joint_send))
+    joint_blocks = joint + [swap_x(one) for one in joint]
+    (outer_grad,) = placed(place_outer_kernel, "place_outer", spot, outer_blocks, [(D, D)])
+    inner_grad, out_grad, lines = placed(
+        place_inner_kernel, "place_inner", spot, inner_blocks,
+        [(192, 4 * D), (192, D), (4, 16, D)],
+    )
+    q_grad, k_grad, v_grad, joint_lines = placed(
+        place_joint_kernel, "place_joint", spot, joint_blocks,
+        [(192, D)] * 3 + [(2, 2, 16, 3 * HALF)],
+    )
+    grad_b1 = lines[0, 0]
+    grad_bo, grad_g1, grad_s1, grad_b2 = (lines[1, 0, 192 * n : 192 * n + 192] for n in range(4))
+    grad_g2, grad_s2 = (lines[2, 0, 192 * n : 192 * n + 192] for n in range(2))
+    joint_sums = joint_lines[:, 0, 0]
+
+    def own(vector):
+        return lax.dynamic_slice_in_dim(vector.reshape(D), f * 192, 192)
+
+    grad_bq, grad_bv = own(joint_sums[:, :HALF]), own(joint_sums[:, 2 * HALF :])
+    return (
+        outputs, input_grad, q_grad, grad_bq, k_grad, v_grad, grad_bv, out_grad, grad_bo,
+        grad_g1, grad_s1, inner_grad, grad_b1, outer_grad, grad_b2, grad_g2, grad_s2,
+    )
+
+
 def solution(mesh):
     placed = (
         P("fsdp", "ctx", None),
@@ -519,8 +1246,9 @@
         P("fsdp"),
         P("fsdp"),
     )
+    fast = dict(mesh.shape) == {"ctx": 8, "fsdp": 4}
     return jax.shard_map(
-        body,
+        fast_body if fast else body,
         mesh=mesh,
         in_specs=placed,
         out_specs=(

time: 1120 us -> 384 us (0.34)
  blocking collectives: 461 us -> 0 us
  waiting for transfers between devices: 371 us -> 195 us
  matrix products: 120 us -> 0 us
  Pallas kernels: 0 us -> 80.9 us
  starting transfers between devices: 1.3 us -> 72.2 us
  other arithmetic: 67.4 us -> 9.17 us
  local copies, waits for them, and re-layouts: 76.2 us -> 24.2 us
  between operations: 18.5 us -> 1.49 us
    psum x1 -> x0, blocking collectives: 301 us -> none  [body(): lax.psum((shard_grads[0], shard_grads[1], shard_grads[2], shard_grads[3],...]
    all_gather x14 -> x0, waiting for transfers between devices: 245 us -> none  [the longest x2 91 us: body(): lax.all_gather(values_local, 'ctx', axis=1, tiled=True)]
    ppermute x0 -> x61, waiting for transfers between devices: none -> 195 us  [the longest x55 192 us: permute(): return lambda block: lax.ppermute(block, ('ctx', 'fsdp'), pairs)]
    all_gather x5 -> x0, blocking collectives: 135 us -> none  [the longest x2 65.3 us: body(): lax.all_gather(log_total.transpose(0, 2, 1), 'ctx', axis=1, tiled=True)]
    dot_general x52 -> x0, matrix products: 120 us -> none  [the longest x4 22.8 us: key_grad_step(): jnp.einsum('bhqk,bqhd->bkhd', grad_scores, split_heads(query_rows), prefe...]
    reduce_scatter x3 -> x0, waiting for transfers between devices: 99.7 us -> none  [the longest x1 50.4 us: body(): lax.psum_scatter(grad_set[11].astype(jnp.bfloat16), 'fsdp', scatter_dimen...]
    pallas_call x0 -> x8, Pallas kernels: none -> 80.9 us  [the longest x1 20.4 us: attend_back(): pl.pallas_call(attend_back_kernel, out_shape=[shape((4 * ROWS, D), jnp.fl...]
    ppermute x0 -> x61, starting transfers between devices: none -> 72.2 us  [the longest x55 54.8 us: permute(): return lambda block: lax.ppermute(block, ('ctx', 'fsdp'), pairs)]
  transfers between devices with their start and end apart: 20 -> 61, of which waited for: 11 -> 23; matrix products, arithmetic and copies ran while one was open for 22% -> 6% of each run, Pallas kernels for 0% -> 13%
where the time goes in v1:
time: 384 us; the launch traced here: 383 us
  waiting for transfers between devices  195 us (51%)
  Pallas kernels  80.9 us (21%)
  starting transfers between devices  72.2 us (19%)
  local copies, waits for them, and re-layouts  24.2 us (6%)
  other arithmetic  9.17 us (2%)
    ppermute x55, waiting for transfers between devices, permute(): return lambda block: lax.ppermute(block, ('ctx', 'fsdp'), pairs)  192 us
    ppermute x55, starting transfers between devices, permute(): return lambda block: lax.ppermute(block, ('ctx', 'fsdp'), pairs)  54.8 us
    pallas_call x1, Pallas kernels, attend_back(): pl.pallas_call(attend_back_kernel, out_shape=[shape((4 * ROWS, D), jnp.fl...  20.4 us
    ppermute x6, starting transfers between devices, permute_back(): return lambda block: lax.ppermute(block, ('ctx', 'fsdp'), pairs)  17.4 us
    pallas_call x1, Pallas kernels, middle_two(): pl.pallas_call(middle_two_kernel, out_shape=[shape((MIDDLE, D), half), sh...  15.2 us
    pallas_call x1, Pallas kernels, attend(): pl.pallas_call(attend_kernel, out_shape=[shape((8 * ROWS, D), half), shap...  14.9 us
    pallas_call x1, Pallas kernels, middle_three(): pl.pallas_call(middle_three_kernel, out_shape=[shape((2, 4, 192, D), half...  11 us
    pallas_call x3, Pallas kernels, placed(): pl.pallas_call(kernel, out_shape=[jax.ShapeDtypeStruct(shape, jnp.float32...  10.7 us
  transfers between devices with their start and end apart: 61, of which 23 were waited for; matrix products, arithmetic and copies ran while one was open for 6% of the time, Pallas kernels for 13%

profile of v1, /device:TPU:0, one launch (start us, length us, event | category | flops | bytes accessed | tf_op | source)
XLA Modules:
  0.0 382.8 jit_solution(1842558523411712580)
XLA Ops:
  7.2 9.7 %collective-permute-done.11.w2 = bf16[192,1152]{1,0:T(8,128)(2,1)} collective-permute-done((bf16[192,1152]{1,0:T(8,128)(2,1)}, bf16[192,1152]{1,0:T(8,128)(2,1)}, u32[]{:S(2)}, u32[]{:S(2)}) %collective-permute-start.11) | collective-permute-done | bytes 442400 | tf_op jit(solution)/shard_map/ppermute | solution.py:523
  19.4 6.1 %concatenate.12 = bf16[2432]{0:T(1024)(128)(2,1)S(1)} concatenate(bf16[192]{0:T(256)(128)(2,1)} %param.22, bf16[192]{0:T(256)(128)(2,1)} %param.25, bf16[192]{0:T(256)(128)(2,1)} %param.27, bf16[192]{0:T(256)(128)(2,1)} %param.28, bf16[192]{0:T(256)(128)(2,1)} %param.29, bf16[192]{0:T(256)(128)(2,1)} %param.33, bf16[192]{0:T(256)(128)(2,1)} %param.34, bf16[192]{0:T(256)(128)(2,1)} %param.35, ...), dimensions={0} | concatenate | bytes 9728 | tf_op jit(solution)/shard_map/concatenate | solution.py:1127
  32.5 4.8 %collective-permute-done.3.b1 = bf16[128,768]{1,0:T(8,128)(2,1)} collective-permute-done((bf16[128,768]{1,0:T(8,128)(2,1)S(1)}, bf16[128,768]{1,0:T(8,128)(2,1)}, u32[]{:S(2)}, u32[]{:S(2)}) %collective-permute-start.3) | collective-permute-done | bytes 196640 | tf_op jit(solution)/shard_map/ppermute | solution.py:523
  42.4 10.3 %collective-permute-done.23.i2 = bf16[192,3072]{1,0:T(8,128)(2,1)S(1)} collective-permute-done((bf16[192,3072]{1,0:T(8,128)(2,1)}, bf16[192,3072]{1,0:T(8,128)(2,1)S(1)}, u32[]{:S(2)}, u32[]{:S(2)}) %collective-permute-start.23) | collective-permute-done | bytes 1179680 | tf_op jit(solution)/shard_map/ppermute | solution.py:523
  58.6 14.9 %attend.1 = (bf16[1024,768]{1,0:T(8,128)(2,1)}, bf16[768,1152]{1,0:T(8,128)(2,1)}, bf16[512,384]{1,0:T(8,128)(2,1)}, bf16[1024,384]{1,0:T(8,128)(2,1)}, bf16[102...) custom-call(s32[15]{0:T(128)} %stack.115.info, ...), custom_call_target="tpu_custom_call" | custom-call | flops 10000000000 | bytes 20000000 | tf_op jit(solution)/shard_map/attend/pallas_call | solution.py:681
  77.2 4.8 %collective-permute-done.26.w2 = bf16[768,768]{1,0:T(8,128)(2,1)} collective-permute-done((bf16[768,768]{1,0:T(8,128)(2,1)}, bf16[768,768]{1,0:T(8,128)(2,1)}, u32[]{:S(2)}, u32[]{:S(2)}) %collective-permute-start.26) | collective-permute-done | bytes 1179680 | tf_op jit(solution)/shard_map/ppermute | solution.py:523
  89.3 4.1 %collective-permute-done.15 = bf16[128,384]{1,0:T(8,128)(2,1)S(1)} collective-permute-done((bf16[128,384]{1,0:T(8,128)(2,1)}, bf16[128,384]{1,0:T(8,128)(2,1)S(1)}, u32[]{:S(2)}, u32[]{:S(2)}) %collective-permute-start.15) | collective-permute-done | bytes 98336 | tf_op jit(solution)/shard_map/ppermute | solution.py:523
  100.8 9.8 %collective-permute-start.18 = (bf16[128,384]{1,0:T(8,128)(2,1)}, bf16[128,384]{1,0:T(8,128)(2,1)S(1)}, u32[]{:S(2)}, u32[]{:S(2)}) collective-permute-start(bf16[128,384]{1,0:T(8,128)(2,1)} %collective-permute-done.17), channel_id=1, source_target_pairs={{8,0},{24,1},{10,2},{26,3},{12,4},{28,5},{14,6},{30,7},{9,8},{25,9... | collective-permute-start | bytes 294920 | tf_op jit(solution)/shard_map/ppermute | solution.py:528
  114.4 8.8 %middle_one.1 = (f32[256,768]{1,0:T(8,128)}, f32[256,768]{1,0:T(8,128)}, f32[256,1]{1,0:T(8,128)}, bf16[4,256,768]{2,1,0:T(8,128)(2,1)}, bf16[4,256,768]{2,1,0:T(8,128)(2,1)}) custom-call(s32[6]{0:T(128)} %stack.93.info, bf16[128,384]{1,0:T(8,128)(2,1)} %copy-done.30, bf16[128,384]{1,0:T(8,128)(2,1)} %copy-done.31, bf16[128,384]{1,0:T(8,128)(2,1)} %copy-done.32, ...), custom_call_target="tpu_custom_call" | custom-call | flops 1600000000 | bytes 12000000 | tf_op jit(solution)/shard_map/middle_one/pallas_call | solution.py:917
  123.1 15.2 %middle_two.1 = (bf16[256,768]{1,0:T(8,128)(2,1)}, f32[256,768]{1,0:T(8,128)}, bf16[128,384]{1,0:T(8,128)(2,1)}, bf16[128,384]{1,0:T(8,128)(2,1)}, bf16[128,384]...) custom-call(s32[6]{0:T(128)} %stack.93.info, ...), custom_call_target="tpu_custom_call" | custom-call | flops 4000000000 | bytes 20000000 | tf_op jit(solution)/shard_map/middle_two/pallas_call | solution.py:954
  138.3 11.0 %middle_three.1 = (bf16[2,4,192,768]{3,2,1,0:T(8,128)(2,1)}, bf16[2,4,192,768]{3,2,1,0:T(8,128)(2,1)}, bf16[2,4,256,768]{3,2,1,0:T(8,128)(2,1)}, bf16[2,4,256,768]{3,2,1,0:T(8,128)(2,1)}) custom-call(s32[6]{0:T(128)} %stack.93.info, bf16[4,256,768]{2,1,0:T(8,128)(2,1)} %get-tuple-element.66.act, bf16[4,256,768]{2,1,0:T(8,128)(2,1)} %get-tuple-element.92.inner, ...), custom_call_target="tpu_custom_call" | custom-call | flops 3000000000 | bytes 16000000 | tf_op jit(solution)/shard_map/middle_three/pallas_call | solution.py:998
  169.8 20.4 %attend_back.1 = (f32[512,768]{1,0:T(8,128)}, bf16[512,768]{1,0:T(8,128)(2,1)}, bf16[2,2,112,1152]{3,2,1,0:T(8,128)(2,1)}, bf16[2,2,112,1152]{3,2,1,0:T(8,128)(2,1)}) custom-call(s32[15]{0:T(128)} %stack.115.info, bf16[1024,768]{1,0:T(8,128)(2,1)} %get-tuple-element.74.xs, bf16[768,1152]{1,0:T(8,128)(2,1)} %get-tuple-element.75.ws, ...), custom_call_target="tpu_custom_call" | custom-call | flops 14000000000 | bytes 20000000 | tf_op jit(solution)/shard_map/attend_back/pallas_call | solution.py:721
  199.9 22.1 %collective-permute-done.54 = bf16[4,192,768]{2,1,0:T(8,128)(2,1)S(1)} collective-permute-done((bf16[4,192,768]{2,1,0:T(8,128)(2,1)S(1)}, bf16[4,192,768]{2,1,0:T(8,128)(2,1)S(1)}, u32[]{:S(2)}, u32[]{:S(2)}) %collective-permute-start.54) | collective-permute-done | bytes 1179680 | tf_op jit(solution)/shard_map/ppermute | solution.py:523
  223.8 31.9 %collective-permute-done.46 = bf16[4,256,768]{2,1,0:T(8,128)(2,1)S(1)} collective-permute-done((bf16[4,256,768]{2,1,0:T(8,128)(2,1)S(1)}, bf16[4,256,768]{2,1,0:T(8,128)(2,1)S(1)}, u32[]{:S(2)}, u32[]{:S(2)}) %collective-permute-start.46) | collective-permute-done | bytes 1572896 | tf_op jit(solution)/shard_map/ppermute | solution.py:523
  261.4 12.6 %collective-permute-done.47 = bf16[2,256,768]{2,1,0:T(8,128)(2,1)S(1)} collective-permute-done((bf16[2,256,768]{2,1,0:T(8,128)(2,1)S(1)}, bf16[2,256,768]{2,1,0:T(8,128)(2,1)S(1)}, u32[]{:S(2)}, u32[]{:S(2)}) %collective-permute-start.47) | collective-permute-done | bytes 786464 | tf_op jit(solution)/shard_map/ppermute | solution.py:523
  277.2 15.8 %collective-permute-done.48 = bf16[1,256,768]{2,1,0:T(8,128)(2,1)S(1)} collective-permute-done((bf16[1,256,768]{2,1,0:T(8,128)(2,1)S(1)}, bf16[1,256,768]{2,1,0:T(8,128)(2,1)S(1)}, u32[]{:S(2)}, u32[]{:S(2)}) %collective-permute-start.48) | collective-permute-done | bytes 393248 | tf_op jit(solution)/shard_map/ppermute | solution.py:523
  299.0 19.8 %collective-permute-done.49 = bf16[256,768]{1,0:T(8,128)(2,1)S(1)} collective-permute-done((bf16[256,768]{1,0:T(8,128)(2,1)S(1)}, bf16[256,768]{1,0:T(8,128)(2,1)S(1)}, u32[]{:S(2)}, u32[]{:S(2)}) %collective-permute-start.49) | collective-permute-done | bytes 393248 | tf_op jit(solution)/shard_map/ppermute | solution.py:523
  319.0 4.7 %collective-permute-done.41 = bf16[112,1152]{1,0:T(8,128)(2,1)S(1)} collective-permute-done((bf16[112,1152]{1,0:T(8,128)(2,1)S(1)}, bf16[112,1152]{1,0:T(8,128)(2,1)S(1)}, u32[]{:S(2)}, u32[]{:S(2)}) %collective-permute-start.41) | collective-permute-done | bytes 258080 | tf_op jit(solution)/shard_map/ppermute | solution.py:523
  324.1 13.4 %collective-permute-done.42.p1 = bf16[112,1152]{1,0:T(8,128)(2,1)S(1)} collective-permute-done((bf16[112,1152]{1,0:T(8,128)(2,1)S(1)}, bf16[112,1152]{1,0:T(8,128)(2,1)S(1)}, u32[]{:S(2)}, u32[]{:S(2)}) %collective-permute-start.42) | collective-permute-done | bytes 258080 | tf_op jit(solution)/shard_map/ppermute | solution.py:523
  342.7 3.9 %collective-permute-done.44.p3 = bf16[112,1152]{1,0:T(8,128)(2,1)S(1)} collective-permute-done((bf16[112,1152]{1,0:T(8,128)(2,1)S(1)}, bf16[112,1152]{1,0:T(8,128)(2,1)S(1)}, u32[]{:S(2)}, u32[]{:S(2)}) %collective-permute-start.44) | collective-permute-done | bytes 258080 | tf_op jit(solution)/shard_map/ppermute | solution.py:523
  353.0 6.3 %collective-permute-done.60.p3 = bf16[192,768]{1,0:T(8,128)(2,1)S(1)} collective-permute-done((bf16[192,768]{1,0:T(8,128)(2,1)S(1)}, bf16[192,768]{1,0:T(8,128)(2,1)S(1)}, u32[]{:S(2)}, u32[]{:S(2)}) %collective-permute-start.60) | collective-permute-done | bytes 294944 | tf_op jit(solution)/shard_map/ppermute | solution.py:523
  363.5 4.2 %collective-permute-done.51.p2 = bf16[256,768]{1,0:T(8,128)(2,1)S(1)} collective-permute-done((bf16[256,768]{1,0:T(8,128)(2,1)S(1)}, bf16[256,768]{1,0:T(8,128)(2,1)S(1)}, u32[]{:S(2)}, u32[]{:S(2)}) %collective-permute-start.51) | collective-permute-done | bytes 393248 | tf_op jit(solution)/shard_map/ppermute | solution.py:523
  367.7 7.5 %collective-permute-done.52.p3 = bf16[256,768]{1,0:T(8,128)(2,1)S(1)} collective-permute-done((bf16[256,768]{1,0:T(8,128)(2,1)S(1)}, bf16[256,768]{1,0:T(8,128)(2,1)S(1)}, u32[]{:S(2)}, u32[]{:S(2)}) %collective-permute-start.52) | collective-permute-done | bytes 393248 | tf_op jit(solution)/shard_map/ppermute | solution.py:523
  376.0 3.8 %place_inner.1 = (f32[192,3072]{1,0:T(8,128)}, f32[192,768]{1,0:T(8,128)}, f32[4,16,768]{2,1,0:T(8,128)}) custom-call(s32[6]{0:T(128)} %stack.93.info, bf16[256,768]{1,0:T(8,128)(2,1)} %copy-done.7, bf16[256,768]{1,0:T(8,128)(2,1)} %copy-done.20, bf16[256,768]{1,0:T(8,128)(2,1)} %copy-done.22, bf16[256,768]{1,0:T(8,128)(2,1)} %copy-done.23), custom_call_target="tpu_custom_call" | custom-call | tf_op jit(solution)/shard_map/place_inner/pallas_call | solution.py:1066
  (262 shorter events, 115.3 us)
Async XLA Ops:
  6.4 51.5 %collective-permute-start.10 = (bf16[192,1152]{1,0:T(8,128)(2,1)}, bf16[192,1152]{1,0:T(8,128)(2,1)}, u32[]{:S(2)}, u32[]{:S(2)}) collective-permute-start(bf16[192,1152]{1,0:T(8,128)(2,1)} %pad_maximum_fusion.w0), channel_id=1, source_target_pairs={{0,1},{1,0},{2,3},{3,2},{4,5},{5,4},{6,7},{7,6},{8,9},{9,8},{10,11... | collective-permute-start | bytes 1327112 | tf_op jit(solution)/shard_map/ppermute | solution.py:523
  25.9 26.9 %collective-permute-start.23 = (bf16[192,3072]{1,0:T(8,128)(2,1)}, bf16[192,3072]{1,0:T(8,128)(2,1)S(1)}, u32[]{:S(2)}, u32[]{:S(2)}) collective-permute-start(bf16[192,3072]{1,0:T(8,128)(2,1)} %i0.1), channel_id=1, source_target_pairs={{0,2},{1,3},{2,0},{3,1},{4,6},{5,7},{6,4},{7,5},{8,10},{9,11},{10,... | collective-permute-start | bytes 3538952 | tf_op jit(solution)/shard_map/ppermute | solution.py:523
  53.4 28.6 %collective-permute-start.26 = (bf16[768,768]{1,0:T(8,128)(2,1)}, bf16[768,768]{1,0:T(8,128)(2,1)}, u32[]{:S(2)}, u32[]{:S(2)}) collective-permute-start(bf16[768,768]{1,0:T(8,128)(2,1)} %w0), channel_id=1, source_target_pairs={{0,2},{1,3},{2,0},{3,1},{4,6},{5,7},{6,4},{7,5},{8,10},{9,11},{10,... | collective-permute-start | bytes 3538952 | tf_op jit(solution)/shard_map/ppermute | solution.py:523
  58.1 55.6 %collective-permute-start.22 = (bf16[192,3072]{1,0:T(8,128)(2,1)S(1)}, bf16[192,3072]{1,0:T(8,128)(2,1)}, u32[]{:S(2)}, u32[]{:S(2)}) collective-permute-start(bf16[192,3072]{1,0:T(8,128)(2,1)S(1)} %copy-done.2), channel_id=1, source_target_pairs={{0,1},{1,0},{2,3},{3,2},{4,5},{5,4},{6,7},{7,6},{8,9},{9,8},{10,11... | collective-permute-start | bytes 3538952 | tf_op jit(solution)/shard_map/ppermute | solution.py:523
  58.5 55.3 %collective-permute-start.24 = (bf16[192,3072]{1,0:T(8,128)(2,1)S(1)}, bf16[192,3072]{1,0:T(8,128)(2,1)}, u32[]{:S(2)}, u32[]{:S(2)}) collective-permute-start(bf16[192,3072]{1,0:T(8,128)(2,1)S(1)} %collective-permute-done.23.i2), channel_id=1, source_target_pairs={{0,1},{1,0},{2,3},{3,2},{4,5},{5,4},{6,7},{7,6},{8,9},{9,8},{10,11... | collective-permute-start | bytes 3538952 | tf_op jit(solution)/shard_map/ppermute | solution.py:523
  75.1 48.0 %collective-permute-start.25 = (bf16[768,768]{1,0:T(8,128)(2,1)}, bf16[768,768]{1,0:T(8,128)(2,1)}, u32[]{:S(2)}, u32[]{:S(2)}) collective-permute-start(bf16[768,768]{1,0:T(8,128)(2,1)} %w0), channel_id=1, source_target_pairs={{0,1},{1,0},{2,3},{3,2},{4,5},{5,4},{6,7},{7,6},{8,9},{9,8},{10,11... | collective-permute-start | bytes 3538952 | tf_op jit(solution)/shard_map/ppermute | solution.py:523
  82.1 41.1 %collective-permute-start.27 = (bf16[768,768]{1,0:T(8,128)(2,1)}, bf16[768,768]{1,0:T(8,128)(2,1)}, u32[]{:S(2)}, u32[]{:S(2)}) collective-permute-start(bf16[768,768]{1,0:T(8,128)(2,1)} %collective-permute-done.26.w2), channel_id=1, source_target_pairs={{0,1},{1,0},{2,3},{3,2},{4,5},{5,4},{6,7},{7,6},{8,9},{9,8},{10,11... | collective-permute-start | bytes 3538952 | tf_op jit(solution)/shard_map/ppermute | solution.py:523
  149.3 45.4 %collective-permute-start.45 = (bf16[2,4,256,768]{3,2,1,0:T(8,128)(2,1)}, bf16[2,4,256,768]{3,2,1,0:T(8,128)(2,1)S(1)}, u32[]{:S(2)}, u32[]{:S(2)}) collective-permute-start(bf16[2,4,256,768]{3,2,1,0:T(8,128)(2,1)} %get-tuple-element.97), channel_id=1, source_target_pairs={{0,1},{1,0},{2,3},{3,2},{4,5},{5,4},{6,7},{7,6},{8,9},{9,8},{10,11... | collective-permute-start | bytes 9437192 | tf_op jit(solution)/shard_map/ppermute | solution.py:523
  150.8 39.9 %collective-permute-start.53 = (bf16[2,4,192,768]{3,2,1,0:T(8,128)(2,1)}, bf16[2,4,192,768]{3,2,1,0:T(8,128)(2,1)}, u32[]{:S(2)}, u32[]{:S(2)}) collective-permute-start(bf16[2,4,192,768]{3,2,1,0:T(8,128)(2,1)} %get-tuple-element.102), channel_id=1, source_target_pairs={{0,1},{1,0},{2,3},{3,2},{4,5},{5,4},{6,7},{7,6},{8,9},{9,8},{10,11... | collective-permute-start | bytes 7077896 | tf_op jit(solution)/shard_map/ppermute | solution.py:523
  193.2 28.9 %collective-permute-start.54 = (bf16[4,192,768]{2,1,0:T(8,128)(2,1)S(1)}, bf16[4,192,768]{2,1,0:T(8,128)(2,1)S(1)}, u32[]{:S(2)}, u32[]{:S(2)}) collective-permute-start(bf16[4,192,768]{2,1,0:T(8,128)(2,1)S(1)} %fusion.3), channel_id=1, source_target_pairs={{0,2},{1,3},{2,0},{3,1},{4,6},{5,7},{6,4},{7,5},{8,10},{9,11},{10,... | collective-permute-start | bytes 3538952 | tf_op jit(solution)/shard_map/ppermute | solution.py:523
  195.6 60.2 %collective-permute-start.46 = (bf16[4,256,768]{2,1,0:T(8,128)(2,1)S(1)}, bf16[4,256,768]{2,1,0:T(8,128)(2,1)S(1)}, u32[]{:S(2)}, u32[]{:S(2)}) collective-permute-start(bf16[4,256,768]{2,1,0:T(8,128)(2,1)S(1)} %fusion.2), channel_id=1, source_target_pairs={{0,2},{1,3},{2,0},{3,1},{4,6},{5,7},{6,4},{7,5},{8,10},{9,11},{10,... | collective-permute-start | bytes 4718600 | tf_op jit(solution)/shard_map/ppermute | solution.py:523
  197.1 60.5 %collective-permute-start.35 = (bf16[256,768]{1,0:T(8,128)(2,1)S(1)}, bf16[256,768]{1,0:T(8,128)(2,1)S(1)}, u32[]{:S(2)}, u32[]{:S(2)}) collective-permute-start(bf16[256,768]{1,0:T(8,128)(2,1)S(1)} %slice.281), channel_id=1, source_target_pairs={{0,4},{1,5},{2,6},{3,7},{4,0},{5,1},{6,2},{7,3},{8,12},{9,13},{10,... | collective-permute-start | bytes 1179656 | tf_op jit(solution)/shard_map/ppermute | solution.py:523
  199.0 75.9 %collective-permute-start.39 = (bf16[2,112,1152]{2,1,0:T(8,128)(2,1)S(1)}, bf16[2,112,1152]{2,1,0:T(8,128)(2,1)S(1)}, u32[]{:S(2)}, u32[]{:S(2)}) collective-permute-start(bf16[2,112,1152]{2,1,0:T(8,128)(2,1)S(1)} %fusion.8), channel_id=1, source_target_pairs={{0,2},{1,3},{2,0},{3,1},{4,6},{5,7},{6,4},{7,5},{8,10},{9,11},{10,... | collective-permute-start | bytes 1548296 | tf_op jit(solution)/shard_map/ppermute | solution.py:523
  222.3 38.3 %collective-permute-start.55 = (bf16[2,192,768]{2,1,0:T(8,128)(2,1)S(1)}, bf16[2,192,768]{2,1,0:T(8,128)(2,1)S(1)}, u32[]{:S(2)}, u32[]{:S(2)}) collective-permute-start(bf16[2,192,768]{2,1,0:T(8,128)(2,1)S(1)} %slice.279), channel_id=1, source_target_pairs={{0,4},{1,5},{2,6},{3,7},{4,0},{5,1},{6,2},{7,3},{8,12},{9,13},{10,... | collective-permute-start | bytes 1769480 | tf_op jit(solution)/shard_map/ppermute | solution.py:523
  257.8 66.2 %collective-permute-start.36 = (bf16[128,768]{1,0:T(8,128)(2,1)S(1)}, bf16[128,768]{1,0:T(8,128)(2,1)S(1)}, u32[]{:S(2)}, u32[]{:S(2)}) collective-permute-start(bf16[128,768]{1,0:T(8,128)(2,1)S(1)} %get-tuple-element.103), channel_id=1, source_target_pairs={{0,0},{16,1},{2,2},{18,3},{4,4},{20,5},{6,6},{22,7},{1,8},{17,9},{... | collective-permute-start | bytes 589832 | tf_op jit(solution)/shard_map/ppermute | solution.py:528
  258.5 65.6 %collective-permute-start.37 = (bf16[128,768]{1,0:T(8,128)(2,1)S(1)}, bf16[128,768]{1,0:T(8,128)(2,1)S(1)}, u32[]{:S(2)}, u32[]{:S(2)}) collective-permute-start(bf16[128,768]{1,0:T(8,128)(2,1)S(1)} %get-tuple-element.104), channel_id=1, source_target_pairs={{8,0},{24,1},{10,2},{26,3},{12,4},{28,5},{14,6},{30,7},{9,8},{25,9... | collective-permute-start | bytes 589832 | tf_op jit(solution)/shard_map/ppermute | solution.py:528
  275.0 20.8 %collective-permute-start.40 = (bf16[1,112,1152]{2,1,0:T(8,128)(2,1)S(1)}, bf16[1,112,1152]{2,1,0:T(8,128)(2,1)S(1)}, u32[]{:S(2)}, u32[]{:S(2)}) collective-permute-start(bf16[1,112,1152]{2,1,0:T(8,128)(2,1)S(1)} %slice.283), channel_id=1, source_target_pairs={{0,8},{1,9},{2,10},{3,11},{4,12},{5,13},{6,14},{7,15},{8,0},{9,1},... | collective-permute-start | bytes 774152 | tf_op jit(solution)/shard_map/ppermute | solution.py:523
  276.6 19.7 %collective-permute-start.57 = (bf16[192,768]{1,0:T(8,128)(2,1)S(1)}, bf16[192,768]{1,0:T(8,128)(2,1)S(1)}, u32[]{:S(2)}, u32[]{:S(2)}) collective-permute-start(bf16[192,768]{1,0:T(8,128)(2,1)S(1)} %fusion.11), channel_id=1, source_target_pairs={{0,16},{1,17},{2,18},{3,19},{4,20},{5,21},{6,22},{7,23},{8,24},{9,... | collective-permute-start | bytes 884744 | tf_op jit(solution)/shard_map/ppermute | solution.py:523
  293.2 25.7 %collective-permute-start.49 = (bf16[256,768]{1,0:T(8,128)(2,1)S(1)}, bf16[256,768]{1,0:T(8,128)(2,1)S(1)}, u32[]{:S(2)}, u32[]{:S(2)}) collective-permute-start(bf16[256,768]{1,0:T(8,128)(2,1)S(1)} %fusion.10), channel_id=1, source_target_pairs={{0,16},{1,17},{2,18},{3,19},{4,20},{5,21},{6,22},{7,23},{8,24},{9,... | collective-permute-start | bytes 1179656 | tf_op jit(solution)/shard_map/ppermute | solution.py:523
  296.0 27.8 %collective-permute-start.41 = (bf16[112,1152]{1,0:T(8,128)(2,1)S(1)}, bf16[112,1152]{1,0:T(8,128)(2,1)S(1)}, u32[]{:S(2)}, u32[]{:S(2)}) collective-permute-start(bf16[112,1152]{1,0:T(8,128)(2,1)S(1)} %fusion.12), channel_id=1, source_target_pairs={{0,16},{1,17},{2,18},{3,19},{4,20},{5,21},{6,22},{7,23},{8,24},{9,... | collective-permute-start | bytes 774152 | tf_op jit(solution)/shard_map/ppermute | solution.py:523
  296.5 43.1 %collective-permute-start.58 = (bf16[192,768]{1,0:T(8,128)(2,1)S(1)}, bf16[192,768]{1,0:T(8,128)(2,1)S(1)}, u32[]{:S(2)}, u32[]{:S(2)}) collective-permute-start(bf16[192,768]{1,0:T(8,128)(2,1)S(1)} %add_convert_fusion.1.p0), channel_id=1, source_target_pairs={{0,8},{1,9},{2,10},{3,11},{4,12},{5,13},{6,14},{7,15},{8,0},{9,1},... | collective-permute-start | bytes 884744 | tf_op jit(solution)/shard_map/ppermute | solution.py:523
  318.9 22.7 %collective-permute-start.50 = (bf16[256,768]{1,0:T(8,128)(2,1)S(1)}, bf16[256,768]{1,0:T(8,128)(2,1)S(1)}, u32[]{:S(2)}, u32[]{:S(2)}) collective-permute-start(bf16[256,768]{1,0:T(8,128)(2,1)S(1)} %add_convert_fusion.p0), channel_id=1, source_target_pairs={{0,8},{1,9},{2,10},{3,11},{4,12},{5,13},{6,14},{7,15},{8,0},{9,1},... | collective-permute-start | bytes 1179656 | tf_op jit(solution)/shard_map/ppermute | solution.py:523
  339.8 27.9 %collective-permute-start.51 = (bf16[256,768]{1,0:T(8,128)(2,1)S(1)}, bf16[256,768]{1,0:T(8,128)(2,1)S(1)}, u32[]{:S(2)}, u32[]{:S(2)}) collective-permute-start(bf16[256,768]{1,0:T(8,128)(2,1)S(1)} %add_convert_fusion.p0), channel_id=1, source_target_pairs={{0,4},{1,5},{2,6},{3,7},{4,0},{5,1},{6,2},{7,3},{8,12},{9,13},{10,... | collective-permute-start | bytes 1179656 | tf_op jit(solution)/shard_map/ppermute | solution.py:523
  341.6 33.6 %collective-permute-start.52 = (bf16[256,768]{1,0:T(8,128)(2,1)S(1)}, bf16[256,768]{1,0:T(8,128)(2,1)S(1)}, u32[]{:S(2)}, u32[]{:S(2)}) collective-permute-start(bf16[256,768]{1,0:T(8,128)(2,1)S(1)} %collective-permute-done.50.p1), channel_id=1, source_target_pairs={{0,4},{1,5},{2,6},{3,7},{4,0},{5,1},{6,2},{7,3},{8,12},{9,13},{10,... | collective-permute-start | bytes 1179656 | tf_op jit(solution)/shard_map/ppermute | solution.py:523
  (75 other events, 1132.5 us)

commit v2 on v0

--- a/solution.py
+++ b/solution.py
@@ -3,6 +3,8 @@
 import jax
 import jax.numpy as jnp
 from jax import lax
+from jax.experimental import pallas as pl
+from jax.experimental.pallas import tpu as pltpu
 from jax.sharding import PartitionSpec as P
 
 D = 768
@@ -498,6 +500,769 @@
     return (outputs, input_grad) + tuple(summed)
 
 
+HALF = D // 2
+ROWS = 128
+
+
+def flat(z, x, y, k):
+    return (z * 2 + x) * 4 + y * 2 + k
+
+
+def table(move):
+    return [
+        (flat(z, x, y, k), flat(*move(z, x, y, k)))
+        for z in range(4)
+        for x in range(2)
+        for y in range(2)
+        for k in range(2)
+    ]
+
+
+def permute(move):
+    pairs = table(move)
+    return lambda block: lax.ppermute(block, ("ctx", "fsdp"), pairs)
+
+
+def permute_back(move):
+    pairs = [(b, a) for a, b in table(move)]
+    return lambda block: lax.ppermute(block, ("ctx", "fsdp"), pairs)
+
+
+def to_seq(turn):
+    return lambda z, x, y, k: (2 * k + (z // 2 + turn) % 2, x, y, z % 2)
+
+
+swap_core = permute(lambda z, x, y, k: (z, x, y, k ^ 1))
+swap_y = permute(lambda z, x, y, k: (z, x, y ^ 1, k))
+swap_x = permute(lambda z, x, y, k: (z, x ^ 1, y, k))
+swap_z1 = permute(lambda z, x, y, k: (z ^ 1, x, y, k))
+swap_z2 = permute(lambda z, x, y, k: (z ^ 2, x, y, k))
+seq_send = (permute(to_seq(0)), permute(to_seq(1)))
+seq_return = (permute_back(to_seq(0)), permute_back(to_seq(1)))
+
+
+def low(value):
+    return value.astype(jnp.bfloat16)
+
+
+def wide(value):
+    return value.astype(jnp.float32)
+
+
+def pick(array, index, axis=0):
+    return lax.dynamic_index_in_dim(array, index, axis, keepdims=False)
+
+
+def dot_nt(a, b):
+    return lax.dot_general(a, b, (((1,), (1,)), ((), ())), preferred_element_type=jnp.float32)
+
+
+def dot_tn(a, b):
+    return lax.dot_general(a, b, (((0,), (0,)), ((), ())), preferred_element_type=jnp.float32)
+
+
+def coords(info):
+    c, f = info[0] >> 2, info[0] & 3
+    return c >> 1, c & 1, f >> 1, f & 1, c, f
+
+
+def pack_kernel(
+    info, lens, rows, grads, w_q, w_k, w_v, v0, v1, v2, v3, v4, v5, v6, v7, wide_vec,
+    t0, t1, cot, w_x, small, held,
+):
+    z, x, _, _, _, _ = coords(info)
+    zh = z >> 1
+    t0[...] = rows[zh]
+    t1[...] = rows[1 - zh]
+    cot[:ROWS] = grads[zh]
+    cot[ROWS:] = grads[1 - zh]
+    columns = pl.ds(pl.multiple_of(x * HALF, 128), HALF)
+    for n, weight in enumerate((w_q, w_k, w_v)):
+        w_x[:, HALF * n : HALF * n + HALF] = weight[:, columns]
+    held[...] = jnp.zeros_like(held)
+    for n, vector in enumerate((v0, v1, v2, v3, v4, v5, v6, v7)):
+        held[n : n + 1, :192] = wide(vector[...]).reshape(1, 192)
+    held[8:9, :] = wide(wide_vec[...]).reshape(1, D)
+    lane = lax.broadcasted_iota(jnp.int32, (1, D), 1)
+    ends = jnp.zeros((1, D), jnp.int32)
+    for n in range(2):
+        ends = jnp.where(lane == n, lens[n] >> 7, ends)
+        ends = jnp.where(lane == 2 + n, lens[n] & 127, ends)
+    held[9:10, :] = wide(ends)
+    small[...] = low(held[...])
+
+
+def attend_kernel(
+    info, b0, b1, b2, b3, b4, b5, b6, b7, w0, w1, w2, w3, s0, s1, s2, s3,
+    xs, ws, q_out, k_out, v_out, p_out, cu, cv, cxu, cxv, key_bias, small,
+):
+    step = pl.program_id(0)
+    z, x, y, k, _, f = coords(info)
+
+    @pl.when(step == 0)
+    def _():
+        for n, piece in enumerate((s0, s1, s2, s3)):
+            small[f ^ n] = wide(piece[...])
+        line = small[2 * y + (z >> 1)][9:10, :]
+        lane = lax.broadcasted_iota(jnp.int32, (1, D), 1)
+        part = jnp.where(lane == (z & 1), 128.0 * line, 0.0)
+        part = part + jnp.where(lane == 2 + (z & 1), line, 0.0)
+        end = jnp.sum(part, axis=1, keepdims=True)
+        z_low = 2 * (z & 1)
+        blocks = (b0, b1, b2, b3, b4, b5, b6, b7)
+        for n, block in enumerate(blocks):
+            z_block = (z_low if n % 2 == 0 else 2 - z_low) + (k if n < 4 else 1 - k)
+            x_block = x if n % 4 < 2 else 1 - x
+            xs[n * ROWS : (n + 1) * ROWS, :] = block[...]
+            place = (2 * z_block + x_block) * ROWS + lax.broadcasted_iota(jnp.int32, (1, ROWS), 1)
+            key_bias[:, n * ROWS : (n + 1) * ROWS] = jnp.where(wide(place) < end, 0.0, NEG_FILL)
+        for n, piece in enumerate((w0, w1, w2, w3)):
+            ws[pl.ds(pl.multiple_of(192 * (f ^ n), 64), 192), :] = piece[...]
+
+        def bias(row):
+            return jnp.concatenate(
+                [small[2 * x + n][row : row + 1, :192] for n in range(2)], axis=1
+            )
+
+        q_out[...] = low(wide(low(matmul(xs[: 4 * ROWS, :], ws[:, :HALF]) + bias(0))) * SCALE)
+        k_out[...] = low(matmul(xs[...], ws[:, HALF : 2 * HALF]))
+        v_out[...] = low(matmul(xs[...], ws[:, 2 * HALF :]) + bias(1))
+
+    lanes = pl.ds(pl.multiple_of(step * 128, 128), 128)
+    first = lax.broadcasted_iota(jnp.int32, (1, 128), 1) < HD
+    queries = q_out[:, lanes]
+    keys = k_out[:, lanes]
+    values = v_out[:, lanes]
+    for part in range(2):
+        rows = slice(part * 256, part * 256 + 256)
+        found = []
+        for head in range(2):
+            mine = first if head == 0 else jnp.logical_not(first)
+            scores = dot_nt(jnp.where(mine, queries[rows], 0), keys) + key_bias[...]
+            top = jnp.max(scores, axis=1, keepdims=True)
+            weights = jnp.exp(scores - top)
+            total = jnp.sum(weights, axis=1, keepdims=True)
+            probs = low(weights * (1.0 / total))
+            p_out[head, rows, :] = probs
+            found.append(matmul(probs, values))
+        context = low(jnp.where(first, found[0], found[1]))
+        one, two = (cu, cv) if part == 0 else (cxu, cxv)
+        one[...] = context[:ROWS]
+        two[...] = context[ROWS:]
+
+
+def pair_back(queries_ref, keys, values, probs_ref, grads):
+    first = lax.broadcasted_iota(jnp.int32, (1, 128), 1) < HD
+    grad_k = jnp.zeros((8 * ROWS, 128), jnp.float32)
+    grad_v = jnp.zeros((8 * ROWS, 128), jnp.float32)
+    grad_qs = []
+    for part in range(2):
+        rows = slice(part * 256, part * 256 + 256)
+        one, two = grads[2 * part : 2 * part + 2]
+        grad_rows = jnp.concatenate([one[...], two[...]], axis=0)
+        queries = queries_ref[rows, :]
+        grad_q = jnp.zeros((256, 128), jnp.float32)
+        for head in range(2):
+            mine = first if head == 0 else jnp.logical_not(first)
+            grad_mine = jnp.where(mine, grad_rows, 0)
+            probs = probs_ref[head, rows, :]
+            grad_probs = dot_nt(grad_mine, values)
+            product = wide(probs) * grad_probs
+            delta = jnp.sum(product, axis=1, keepdims=True)
+            grad_scores = low(product - wide(probs) * delta)
+            grad_q = grad_q + matmul(grad_scores, jnp.where(mine, keys, 0))
+            grad_k = grad_k + dot_tn(grad_scores, jnp.where(mine, queries, 0))
+            grad_v = grad_v + dot_tn(probs, grad_mine)
+        grad_qs.append(low(grad_q * SCALE))
+    return grad_qs, low(grad_k), low(grad_v)
+
+
+def attend_back_kernel(queries, keys, values, probs, gu, gv, gxu, gxv, dq, dk, dv):
+    grad_qs, dk[...], dv[...] = pair_back(
+        queries, keys[...], values[...], probs, (gu, gv, gxu, gxv)
+    )
+    dq[:256, :], dq[256:, :] = grad_qs
+
+
+def attend_last_kernel(
+    info, xs, ws, queries, keys, values, probs, gu, gv, gxu, gxv, dq_in, dk_in, dv_in,
+    dx_own, dx_other, keep, send, dq, dk, dv, dw,
+):
+    cut = 2 * 128
+    grad_qs, grad_k, grad_v = pair_back(
+        queries, keys[...], values[...], probs, (gu, gv, gxu, gxv)
+    )
+    dq[:, :cut], dk[:, :cut], dv[:, :cut] = dq_in[...], dk_in[...], dv_in[...]
+    dq[:256, cut:], dq[256:, cut:] = grad_qs
+    dk[:, cut:], dv[:, cut:] = grad_k, grad_v
+    own = slice(0, 4 * ROWS)
+    other = slice(4 * ROWS, 8 * ROWS)
+    w_q, w_k, w_v = ws[:, :HALF], ws[:, HALF : 2 * HALF], ws[:, 2 * HALF :]
+    dx_other[...] = low(dot_nt(dk[other, :], w_k) + dot_nt(dv[other, :], w_v))
+    dx_own[...] = dot_nt(dq[...], w_q) + dot_nt(dk[own, :], w_k) + dot_nt(dv[own, :], w_v)
+    dw[:, :HALF] = low(dot_tn(xs[own, :], dq[...]))
+    dw[:, HALF : 2 * HALF] = low(dot_tn(xs[...], dk[...]))
+    dw[:, 2 * HALF :] = low(dot_tn(xs[...], dv[...]))
+    col_sums = jnp.concatenate(
+        [
+            jnp.sum(wide(dq[...]), axis=0, keepdims=True),
+            jnp.zeros((1, HALF), jnp.float32),
+            jnp.sum(wide(dv[...]), axis=0, keepdims=True),
+        ],
+        axis=1,
+    )
+    tail = low(jnp.where(lax.broadcasted_iota(jnp.int32, (16, 1), 0) == 0, col_sums, 0.0))
+    z, _, _, _, _, f = coords(info)
+    for n in range(4):
+        place = send if n % 2 else keep
+        for half in range(2):
+            start = pl.multiple_of(192 * (f ^ n) + 96 * half, 32)
+            place[n // 2, half ^ (z & 1), :96, :] = dw[pl.ds(start, 96), :]
+            place[n // 2, half ^ (z & 1), 96:, :] = tail if half == 0 else tail * 0
+
+
+def middle_one_kernel(
+    info, cm0, cm1, co0, co1, x0, x1, o0, o1, o2, o3, inner_weight, s0, s1, s2, s3,
+    hidden_out, normed_out, inv_out, act, slope, vec, ctx, low_rows, small, order,
+):
+    step = pl.program_id(0)
+    _, x, _, _, _, f = coords(info)
+
+    @pl.when(step == 0)
+    def _():
+        for n, piece in enumerate((s0, s1, s2, s3)):
+            small[f ^ n] = wide(piece[...])
+            order[n] = wide(piece[...])
+        for n in range(8):
+            vec[n : n + 1, :] = jnp.concatenate(
+                [small[m][n : n + 1, :192] for m in range(4)], axis=1
+            )
+        for side, (one, two) in enumerate(((cm0, cm1), (co0, co1))):
+            rows = jnp.concatenate([one[...], two[...]], axis=0)
+            for part in range(2):
+                ctx[2 * (x ^ side) + part] = rows[:, 192 * part : 192 * part + 192]
+        total = wide(jnp.concatenate([x0[...], x1[...]], axis=0)) + vec[2:3, :]
+        for n, piece in enumerate((o0, o1, o2, o3)):
+            total = total + matmul(ctx[f ^ n], piece[...])
+        hidden, normed, inv = layer_norm(total, vec[3:4, :], vec[4:5, :])
+        hidden_out[...] = hidden
+        normed_out[...] = normed
+        inv_out[...] = inv
+        low_rows[...] = low(hidden)
+
+    pre = matmul(low_rows[...], inner_weight[...]) + order[step][8:9, :]
+    bell = 0.5 * (1.0 + lax.erf(pre * ROOT_HALF))
+    act[0] = low(pre * bell)
+    slope[0] = low(bell + pre * INV_ROOT_TAU * jnp.exp(-0.5 * pre * pre))
+
+
+def norm_grad(grad, normed, inv, gain):
+    scaled = grad * gain
+    return inv * (
+        scaled
+        - jnp.mean(scaled, axis=-1, keepdims=True)
+        - normed * jnp.mean(scaled * normed, axis=-1, keepdims=True)
+    )
+
+
+def column_sum(value):
+    return jnp.sum(value, axis=0, keepdims=True)
+
+
+def middle_two_kernel(
+    info, lens, act, act_block, hidden, cot, vec, w0, w1, w2, w3,
+    out, second_out, outer_out, sums, keep, send, w_all, w_sem,
+):
+    step = pl.program_id(0)
+    z, x, _, _, c, f = coords(info)
+
+    @pl.when(step == 0)
+    def _():
+        copies = [
+            pltpu.make_async_copy(ref, w_all.at[n], w_sem.at[n])
+            for n, ref in enumerate((w0, w1, w2, w3))
+        ]
+        for copy in copies:
+            copy.start()
+        b_2, g_2, s_2 = vec[5:6, :], vec[6:7, :], vec[7:8, :]
+        total = hidden[...] + b_2
+        for n in range(4):
+            copies[n].wait()
+            total = total + matmul(act[n], w_all[n])
+        result, normed, inv = layer_norm(total, g_2, s_2)
+        zh = z >> 1
+        out[zh] = low(result[:ROWS])
+        out[1 - zh] = low(result[ROWS:])
+        row = lax.broadcasted_iota(jnp.int32, (2 * ROWS, 1), 0)
+        end = jnp.where(row < ROWS, lens[zh], lens[1 - zh] + ROWS)
+        grad = wide(cot[...]) * jnp.where(row + c * ROWS < end, 1.0, 0.0)
+        grad_second = norm_grad(grad, normed, inv, g_2)
+        second_out[...] = grad_second
+        grad_outer = low(grad_second)
+        outer_out[...] = grad_outer
+        sums[...] = jnp.zeros_like(sums)
+        for n, value in enumerate((wide(grad_outer), grad * normed, grad)):
+            sums[n : n + 1, :] = column_sum(value)
+
+    @pl.when(step > 0)
+    def _():
+        grad = low(dot_tn(act_block[0], outer_out[...]))
+        for place, wanted in ((send, step < 3), (keep, step >= 3)):
+
+            @pl.when(wanted)
+            def _(place=place):
+                for n in range(4):
+                    place[0, n ^ (2 * (z & 1) + x)] = grad[192 * n : 192 * n + 192]
+
+
+def middle_three_kernel(
+    info, outer, second, slope, normed_one, inv_one, vec, inner_weight,
+    o0, o1, o2, o3, w0, w1, w2, w3,
+    first_out, gm0, gm1, go0, go1, inner_out, branch_out, sums,
+    o_all, i_all, w_all, gc, o_sem, i_sem, w_sem,
+):
+    _, x, _, _, _, f = coords(info)
+    copies = {}
+    for e in range(4):
+        columns = pl.ds(pl.multiple_of(D * (f ^ e), 128), D)
+        copies["w", e] = pltpu.make_async_copy((w0, w1, w2, w3)[e], w_all.at[e], w_sem.at[e])
+        copies["i", e] = pltpu.make_async_copy(
+            inner_weight.at[:, columns], i_all.at[e], i_sem.at[e]
+        )
+        copies["w", e].start()
+        copies["i", e].start()
+    for n, ref in enumerate((o0, o1, o2, o3)):
+        copies["o", n] = pltpu.make_async_copy(ref, o_all.at[n], o_sem.at[n])
+        copies["o", n].start()
+    sums[...] = jnp.zeros_like(sums)
+    grad_hidden = second[...]
+    for e in range(4):
+        copies["w", e].wait()
+        inner = low(dot_nt(outer[...], w_all[e]) * wide(slope[e]))
+        inner_out[e] = inner
+        sums[pl.ds(8 + (f ^ e), 1), :] = column_sum(wide(inner))
+        copies["i", e].wait()
+        grad_hidden = grad_hidden + dot_nt(inner, i_all[e])
+    grad_first = norm_grad(grad_hidden, normed_one[...], inv_one[...], vec[3:4, :])
+    first_out[...] = grad_first
+    branch = low(grad_first)
+    branch_out[...] = branch
+    for n, value in enumerate((wide(branch), grad_hidden * normed_one[...], grad_hidden)):
+        sums[n : n + 1, :] = column_sum(value)
+    for n in range(4):
+        copies["o", n].wait()
+        gc[f ^ n] = low(dot_nt(branch, o_all[n]))
+    for side, (one, two) in enumerate(((gm0, gm1), (go0, go1))):
+        rows = jnp.concatenate([gc[2 * (x ^ side)], gc[2 * (x ^ side) + 1]], axis=1)
+        one[...] = rows[:ROWS]
+        two[...] = rows[ROWS:]
+
+
+def middle_four_kernel(
+    info, inner, hidden, branch, cm0, cm1, co0, co1, sums_one, sums_two,
+    keep, send, held, out_held, vec_held,
+):
+    step = pl.program_id(0)
+    _, x, _, _, _, f = coords(info)
+    block = f ^ step
+
+    @pl.when(step == 0)
+    def _():
+        for side, (one, two) in enumerate(((cm0, cm1), (co0, co1))):
+            rows = jnp.concatenate([one[...], two[...]], axis=0)
+            start = pl.multiple_of(HALF * (x ^ side), 128)
+            out_held[pl.ds(start, HALF), :] = low(dot_tn(rows, branch[...]))
+        vec_held[...] = jnp.zeros_like(vec_held)
+        top = lax.broadcasted_iota(jnp.int32, (16, 1), 0) == 0
+        for n in range(4):
+            cut = slice(192 * n, 192 * n + 192)
+            lines = (
+                sums_two[8 + n : 9 + n, :],
+                jnp.concatenate(
+                    [sums_two[m : m + 1, cut] for m in range(3)] + [sums_one[0:1, cut]], axis=1
+                ),
+                jnp.concatenate(
+                    [sums_one[1:2, cut], sums_one[2:3, cut], jnp.zeros((1, HALF), jnp.float32)],
+                    axis=1,
+                ),
+            )
+            for m, line in enumerate(lines):
+                vec_held[m, n] = low(jnp.where(top, line, 0.0))
+
+    held[...] = low(dot_tn(low(hidden[...]), inner[0]))
+    for n in range(4):
+        place = send if n % 2 else keep
+        start = 192 * (f ^ n)
+        place[n // 2, 0, :192, :] = held[pl.ds(pl.multiple_of(start, 64), 192), :]
+        place[n // 2, 0, 192:240, :] = out_held[pl.ds(pl.multiple_of(start + 48 * block, 16), 48), :]
+        place[n // 2, 0, 240:, :] = vec_held[block, f ^ n]
+
+
+MIDDLE = 2 * ROWS
+VMEM_LIMIT = 56 * 1024 * 1024
+BF, FP = jnp.bfloat16, jnp.float32
+
+
+def whole(shape):
+    return pl.BlockSpec(tuple(shape), lambda *_: (0,) * len(shape))
+
+
+def lane_block(rows, start=0):
+    return pl.BlockSpec((rows, 128), lambda step, *_: (0, step + start))
+
+
+def call(kernel, name, grid, scalars, operands, outs, scratch=(), work=(1, 1)):
+    return pl.pallas_call(
+        kernel,
+        out_shape=[jax.ShapeDtypeStruct(shape, kind) for shape, kind, _ in outs],
+        grid_spec=pltpu.PrefetchScalarGridSpec(
+            num_scalar_prefetch=len(scalars),
+            grid=(grid,),
+            in_specs=[spec or whole(array.shape) for array, spec in operands],
+            out_specs=[spec or whole(shape) for shape, _, spec in outs],
+            scratch_shapes=list(scratch),
+        ),
+        compiler_params=pltpu.CompilerParams(
+            dimension_semantics=("arbitrary",), vmem_limit_bytes=VMEM_LIMIT
+        ),
+        cost_estimate=pl.CostEstimate(
+            flops=work[0] * 1_000_000_000, bytes_accessed=work[1] * 1_000_000, transcendentals=0
+        ),
+        name=name,
+    )(*scalars, *[array for array, _ in operands])
+
+
+def plain(arrays):
+    return [(array, None) for array in arrays]
+
+
+def anywhere(arrays):
+    return [(array, pl.BlockSpec(memory_space=pl.ANY)) for array in arrays]
+
+
+def probs_block(start=0):
+    return pl.BlockSpec((2, 4 * ROWS, 8 * ROWS), lambda step, *_: (step + start, 0, 0))
+
+
+def pack(info, lens, inputs, cotangent, weights, vectors):
+    return call(
+        pack_kernel, "pack", 1, (info, lens), plain([inputs, cotangent, *weights, *vectors]),
+        [
+            ((ROWS, D), BF, None), ((ROWS, D), BF, None), ((MIDDLE, D), BF, None),
+            ((192, 3 * HALF), BF, None), ((16, D), BF, None),
+        ],
+        [pltpu.VMEM((16, D), FP)], (1, 4),
+    )
+
+
+def attend(info, blocks, pieces, small):
+    return call(
+        attend_kernel, "attend", 3, (info,), plain([*blocks, *pieces, *small]),
+        [
+            ((8 * ROWS, D), BF, None), ((D, 3 * HALF), BF, None), ((4 * ROWS, HALF), BF, None),
+            ((8 * ROWS, HALF), BF, None), ((8 * ROWS, HALF), BF, None),
+            ((6, 4 * ROWS, 8 * ROWS), BF, probs_block()),
+        ]
+        + [((ROWS, HALF), BF, lane_block(ROWS))] * 4,
+        [pltpu.VMEM((1, 8 * ROWS), FP), pltpu.VMEM((4, 16, D), FP)], (10, 15),
+    )
+
+
+def attend_back(queries, keys, values, probs, grads):
+    return call(
+        attend_back_kernel, "attend_back", 2, (),
+        [
+            (queries, lane_block(4 * ROWS)), (keys, lane_block(8 * ROWS)),
+            (values, lane_block(8 * ROWS)), (probs, probs_block()),
+        ]
+        + [(grad, lane_block(ROWS)) for grad in grads],
+        [
+            ((4 * ROWS, 256), BF, lane_block(4 * ROWS)),
+            ((8 * ROWS, 256), BF, lane_block(8 * ROWS)),
+            ((8 * ROWS, 256), BF, lane_block(8 * ROWS)),
+        ],
+        (), (8, 10),
+    )
+
+
+def attend_last(info, xs, ws, queries, keys, values, probs, grads, parts):
+    joint = (2, 2, 112, 3 * HALF)
+    return call(
+        attend_last_kernel, "attend_last", 1, (info,),
+        plain([xs, ws])
+        + [
+            (queries, lane_block(4 * ROWS, 2)), (keys, lane_block(8 * ROWS, 2)),
+            (values, lane_block(8 * ROWS, 2)), (probs, probs_block(2)),
+        ]
+        + [(grad, lane_block(ROWS, 2)) for grad in grads]
+        + plain(parts),
+        [((4 * ROWS, D), FP, None), ((4 * ROWS, D), BF, None), (joint, BF, None), (joint, BF, None)],
+        [
+            pltpu.VMEM((4 * ROWS, HALF), BF), pltpu.VMEM((8 * ROWS, HALF), BF),
+            pltpu.VMEM((8 * ROWS, HALF), BF), pltpu.VMEM((D, 3 * HALF), BF),
+        ],
+        (8, 10),
+    )
+
+
+def middle_one(info, ctx, rows, out_p, inner_weight, small):
+    block = pl.BlockSpec((1, MIDDLE, D), lambda step, *_: (step, 0, 0))
+    return call(
+        middle_one_kernel, "middle_one", 4, (info,),
+        plain([*ctx, *rows, *out_p])
+        + [(inner_weight, pl.BlockSpec((D, D), lambda step, info: (0, (info[0] & 3) ^ step)))]
+        + plain(small),
+        [
+            ((MIDDLE, D), FP, None), ((MIDDLE, D), FP, None), ((MIDDLE, 1), FP, None),
+            ((4, MIDDLE, D), BF, block), ((4, MIDDLE, D), BF, block), ((8, D), FP, None),
+        ],
+        [
+            pltpu.VMEM((4, MIDDLE, 192), BF), pltpu.VMEM((MIDDLE, D), BF),
+            pltpu.VMEM((4, 16, D), FP), pltpu.VMEM((4, 16, D), FP),
+        ],
+        (4, 10),
+    )
+
+
+def middle_two(info, lens, act, hidden, cot, vec, outer_p):
+    def turn(step, *_):
+        at = jnp.maximum(step - 1, 0)
+        return (jnp.where(at < 2, 2 * at + 1, 2 * at - 4), 0, 0)
+
+    blocks = (2, 4, 192, D)
+    return call(
+        middle_two_kernel, "middle_two", 5, (info, lens),
+        [(act, None), (act, pl.BlockSpec((1, MIDDLE, D), turn))]
+        + plain([hidden, cot, vec])
+        + anywhere(outer_p),
+        [
+            ((2, ROWS, D), BF, None), ((MIDDLE, D), FP, None), ((MIDDLE, D), BF, None),
+            ((8, D), FP, None),
+            (blocks, BF, pl.BlockSpec((1, 4, 192, D), lambda s, *_: (jnp.maximum(s - 3, 0), 0, 0, 0))),
+            (blocks, BF, pl.BlockSpec((1, 4, 192, D), lambda s, *_: (jnp.where(s < 2, 0, 1), 0, 0, 0))),
+        ],
+        [pltpu.VMEM((4, D, D), BF), pltpu.SemaphoreType.DMA((4,))], (4, 10),
+    )
+
+
+def middle_three(info, outer, second, slope, normed, inv, vec, inner_weight, out_p, outer_p):
+    return call(
+        middle_three_kernel, "middle_three", 1, (info,),
+        plain([outer, second, slope, normed, inv, vec]) + anywhere([inner_weight, *out_p, *outer_p]),
+        [((MIDDLE, D), FP, None)]
+        + [((ROWS, HALF), BF, None)] * 4
+        + [((4, MIDDLE, D), BF, None), ((MIDDLE, D), BF, None), ((16, D), FP, None)],
+        [
+            pltpu.VMEM((4, 192, D), BF), pltpu.VMEM((4, D, D), BF), pltpu.VMEM((4, D, D), BF),
+            pltpu.VMEM((4, MIDDLE, 192), BF), pltpu.SemaphoreType.DMA((4,)),
+            pltpu.SemaphoreType.DMA((4,)), pltpu.SemaphoreType.DMA((4,)),
+        ],
+        (4, 14),
+    )
+
+
+def middle_four(info, inner, hidden, branch, ctx, sums):
+    def spot(step, info):
+        z, x, _, _, _, f = coords(info)
+        return (0, f ^ step ^ (2 * x + (z & 1)), 0, 0)
+
+    block = pl.BlockSpec((2, 1, 256, D), spot)
+    return call(
+        middle_four_kernel, "middle_four", 4, (info,),
+        [(inner, pl.BlockSpec((1, MIDDLE, D), lambda step, *_: (step, 0, 0)))]
+        + plain([hidden, branch, *ctx, *sums]),
+        [((2, 4, 256, D), BF, block)] * 2,
+        [pltpu.VMEM((D, D), BF), pltpu.VMEM((D, D), BF), pltpu.VMEM((4, 4, 16, D), BF)],
+        (4, 8),
+    )
+
+
+def place_outer_kernel(info, p0, p1, p2, p3, out):
+    z, x, _, _, _, _ = coords(info)
+    for n, piece in enumerate((p0, p1, p2, p3)):
+        out[pl.ds(pl.multiple_of(192 * (n ^ (2 * (z & 1) + x)), 64), 192), :] = wide(piece[...])
+
+
+def place_inner_kernel(info, p0, p1, p2, p3, inner, out, vec):
+    z, x, _, _, _, _ = coords(info)
+    for n, piece in enumerate((p0, p1, p2, p3)):
+        at = n ^ (2 * x + (z & 1))
+        inner[:, pl.ds(pl.multiple_of(D * at, 128), D)] = wide(piece[:192, :])
+        out[pl.ds(pl.multiple_of(48 * at, 16), 48), :] = wide(piece[192:240, :])
+        vec[at] = wide(piece[240:, :])
+
+
+def place_joint_kernel(info, p0, p1, p2, p3, query, key, value, vec):
+    z, x, _, _, _, _ = coords(info)
+    z_bit = z & 1
+    for n, piece in enumerate((p0, p1, p2, p3)):
+        rows = pl.ds(pl.multiple_of(96 * (n % 2 ^ z_bit), 32), 96)
+        columns = pl.ds(pl.multiple_of(HALF * (n // 2 ^ x), 128), HALF)
+        for m, out in enumerate((query, key, value)):
+            out[rows, columns] = wide(piece[:96, HALF * m : HALF * m + HALF])
+        vec[n // 2 ^ x, n % 2 ^ z_bit] = wide(piece[96:, :])
+
+
+def placed(kernel, name, info, pieces, shapes):
+    return call(
+        kernel, name, 1, (info,), plain(pieces), [(shape, FP, None) for shape in shapes], (), (1, 6)
+    )
+
+
+def unshuffle(array, bit):
+    return jnp.where(bit == 0, array, array[::-1])
+
+
+def tied(values, *events):
+    return lax.optimization_barrier((values, events))[0]
+
+
+def z_level(low_half):
+    one = low(wide(low_half) + wide(swap_z2(low_half)))
+    return one
+
+
+def fast_body(
+    inputs, cotangent, lengths, w_query, b_query, w_key, w_value, b_value, w_output, b_output,
+    gain_one, bias_one, w_inner, b_inner, w_outer, b_outer, gain_two, bias_two,
+):
+    info = lax.axis_index(("ctx", "fsdp")).astype(jnp.int32).reshape(1)
+    f = lax.axis_index("fsdp")
+    zh = lax.axis_index("ctx") // 4
+
+    inner_weight = lax.all_gather(w_inner, "fsdp", axis=0, tiled=True)
+    t0, t1, cot, w_x, small = pack(
+        info, lengths, inputs, cotangent, (w_query, w_key, w_value),
+        (b_query, b_value, b_output, gain_one, bias_one, b_outer, gain_two, bias_two, b_inner),
+    )
+
+    bu, bv = seq_send[0](t0), seq_send[1](t1)
+    w_y, small_y, out_y = swap_y(w_x), swap_y(small), swap_y(tied(w_output, t0))
+    bu, bv, small_y = tied((bu, bv, small_y))
+    bxu, bxv = swap_x(bu), swap_x(bv)
+    bku, bkv = swap_core(bu), swap_core(bv)
+    bku, bkv, bxu, bxv, w_y, out_y = tied((bku, bkv, bxu, bxv, w_y, out_y))
+    outer_y = swap_y(tied(w_outer, out_y))
+    rest = [swap_core(b) for b in (bxu, bxv)] + [swap_core(tied(w_x, w_y)), swap_core(w_y)]
+    rest, small_y = tied((rest, small_y))
+    small_k, small_ky = swap_core(tied(small, rest)), swap_core(small_y)
+    blocks = [bu, bv, bxu, bxv, bku, bkv, rest[0], rest[1]]
+    qkv_p = [w_x, rest[2], w_y, rest[3]]
+    smalls = [small, small_k, small_y, small_ky]
+
+    xs, ws, queries, keys, values, probs, cu, cv, cxu, cxv = attend(info, blocks, qkv_p, smalls)
+
+    cu, cv = seq_return[0](cu), seq_return[1](cv)
+    cxu, cxv = swap_x(cxu), swap_x(cxv)
+    cu, cv, cxu, cxv = tied((cu, cv, cxu, cxv))
+    cxu, cxv = seq_return[0](cxu), seq_return[1](cxv)
+    out_k, out_ky = swap_core(tied(w_output, cu)), swap_core(tied(out_y, cu))
+    cxu, cxv, out_k, out_ky, outer_y = tied((cxu, cxv, out_k, out_ky, outer_y))
+    ctx = [cu, cv, cxu, cxv]
+    out_p = [w_output, out_k, out_y, out_ky]
+    outer_k, outer_ky = swap_core(tied(w_outer, cxu)), swap_core(outer_y)
+
+    hidden, normed, inv, act, slope, vec = middle_one(
+        info, ctx, [t0, t1], out_p, inner_weight, smalls
+    )
+    outer_p = [w_outer, outer_k, outer_y, outer_ky]
+    outputs, second, outer, sums_two, o_keep, o_send = middle_two(
+        info, lengths, act, hidden, cot, vec, outer_p
+    )
+    o_came = swap_core(o_send)
+    grad_first, gm0, gm1, go0, go1, inner, branch, sums_one = middle_three(
+        info, outer, second, slope, normed, inv, vec, inner_weight, out_p, outer_p
+    )
+    go0, go1 = seq_send[0](go0), seq_send[1](go1)
+    gm0, gm1 = seq_send[0](gm0), seq_send[1](gm1)
+    o_far = low(wide(o_keep[1]) + wide(o_came[1]))
+    o_near = wide(o_keep[0]) + wide(o_came[0])
+    o_came = swap_y(o_far[2:])
+    inner, o_far, o_near = tied((inner, o_far, o_near))
+    i_keep, i_send = middle_four(info, inner, hidden, branch, ctx, (sums_two, sums_one))
+    go0, go1, gm0, gm1, i_send, o_came = tied((go0, go1, gm0, gm1, i_send, o_came))
+    go0, go1 = swap_x(go0), swap_x(go1)
+    i_came = swap_core(i_send)
+    o_zed = swap_z1(low(o_near[2:] + wide(o_came)))
+    o_came = swap_y(tied(o_far[:2], o_came))
+    go0, go1, i_came = tied((go0, go1, i_came))
+    i_far = low(wide(i_keep[1, 2:]) + wide(i_came[1, 2:]))
+    i_far2 = low(wide(i_keep[1, :2]) + wide(i_came[1, :2]))
+    i_near = wide(i_keep[0]) + wide(i_came[0])
+    grads, i_far, i_far2, i_near = tied(([gm0, gm1, go0, go1], i_far, i_far2, i_near))
+    parts = attend_back(queries, keys, values, probs, grads)
+    i_came = swap_y(i_far)
+    parts, o_came, o_zed = tied((parts, o_came, o_zed))
+    o_sum = o_near[:2] + wide(o_came) + wide(o_zed)
+    o_came = swap_x(low(o_sum[1]))
+    dx_own, dx_other, j_keep, j_send = attend_last(
+        info, xs, ws, queries, keys, values, probs, grads, tied(parts, o_sum)
+    )
+    dx_own, dx_other, j_keep, j_send, o_came, i_came = tied(
+        (dx_own, dx_other, j_keep, j_send, o_came, i_came)
+    )
+    dx_came, j_came = swap_core(dx_other), swap_core(j_send)
+    i_sum = i_near[2:] + wide(i_came)
+    o_sum = low(o_sum[0] + wide(o_came))
+    i_came = swap_x(low(i_sum))
+    i_came2 = swap_y(tied(i_far2, i_sum))
+    o_came = swap_z2(o_sum)
+    dx_came, j_came = tied((dx_came, j_came))
+    dx = dx_own + wide(dx_came)
+    j_far = low(wide(j_keep[1]) + wide(j_came[1]))
+    j_near = wide(j_keep[0]) + wide(j_came[0])
+    dx_came = swap_x(low(dx[2 * ROWS :]))
+    i_came, i_came2, dx_came, o_came = tied((i_came, i_came2, dx_came, o_came))
+    j_came = swap_y(tied(j_far, i_came2))
+    o_sum = low(wide(o_sum) + wide(o_came))
+    i_sum = i_near[:2] + wide(i_came2) + wide(i_came)
+    dx = low(dx[: 2 * ROWS] + wide(dx_came))
+    i_came = swap_z1(low(i_sum[1]))
+    dx0, dx1 = seq_return[0](dx[:ROWS]), seq_return[1](dx[ROWS:])
+    o_x = swap_x(o_sum)
+    i_came, dx0, dx1, j_came, o_x = tied((i_came, dx0, dx1, j_came, o_x))
+    i_sum = low(i_sum[0] + wide(i_came))
+    j_sum = j_near + wide(j_came)
+    input_grad = grad_first + wide(jnp.concatenate([dx0, dx1], axis=0))
+    input_grad = unshuffle(input_grad.reshape(2, ROWS, D), zh)
+    i_came = swap_z2(i_sum)
+    j_came = swap_z1(low(j_sum[1]))
+    o_z, o_zx = swap_z1(o_sum), swap_z1(o_x)
+    j_came, i_came, o_z, o_zx = tied((j_came, i_came, o_z, o_zx))
+    j_sum = low(j_sum[0] + wide(j_came))
+    i_sum = low(wide(i_sum) + wide(i_came))
+    (outer_grad,) = placed(place_outer_kernel, "place_outer", info, [o_sum, o_x, o_z, o_zx], [(D, D)])
+    j_came = swap_z2(j_sum)
+    i_z, i_x = swap_z1(i_sum), swap_x(i_sum)
+    j_came, i_z, i_x = tied((j_came, i_z, i_x))
+    j_sum = low(wide(j_sum) + wide(j_came))
+    i_zx = swap_x(i_z)
+    j_z, j_x = swap_z1(j_sum), swap_x(j_sum)
+    j_z, j_x, i_zx = tied((j_z, j_x, i_zx))
+    j_zx = swap_x(j_z)
+    inner_grad, out_grad, lines = placed(
+        place_inner_kernel, "place_inner", info, [i_sum, i_z, i_x, i_zx],
+        [(192, 4 * D), (192, D), (4, 16, D)],
+    )
+    q_grad, k_grad, v_grad, joint_lines = placed(
+        place_joint_kernel, "place_joint", info, [j_sum, j_z, j_x, j_zx],
+        [(192, D)] * 3 + [(2, 2, 16, 3 * HALF)],
+    )
+    grad_b1 = lines[0, 0]
+    grad_bo, grad_g1, grad_s1, grad_b2 = (lines[1, 0, 192 * n : 192 * n + 192] for n in range(4))
+    grad_g2, grad_s2 = (lines[2, 0, 192 * n : 192 * n + 192] for n in range(2))
+    joint_sums = joint_lines[:, 0, 0]
+
+    def own(vector):
+        return lax.dynamic_slice_in_dim(vector.reshape(D), f * 192, 192)
+
+    grad_bq, grad_bv = own(joint_sums[:, :HALF]), own(joint_sums[:, 2 * HALF :])
+    return (
+        outputs, input_grad, q_grad, grad_bq, k_grad, v_grad, grad_bv, out_grad, grad_bo,
+        grad_g1, grad_s1, inner_grad, grad_b1, outer_grad, grad_b2, grad_g2, grad_s2,
+    )
+
+
 def solution(mesh):
     placed = (
         P("fsdp", "ctx", None),
@@ -519,8 +1284,9 @@
         P("fsdp"),
         P("fsdp"),
     )
+    fast = dict(mesh.shape) == {"ctx": 8, "fsdp": 4}
     return jax.shard_map(
-        body,
+        fast_body if fast else body,
         mesh=mesh,
         in_specs=placed,
         out_specs=(

time: 1120 us -> 317 us (0.28)
  blocking collectives: 461 us -> 0 us
  waiting for transfers between devices: 371 us -> 126 us
  matrix products: 120 us -> 0 us
  Pallas kernels: 0 us -> 84.2 us
  starting transfers between devices: 1.3 us -> 70.8 us
  local copies, waits for them, and re-layouts: 76.2 us -> 11.1 us
  other arithmetic: 67.4 us -> 8.71 us
    psum x1 -> x0, blocking collectives: 301 us -> none  [body(): lax.psum((shard_grads[0], shard_grads[1], shard_grads[2], shard_grads[3],...]
    all_gather x14 -> x1, waiting for transfers between devices: 245 us -> 0.01 us  [fast_body(): inner_weight = lax.all_gather(w_inner, 'fsdp', axis=0, tiled=True)]
    all_gather x5 -> x0, blocking collectives: 135 us -> none  [the longest x2 65.3 us: body(): lax.all_gather(log_total.transpose(0, 2, 1), 'ctx', axis=1, tiled=True)]
    ppermute x0 -> x61, waiting for transfers between devices: none -> 125 us  [the longest x55 108 us: permute(): return lambda block: lax.ppermute(block, ('ctx', 'fsdp'), pairs)]
    dot_general x52 -> x0, matrix products: 120 us -> none  [the longest x4 22.8 us: key_grad_step(): jnp.einsum('bhqk,bqhd->bkhd', grad_scores, split_heads(query_rows), prefe...]
    reduce_scatter x3 -> x0, waiting for transfers between devices: 99.7 us -> none  [the longest x1 50.4 us: body(): lax.psum_scatter(grad_set[11].astype(jnp.bfloat16), 'fsdp', scatter_dimen...]
    pallas_call x0 -> x11, Pallas kernels: none -> 84.2 us  [call(): pl.pallas_call(kernel, out_shape=[jax.ShapeDtypeStruct(shape, kind) for s...]
    ppermute x0 -> x61, starting transfers between devices: none -> 70.7 us  [the longest x55 60 us: permute(): return lambda block: lax.ppermute(block, ('ctx', 'fsdp'), pairs)]
  transfers between devices with their start and end apart: 20 -> 62, of which waited for: 11 -> 22; matrix products, arithmetic and copies ran while one was open for 22% -> 3% of each run, Pallas kernels for 0% -> 22%
where the time goes in v2:
time: 317 us; the launch traced here: 316 us
  waiting for transfers between devices  126 us (40%)
  Pallas kernels  84.2 us (27%)
  starting transfers between devices  70.8 us (22%)
  between operations  14.8 us (5%)
  local copies, waits for them, and re-layouts  11.1 us (4%)
  other arithmetic  8.71 us (3%)
    ppermute x55, waiting for transfers between devices, permute(): return lambda block: lax.ppermute(block, ('ctx', 'fsdp'), pairs)  108 us
    pallas_call x11, Pallas kernels, call(): pl.pallas_call(kernel, out_shape=[jax.ShapeDtypeStruct(shape, kind) for s...  84.2 us
    ppermute x55, starting transfers between devices, permute(): return lambda block: lax.ppermute(block, ('ctx', 'fsdp'), pairs)  60 us
    ppermute x6, waiting for transfers between devices, permute_back(): return lambda block: lax.ppermute(block, ('ctx', 'fsdp'), pairs)  17.1 us
    ppermute x6, starting transfers between devices, permute_back(): return lambda block: lax.ppermute(block, ('ctx', 'fsdp'), pairs)  10.7 us
  transfers between devices with their start and end apart: 62, of which 22 were waited for; matrix products, arithmetic and copies ran while one was open for 3% of the time, Pallas kernels for 22%

profile of v2, /device:TPU:0, one launch (start us, length us, event | category | flops | bytes accessed | tf_op | source)
XLA Modules:
  0.0 315.8 jit_solution(8949369891475628745)
XLA Ops:
  8.0 3.3 %pack.1 = (bf16[128,768]{1,0:T(8,128)(2,1)}, bf16[128,768]{1,0:T(8,128)(2,1)}, bf16[256,768]{1,0:T(8,128)(2,1)}, bf16[192,1152]{1,0:T(8,128)(2,1)}, bf16[16,768]{1,0:T(8,128)(2,1)}) custom-call(s32[1]{0:T(128)} %bitcast.info, s32[2]{0:T(128)} %lens.3, bf16[2,128,768]{2,1,0:T(8,128)(2,1)} %rows.1, bf16[2,128,768]{2,1,0:T(8,128)(2,1)} %grads.1, ...), custom_call_target="tpu_custom_call" | custom-call | flops 1000000000 | bytes 4000000 | tf_op jit(solution)/shard_map/pack/pallas_call | solution.py:915
  11.3 3.0 collective-permute-start.8
  19.5 22.0 %collective-permute-done.2.s2 = bf16[16,768]{1,0:T(8,128)(2,1)S(1)} collective-permute-done((bf16[16,768]{1,0:T(8,128)(2,1)}, bf16[16,768]{1,0:T(8,128)(2,1)S(1)}, u32[]{:S(2)}, u32[]{:S(2)}) %collective-permute-start.2) | collective-permute-done | bytes 24608 | tf_op jit(solution)/shard_map/ppermute | solution.py:523
  43.9 4.7 %collective-permute-done.5.b2 = bf16[128,768]{1,0:T(8,128)(2,1)S(1)} collective-permute-done((bf16[128,768]{1,0:T(8,128)(2,1)S(1)}, bf16[128,768]{1,0:T(8,128)(2,1)S(1)}, u32[]{:S(2)}, u32[]{:S(2)}) %collective-permute-start.5) | collective-permute-done | bytes 196640 | tf_op jit(solution)/shard_map/ppermute | solution.py:523
  59.1 13.6 %attend.1 = (bf16[1024,768]{1,0:T(8,128)(2,1)}, bf16[768,1152]{1,0:T(8,128)(2,1)}, bf16[512,384]{1,0:T(8,128)(2,1)}, bf16[1024,384]{1,0:T(8,128)(2,1)}, bf16[102...) custom-call(s32[1]{0:T(128)} %bitcast.info, ...), custom_call_target="tpu_custom_call" | custom-call | flops 10000000000 | bytes 15000000 | tf_op jit(solution)/shard_map/attend/pallas_call | solution.py:915
  74.3 3.0 collective-permute-start.16
  86.1 4.1 %collective-permute-start.20 = (bf16[128,384]{1,0:T(8,128)(2,1)S(1)}, bf16[128,384]{1,0:T(8,128)(2,1)S(1)}, u32[]{:S(2)}, u32[]{:S(2)}) collective-permute-start(bf16[128,384]{1,0:T(8,128)(2,1)S(1)} %collective-permute-done.18), channel_id=1, source_target_pairs={{8,0},{24,1},{10,2},{26,3},{12,4},{28,5},{14,6},{30,7},{9,8},{25,9... | collective-permute-start | bytes 294920 | tf_op jit(solution)/shard_map/ppermute | solution.py:528
  95.9 7.5 %middle_one.1 = (f32[256,768]{1,0:T(8,128)}, f32[256,768]{1,0:T(8,128)}, f32[256,1]{1,0:T(8,128)}, bf16[4,256,768]{2,1,0:T(8,128)(2,1)}, bf16[4,256,768]{2,1,0:T(8,128)(2,1)}, /*index=5*/f32[8,768]{1,0:T(8,128)}) custom-call(s32[1]{0:T(128)} %bitcast.info, bf16[128,384]{1,0:T(8,128)(2,1)} %copy-done.37, bf16[128,384]{1,0:T(8,128)(2,1)} %copy-done.38, ...), custom_call_target="tpu_custom_call" | custom-call | flops 4000000000 | bytes 10000000 | tf_op jit(solution)/shard_map/middle_one/pallas_call | solution.py:915
  104.5 12.1 %middle_two.1 = (bf16[2,128,768]{2,1,0:T(8,128)(2,1)}, f32[256,768]{1,0:T(8,128)}, bf16[256,768]{1,0:T(8,128)(2,1)}, f32[8,768]{1,0:T(8,128)}, bf16[2,4,192,768]...) custom-call(s32[1]{0:T(128)} %bitcast.info, s32[2]{0:T(128)} %lens.3, ...), custom_call_target="tpu_custom_call" | custom-call | flops 4000000000 | bytes 10000000 | tf_op jit(solution)/shard_map/middle_two/pallas_call | solution.py:915
  116.6 4.7 %collective-permute-done.30 = bf16[2,4,192,768]{3,2,1,0:T(8,128)(2,1)S(1)} collective-permute-done((bf16[2,4,192,768]{3,2,1,0:T(8,128)(2,1)}, bf16[2,4,192,768]{3,2,1,0:T(8,128)(2,1)S(1)}, u32[]{:S(2)}, u32[]{:S(2)}) %collective-permute-start.30) | collective-permute-done | bytes 2359328 | tf_op jit(solution)/shard_map/ppermute | solution.py:523
  124.5 11.2 %middle_three.1 = (f32[256,768]{1,0:T(8,128)}, bf16[128,384]{1,0:T(8,128)(2,1)}, bf16[128,384]{1,0:T(8,128)(2,1)}, bf16[128,384]{1,0:T(8,128)(2,1)}, bf16[128,38...) custom-call(s32[1]{0:T(128)} %bitcast.info, ...), custom_call_target="tpu_custom_call" | custom-call | flops 4000000000 | bytes 14000000 | tf_op jit(solution)/shard_map/middle_three/pallas_call | solution.py:915
  140.7 3.5 %collective-permute-start.29 = (bf16[128,384]{1,0:T(8,128)(2,1)}, bf16[128,384]{1,0:T(8,128)(2,1)S(1)}, u32[]{:S(2)}, u32[]{:S(2)}) collective-permute-start(bf16[128,384]{1,0:T(8,128)(2,1)} %get-tuple-element.207), channel_id=1, source_target_pairs={{0,8},{1,24},{2,10},{3,26},{4,12},{5,28},{6,14},{7,30},{8,9},{9,25... | collective-permute-start | bytes 294920 | tf_op jit(solution)/shard_map/ppermute | solution.py:523
  144.1 6.8 %middle_four.1 = (bf16[2,4,256,768]{3,2,1,0:T(8,128)(2,1)}, bf16[2,4,256,768]{3,2,1,0:T(8,128)(2,1)}) custom-call(s32[1]{0:T(128)} %bitcast.info, bf16[4,256,768]{2,1,0:T(8,128)(2,1)} %get-tuple-element.211.inner, f32[256,768]{1,0:T(8,128)} %get-tuple-element.192.hidden, bf16[256,768]{1,0:T(8,128)(2,1)} %get-tuple-element.212.branch, ...), custom_call_target="tpu_custom_call" | custom-call | flops 4000000000 | bytes 8000000 | tf_op jit(solution)/shard_map/middle_four/pallas_call | solution.py:915
  161.8 9.0 %attend_back.1 = (bf16[512,256]{1,0:T(8,128)(2,1)}, bf16[1024,256]{1,0:T(8,128)(2,1)}, bf16[1024,256]{1,0:T(8,128)(2,1)}) custom-call(bf16[512,384]{1,0:T(8,128)(2,1)} %get-tuple-element.228.queries, bf16[1024,384]{1,0:T(8,128)(2,1)} %get-tuple-element.229.keys, bf16[1024,384]{1,0:T(8,128)(2,1)} %get-tuple-element.230.values, ...), custom_call_target="tpu_custom_call" | custom-call | flops 8000000000 | bytes 10000000 | tf_op jit(solution)/shard_map/attend_back/pallas_call | solution.py:915
  175.6 12.1 %attend_last.1 = (f32[512,768]{1,0:T(8,128)}, bf16[512,768]{1,0:T(8,128)(2,1)}, bf16[2,2,112,1152]{3,2,1,0:T(8,128)(2,1)}, bf16[2,2,112,1152]{3,2,1,0:T(8,128)(2,1)}) custom-call(s32[1]{0:T(128)} %bitcast.info, bf16[1024,768]{1,0:T(8,128)(2,1)} %get-tuple-element.226.xs, bf16[768,1152]{1,0:T(8,128)(2,1)} %get-tuple-element.227.ws, ...), custom_call_target="tpu_custom_call" | custom-call | flops 8000000000 | bytes 10000000 | tf_op jit(solution)/shard_map/attend_last/pallas_call | solution.py:915
  195.7 10.9 %collective-permute-done.44 = bf16[192,768]{1,0:T(8,128)(2,1)S(1)} collective-permute-done((bf16[192,768]{1,0:T(8,128)(2,1)S(1)}, bf16[192,768]{1,0:T(8,128)(2,1)S(1)}, u32[]{:S(2)}, u32[]{:S(2)}) %collective-permute-start.44) | collective-permute-done | bytes 294944 | tf_op jit(solution)/shard_map/ppermute | solution.py:523
  206.6 5.1 %collective-permute-done.40 = bf16[2,256,768]{2,1,0:T(8,128)(2,1)S(1)} collective-permute-done((bf16[2,256,768]{2,1,0:T(8,128)(2,1)S(1)}, bf16[2,256,768]{2,1,0:T(8,128)(2,1)S(1)}, u32[]{:S(2)}, u32[]{:S(2)}) %collective-permute-start.40) | collective-permute-done | bytes 786464 | tf_op jit(solution)/shard_map/ppermute | solution.py:523
  211.7 5.9 %collective-permute-done.43 = bf16[256,768]{1,0:T(8,128)(2,1)S(1)} collective-permute-done((bf16[256,768]{1,0:T(8,128)(2,1)S(1)}, bf16[256,768]{1,0:T(8,128)(2,1)S(1)}, u32[]{:S(2)}, u32[]{:S(2)}) %collective-permute-start.43) | collective-permute-done | bytes 393248 | tf_op jit(solution)/shard_map/ppermute | solution.py:523
  223.5 12.8 %collective-permute-done.47 = bf16[128,768]{1,0:T(8,128)(2,1)S(1)} collective-permute-done((bf16[128,768]{1,0:T(8,128)(2,1)S(1)}, bf16[128,768]{1,0:T(8,128)(2,1)S(1)}, u32[]{:S(2)}, u32[]{:S(2)}) %collective-permute-start.47) | collective-permute-done | bytes 196640 | tf_op jit(solution)/shard_map/ppermute | solution.py:528
  241.7 13.0 %collective-permute-done.52.p2 = bf16[192,768]{1,0:T(8,128)(2,1)} collective-permute-done((bf16[192,768]{1,0:T(8,128)(2,1)S(1)}, bf16[192,768]{1,0:T(8,128)(2,1)}, u32[]{:S(2)}, u32[]{:S(2)}) %collective-permute-start.52) | collective-permute-done | bytes 294944 | tf_op jit(solution)/shard_map/ppermute | solution.py:523
  254.8 10.1 %collective-permute-done.50 = bf16[112,1152]{1,0:T(8,128)(2,1)S(1)} collective-permute-done((bf16[112,1152]{1,0:T(8,128)(2,1)S(1)}, bf16[112,1152]{1,0:T(8,128)(2,1)S(1)}, u32[]{:S(2)}, u32[]{:S(2)}) %collective-permute-start.50) | collective-permute-done | bytes 258080 | tf_op jit(solution)/shard_map/ppermute | solution.py:523
  269.6 9.8 %collective-permute-done.54 = bf16[112,1152]{1,0:T(8,128)(2,1)S(1)} collective-permute-done((bf16[112,1152]{1,0:T(8,128)(2,1)S(1)}, bf16[112,1152]{1,0:T(8,128)(2,1)S(1)}, u32[]{:S(2)}, u32[]{:S(2)}) %collective-permute-start.54) | collective-permute-done | bytes 258080 | tf_op jit(solution)/shard_map/ppermute | solution.py:523
  288.6 7.9 %collective-permute-done.58.p2 = bf16[112,1152]{1,0:T(8,128)(2,1)S(1)} collective-permute-done((bf16[112,1152]{1,0:T(8,128)(2,1)S(1)}, bf16[112,1152]{1,0:T(8,128)(2,1)S(1)}, u32[]{:S(2)}, u32[]{:S(2)}) %collective-permute-start.58) | collective-permute-done | bytes 258080 | tf_op jit(solution)/shard_map/ppermute | solution.py:523
  297.2 3.2 %place_inner.1 = (f32[192,3072]{1,0:T(8,128)}, f32[192,768]{1,0:T(8,128)}, f32[4,16,768]{2,1,0:T(8,128)}) custom-call(s32[1]{0:T(128)} %bitcast.info, bf16[256,768]{1,0:T(8,128)(2,1)} %copy-done.6, bf16[256,768]{1,0:T(8,128)(2,1)} %copy-done.20, bf16[256,768]{1,0:T(8,128)(2,1)} %copy-done.19, bf16[256,768]{1,0:T(8,128)(2,1)} %copy-done.21), custom_call_target="tpu_custom_call" | custom-call | flops 1000000000 | bytes 6000000 | tf_op jit(solution)/shard_map/place_inner/pallas_call | solution.py:915
  (243 shorter events, 101.8 us)
Async XLA Ops:
  7.2 88.7 %all-gather.2.cloned.1.call-start = ((), (), s32[]{:S(2)}) async-start(), calls=%async_computation | async-start | bytes 5898240 | tf_op jit(solution)/shard_map/all_gather | solution.py:1133
  11.3 32.3 %collective-permute-start.8 = (bf16[192,768]{1,0:T(8,128)(2,1)S(1)}, bf16[192,768]{1,0:T(8,128)(2,1)S(1)}, u32[]{:S(2)}, u32[]{:S(2)}) collective-permute-start(bf16[192,768]{1,0:T(8,128)(2,1)S(1)} %copy-done.22), channel_id=1, source_target_pairs={{0,2},{1,3},{2,0},{3,1},{4,6},{5,7},{6,4},{7,5},{8,10},{9,11},{10,... | collective-permute-start | bytes 884744 | tf_op jit(solution)/shard_map/ppermute | solution.py:523
  14.3 37.2 %collective-permute-start.7 = (bf16[192,1152]{1,0:T(8,128)(2,1)}, bf16[192,1152]{1,0:T(8,128)(2,1)S(1)}, u32[]{:S(2)}, u32[]{:S(2)}) collective-permute-start(bf16[192,1152]{1,0:T(8,128)(2,1)} %get-tuple-element.167.w0), channel_id=1, source_target_pairs={{0,2},{1,3},{2,0},{3,1},{4,6},{5,7},{6,4},{7,5},{8,10},{9,11},{10,... | collective-permute-start | bytes 1327112 | tf_op jit(solution)/shard_map/ppermute | solution.py:523
  14.4 27.1 %collective-permute-start.1 = (bf16[128,768]{1,0:T(8,128)(2,1)}, bf16[128,768]{1,0:T(8,128)(2,1)S(1)}, u32[]{:S(2)}, u32[]{:S(2)}) collective-permute-start(bf16[128,768]{1,0:T(8,128)(2,1)} %get-tuple-element.156.x1), channel_id=1, source_target_pairs={{0,8},{1,24},{2,10},{3,26},{4,12},{5,28},{6,14},{7,30},{8,9},{9,25... | collective-permute-start | bytes 589832 | tf_op jit(solution)/shard_map/ppermute | solution.py:523
  16.4 25.1 %collective-permute-start = (bf16[128,768]{1,0:T(8,128)(2,1)}, bf16[128,768]{1,0:T(8,128)(2,1)S(1)}, u32[]{:S(2)}, u32[]{:S(2)}) collective-permute-start(bf16[128,768]{1,0:T(8,128)(2,1)} %get-tuple-element.155.x0), channel_id=1, source_target_pairs={{0,0},{1,16},{2,2},{3,18},{4,4},{5,20},{6,6},{7,22},{8,1},{9,17},{... | collective-permute-start | bytes 589832 | tf_op jit(solution)/shard_map/ppermute | solution.py:523
  18.0 23.5 %collective-permute-start.2 = (bf16[16,768]{1,0:T(8,128)(2,1)}, bf16[16,768]{1,0:T(8,128)(2,1)S(1)}, u32[]{:S(2)}, u32[]{:S(2)}) collective-permute-start(bf16[16,768]{1,0:T(8,128)(2,1)} %get-tuple-element.173.s0), channel_id=1, source_target_pairs={{0,2},{1,3},{2,0},{3,1},{4,6},{5,7},{6,4},{7,5},{8,10},{9,11},{10,... | collective-permute-start | bytes 73736 | tf_op jit(solution)/shard_map/ppermute | solution.py:523
  55.2 37.4 %collective-permute-start.23 = (bf16[768,768]{1,0:T(8,128)(2,1)S(1)}, bf16[768,768]{1,0:T(8,128)(2,1)S(1)}, u32[]{:S(2)}, u32[]{:S(2)}) collective-permute-start(bf16[768,768]{1,0:T(8,128)(2,1)S(1)} %copy-done.13), channel_id=1, source_target_pairs={{0,2},{1,3},{2,0},{3,1},{4,6},{5,7},{6,4},{7,5},{8,10},{9,11},{10,... | collective-permute-start | bytes 3538952 | tf_op jit(solution)/shard_map/ppermute | solution.py:523
  123.5 27.4 %collective-permute-start.31 = (bf16[2,192,768]{2,1,0:T(8,128)(2,1)S(1)}, bf16[2,192,768]{2,1,0:T(8,128)(2,1)S(1)}, u32[]{:S(2)}, u32[]{:S(2)}) collective-permute-start(bf16[2,192,768]{2,1,0:T(8,128)(2,1)S(1)} %slice_bitcast_fusion.2), channel_id=1, source_target_pairs={{0,2},{1,3},{2,0},{3,1},{4,6},{5,7},{6,4},{7,5},{8,10},{9,11},{10,... | collective-permute-start | bytes 1769480 | tf_op jit(solution)/shard_map/ppermute | solution.py:523
  135.7 15.2 %collective-permute-start.26 = (bf16[128,384]{1,0:T(8,128)(2,1)}, bf16[128,384]{1,0:T(8,128)(2,1)S(1)}, u32[]{:S(2)}, u32[]{:S(2)}) collective-permute-start(bf16[128,384]{1,0:T(8,128)(2,1)} %get-tuple-element.204), channel_id=1, source_target_pairs={{0,0},{1,16},{2,2},{3,18},{4,4},{5,20},{6,6},{7,22},{8,1},{9,17},{... | collective-permute-start | bytes 294920 | tf_op jit(solution)/shard_map/ppermute | solution.py:523
  155.3 15.5 %collective-permute-start.36 = (bf16[2,192,768]{2,1,0:T(8,128)(2,1)}, bf16[2,192,768]{2,1,0:T(8,128)(2,1)S(1)}, u32[]{:S(2)}, u32[]{:S(2)}) collective-permute-start(bf16[2,192,768]{2,1,0:T(8,128)(2,1)} %add_convert_fusion.3), channel_id=1, source_target_pairs={{0,8},{1,9},{2,10},{3,11},{4,12},{5,13},{6,14},{7,15},{8,0},{9,1},... | collective-permute-start | bytes 1769480 | tf_op jit(solution)/shard_map/ppermute | solution.py:523
  155.3 16.5 %collective-permute-start.35 = (bf16[2,192,768]{2,1,0:T(8,128)(2,1)}, bf16[2,192,768]{2,1,0:T(8,128)(2,1)S(1)}, u32[]{:S(2)}, u32[]{:S(2)}) collective-permute-start(bf16[2,192,768]{2,1,0:T(8,128)(2,1)} %slice.141), channel_id=1, source_target_pairs={{0,2},{1,3},{2,0},{3,1},{4,6},{5,7},{6,4},{7,5},{8,10},{9,11},{10,... | collective-permute-start | bytes 1769480 | tf_op jit(solution)/shard_map/ppermute | solution.py:523
  160.6 27.1 %collective-permute-start.38 = (bf16[2,256,768]{2,1,0:T(8,128)(2,1)S(1)}, bf16[2,256,768]{2,1,0:T(8,128)(2,1)}, u32[]{:S(2)}, u32[]{:S(2)}) collective-permute-start(bf16[2,256,768]{2,1,0:T(8,128)(2,1)S(1)} %get-tuple-element.255), channel_id=1, source_target_pairs={{0,2},{1,3},{2,0},{3,1},{4,6},{5,7},{6,4},{7,5},{8,10},{9,11},{10,... | collective-permute-start | bytes 2359304 | tf_op jit(solution)/shard_map/ppermute | solution.py:523
  189.6 22.1 %collective-permute-start.39 = (bf16[2,256,768]{2,1,0:T(8,128)(2,1)S(1)}, bf16[2,256,768]{2,1,0:T(8,128)(2,1)S(1)}, u32[]{:S(2)}, u32[]{:S(2)}) collective-permute-start(bf16[2,256,768]{2,1,0:T(8,128)(2,1)S(1)} %convert_add_fusion.2), channel_id=1, source_target_pairs={{0,4},{1,5},{2,6},{3,7},{4,0},{5,1},{6,2},{7,3},{8,12},{9,13},{10,... | collective-permute-start | bytes 2359304 | tf_op jit(solution)/shard_map/ppermute | solution.py:523
  190.7 15.9 %collective-permute-start.44 = (bf16[192,768]{1,0:T(8,128)(2,1)S(1)}, bf16[192,768]{1,0:T(8,128)(2,1)S(1)}, u32[]{:S(2)}, u32[]{:S(2)}) collective-permute-start(bf16[192,768]{1,0:T(8,128)(2,1)S(1)} %fusion.6), channel_id=1, source_target_pairs={{0,16},{1,17},{2,18},{3,19},{4,20},{5,21},{6,22},{7,23},{8,24},{9,... | collective-permute-start | bytes 884744 | tf_op jit(solution)/shard_map/ppermute | solution.py:523
  192.8 18.9 %collective-permute-start.40 = (bf16[2,256,768]{2,1,0:T(8,128)(2,1)S(1)}, bf16[2,256,768]{2,1,0:T(8,128)(2,1)S(1)}, u32[]{:S(2)}, u32[]{:S(2)}) collective-permute-start(bf16[2,256,768]{2,1,0:T(8,128)(2,1)S(1)} %get-tuple-element.258), channel_id=1, source_target_pairs={{0,2},{1,3},{2,0},{3,1},{4,6},{5,7},{6,4},{7,5},{8,10},{9,11},{10,... | collective-permute-start | bytes 2359304 | tf_op jit(solution)/shard_map/ppermute | solution.py:523
  194.2 23.5 %collective-permute-start.43 = (bf16[256,768]{1,0:T(8,128)(2,1)S(1)}, bf16[256,768]{1,0:T(8,128)(2,1)S(1)}, u32[]{:S(2)}, u32[]{:S(2)}) collective-permute-start(bf16[256,768]{1,0:T(8,128)(2,1)S(1)} %slice.231), channel_id=1, source_target_pairs={{0,4},{1,5},{2,6},{3,7},{4,0},{5,1},{6,2},{7,3},{8,12},{9,13},{10,... | collective-permute-start | bytes 1179656 | tf_op jit(solution)/shard_map/ppermute | solution.py:523
  217.8 18.5 %collective-permute-start.49 = (bf16[192,768]{1,0:T(8,128)(2,1)S(1)}, bf16[192,768]{1,0:T(8,128)(2,1)}, u32[]{:S(2)}, u32[]{:S(2)}) collective-permute-start(bf16[192,768]{1,0:T(8,128)(2,1)S(1)} %add_convert_fusion.6.p0), channel_id=1, source_target_pairs={{0,4},{1,5},{2,6},{3,7},{4,0},{5,1},{6,2},{7,3},{8,12},{9,13},{10,... | collective-permute-start | bytes 884744 | tf_op jit(solution)/shard_map/ppermute | solution.py:523
  219.0 17.3 %collective-permute-start.48 = (bf16[2,112,1152]{2,1,0:T(8,128)(2,1)S(1)}, bf16[2,112,1152]{2,1,0:T(8,128)(2,1)S(1)}, u32[]{:S(2)}, u32[]{:S(2)}) collective-permute-start(bf16[2,112,1152]{2,1,0:T(8,128)(2,1)S(1)} %fusion.7), channel_id=1, source_target_pairs={{0,2},{1,3},{2,0},{3,1},{4,6},{5,7},{6,4},{7,5},{8,10},{9,11},{10,... | collective-permute-start | bytes 1548296 | tf_op jit(solution)/shard_map/ppermute | solution.py:523
  220.3 16.0 %collective-permute-start.45 = (bf16[256,768]{1,0:T(8,128)(2,1)S(1)}, bf16[256,768]{1,0:T(8,128)(2,1)S(1)}, u32[]{:S(2)}, u32[]{:S(2)}) collective-permute-start(bf16[256,768]{1,0:T(8,128)(2,1)S(1)} %fusion.10), channel_id=1, source_target_pairs={{0,8},{1,9},{2,10},{3,11},{4,12},{5,13},{6,14},{7,15},{8,0},{9,1},... | collective-permute-start | bytes 1179656 | tf_op jit(solution)/shard_map/ppermute | solution.py:523
  236.3 18.5 %collective-permute-start.52 = (bf16[192,768]{1,0:T(8,128)(2,1)S(1)}, bf16[192,768]{1,0:T(8,128)(2,1)}, u32[]{:S(2)}, u32[]{:S(2)}) collective-permute-start(bf16[192,768]{1,0:T(8,128)(2,1)S(1)} %add_convert_fusion.6.p0), channel_id=1, source_target_pairs={{0,8},{1,9},{2,10},{3,11},{4,12},{5,13},{6,14},{7,15},{8,0},{9,1},... | collective-permute-start | bytes 884744 | tf_op jit(solution)/shard_map/ppermute | solution.py:523
  237.0 27.8 %collective-permute-start.53 = (bf16[192,768]{1,0:T(8,128)(2,1)}, bf16[192,768]{1,0:T(8,128)(2,1)}, u32[]{:S(2)}, u32[]{:S(2)}) collective-permute-start(bf16[192,768]{1,0:T(8,128)(2,1)} %collective-permute-done.49.p1), channel_id=1, source_target_pairs={{0,8},{1,9},{2,10},{3,11},{4,12},{5,13},{6,14},{7,15},{8,0},{9,1},... | collective-permute-start | bytes 884744 | tf_op jit(solution)/shard_map/ppermute | solution.py:523
  239.0 25.8 %collective-permute-start.51 = (bf16[256,768]{1,0:T(8,128)(2,1)S(1)}, bf16[256,768]{1,0:T(8,128)(2,1)S(1)}, u32[]{:S(2)}, u32[]{:S(2)}) collective-permute-start(bf16[256,768]{1,0:T(8,128)(2,1)S(1)} %fusion.3), channel_id=1, source_target_pairs={{0,16},{1,17},{2,18},{3,19},{4,20},{5,21},{6,22},{7,23},{8,24},{9,... | collective-permute-start | bytes 1179656 | tf_op jit(solution)/shard_map/ppermute | solution.py:523
  241.6 23.2 %collective-permute-start.50 = (bf16[112,1152]{1,0:T(8,128)(2,1)S(1)}, bf16[112,1152]{1,0:T(8,128)(2,1)S(1)}, u32[]{:S(2)}, u32[]{:S(2)}) collective-permute-start(bf16[112,1152]{1,0:T(8,128)(2,1)S(1)} %fusion.12), channel_id=1, source_target_pairs={{0,8},{1,9},{2,10},{3,11},{4,12},{5,13},{6,14},{7,15},{8,0},{9,1},... | collective-permute-start | bytes 774152 | tf_op jit(solution)/shard_map/ppermute | solution.py:523
  281.2 15.2 %collective-permute-start.59 = (bf16[256,768]{1,0:T(8,128)(2,1)S(1)}, bf16[256,768]{1,0:T(8,128)(2,1)S(1)}, u32[]{:S(2)}, u32[]{:S(2)}) collective-permute-start(bf16[256,768]{1,0:T(8,128)(2,1)S(1)} %collective-permute-done.55.p1), channel_id=1, source_target_pairs={{0,4},{1,5},{2,6},{3,7},{4,0},{5,1},{6,2},{7,3},{8,12},{9,13},{10,... | collective-permute-start | bytes 1179656 | tf_op jit(solution)/shard_map/ppermute | solution.py:523
  (86 other events, 726.1 us)
Sparse Core Ops, SparseCore 0:
  9.6 48.6 all-gather.1

commit v3 on v2

--- a/solution.py
+++ b/solution.py
@@ -567,8 +567,8 @@
 
 
 def pack_kernel(
-    info, lens, rows, grads, w_q, w_k, w_v, v0, v1, v2, v3, v4, v5, v6, v7, wide_vec,
-    t0, t1, cot, w_x, small, held,
+    info, lens, rows, grads, w_q, w_k, w_v, w_o, v0, v1, v2, v3, v4, v5, v6, v7, wide_vec,
+    t0, t1, cot, first, held,
 ):
     z, x, _, _, _, _ = coords(info)
     zh = z >> 1
@@ -577,8 +577,9 @@
     cot[:ROWS] = grads[zh]
     cot[ROWS:] = grads[1 - zh]
     columns = pl.ds(pl.multiple_of(x * HALF, 128), HALF)
+    first[:192, :D] = w_o[...]
     for n, weight in enumerate((w_q, w_k, w_v)):
-        w_x[:, HALF * n : HALF * n + HALF] = weight[:, columns]
+        first[:192, D + HALF * n : D + HALF * n + HALF] = weight[:, columns]
     held[...] = jnp.zeros_like(held)
     for n, vector in enumerate((v0, v1, v2, v3, v4, v5, v6, v7)):
         held[n : n + 1, :192] = wide(vector[...]).reshape(1, 192)
@@ -589,18 +590,27 @@
         ends = jnp.where(lane == n, lens[n] >> 7, ends)
         ends = jnp.where(lane == 2 + n, lens[n] & 127, ends)
     held[9:10, :] = wide(ends)
-    small[...] = low(held[...])
+    first[192:, :D] = low(held[...])
+    first[192:, D:] = jnp.zeros((16, 3 * HALF), jnp.bfloat16)
 
 
 def attend_kernel(
-    info, b0, b1, b2, b3, b4, b5, b6, b7, w0, w1, w2, w3, s0, s1, s2, s3,
-    xs, ws, q_out, k_out, v_out, p_out, cu, cv, cxu, cxv, key_bias, small,
+    info, b0, b1, b2, b3, b4, b5, b6, b7, s0, s1, s2, s3, w0, w1, w2, w3,
+    xs, ws, q_out, k_out, v_out, p_out, cu, cv, cx, key_bias, small, sems,
 ):
     step = pl.program_id(0)
     z, x, y, k, _, f = coords(info)
 
     @pl.when(step == 0)
     def _():
+        copies = [
+            pltpu.make_async_copy(
+                piece.at[:192, D:], ws.at[pl.ds(pl.multiple_of(192 * (f ^ n), 64), 192), :], sems.at[n]
+            )
+            for n, piece in enumerate((w0, w1, w2, w3))
+        ]
+        for copy in copies:
+            copy.start()
         for n, piece in enumerate((s0, s1, s2, s3)):
             small[f ^ n] = wide(piece[...])
         line = small[2 * y + (z >> 1)][9:10, :]
@@ -616,8 +626,8 @@
             xs[n * ROWS : (n + 1) * ROWS, :] = block[...]
             place = (2 * z_block + x_block) * ROWS + lax.broadcasted_iota(jnp.int32, (1, ROWS), 1)
             key_bias[:, n * ROWS : (n + 1) * ROWS] = jnp.where(wide(place) < end, 0.0, NEG_FILL)
-        for n, piece in enumerate((w0, w1, w2, w3)):
-            ws[pl.ds(pl.multiple_of(192 * (f ^ n), 64), 192), :] = piece[...]
+        for copy in copies:
+            copy.wait()
 
         def bias(row):
             return jnp.concatenate(
@@ -646,9 +656,12 @@
             p_out[head, rows, :] = probs
             found.append(matmul(probs, values))
         context = low(jnp.where(first, found[0], found[1]))
-        one, two = (cu, cv) if part == 0 else (cxu, cxv)
-        one[...] = context[:ROWS]
-        two[...] = context[ROWS:]
+        if part == 0:
+            cu[...] = context[:ROWS]
+            cv[...] = context[ROWS:]
+        else:
+            cx[0] = context[:ROWS]
+            cx[1] = context[ROWS:]
 
 
 def pair_back(queries_ref, keys, values, probs_ref, grads):
@@ -684,30 +697,22 @@
     dq[:256, :], dq[256:, :] = grad_qs
 
 
-def attend_last_kernel(
-    info, xs, ws, queries, keys, values, probs, gu, gv, gxu, gxv, dq_in, dk_in, dv_in,
-    dx_own, dx_other, keep, send, dq, dk, dv, dw,
+def joint_kernel(
+    info, xs, dq0, dq1, dq2, dk0, dk1, dk2, dv0, dv1, dv2, keep, send, grads, dw
 ):
-    cut = 2 * 128
-    grad_qs, grad_k, grad_v = pair_back(
-        queries, keys[...], values[...], probs, (gu, gv, gxu, gxv)
-    )
-    dq[:, :cut], dk[:, :cut], dv[:, :cut] = dq_in[...], dk_in[...], dv_in[...]
-    dq[:256, cut:], dq[256:, cut:] = grad_qs
-    dk[:, cut:], dv[:, cut:] = grad_k, grad_v
+    for n, (q, k, v) in enumerate(((dq0, dk0, dv0), (dq1, dk1, dv1), (dq2, dk2, dv2))):
+        start = 128 * n
+        grads[: 4 * ROWS, start : start + 128] = q[...]
+        grads[:, HALF + start : HALF + start + 128] = k[...]
+        grads[:, 2 * HALF + start : 2 * HALF + start + 128] = v[...]
     own = slice(0, 4 * ROWS)
-    other = slice(4 * ROWS, 8 * ROWS)
-    w_q, w_k, w_v = ws[:, :HALF], ws[:, HALF : 2 * HALF], ws[:, 2 * HALF :]
-    dx_other[...] = low(dot_nt(dk[other, :], w_k) + dot_nt(dv[other, :], w_v))
-    dx_own[...] = dot_nt(dq[...], w_q) + dot_nt(dk[own, :], w_k) + dot_nt(dv[own, :], w_v)
-    dw[:, :HALF] = low(dot_tn(xs[own, :], dq[...]))
-    dw[:, HALF : 2 * HALF] = low(dot_tn(xs[...], dk[...]))
-    dw[:, 2 * HALF :] = low(dot_tn(xs[...], dv[...]))
+    dw[:, :HALF] = low(dot_tn(xs[own, :], grads[own, :HALF]))
+    dw[:, HALF:] = low(dot_tn(xs[...], grads[:, HALF:]))
     col_sums = jnp.concatenate(
         [
-            jnp.sum(wide(dq[...]), axis=0, keepdims=True),
+            column_sum(wide(grads[own, :HALF])),
             jnp.zeros((1, HALF), jnp.float32),
-            jnp.sum(wide(dv[...]), axis=0, keepdims=True),
+            column_sum(wide(grads[:, 2 * HALF :])),
         ],
         axis=1,
     )
@@ -721,18 +726,41 @@
             place[n // 2, half ^ (z & 1), 96:, :] = tail if half == 0 else tail * 0
 
 
+def rows_back_kernel(
+    ws, dq0, dq1, dq2, dk0, dk1, dk2, dv0, dv1, dv2, dx_own, dx_other, grads
+):
+    for n, (q, k, v) in enumerate(((dq0, dk0, dv0), (dq1, dk1, dv1), (dq2, dk2, dv2))):
+        start = 128 * n
+        grads[: 4 * ROWS, start : start + 128] = q[...]
+        grads[:, HALF + start : HALF + start + 128] = k[...]
+        grads[:, 2 * HALF + start : 2 * HALF + start + 128] = v[...]
+    dx_other[...] = low(dot_nt(grads[4 * ROWS :, HALF:], ws[:, HALF:]))
+    dx_own[...] = dot_nt(grads[: 4 * ROWS, :], ws[...])
+
+
 def middle_one_kernel(
-    info, cm0, cm1, co0, co1, x0, x1, o0, o1, o2, o3, inner_weight, s0, s1, s2, s3,
-    hidden_out, normed_out, inv_out, act, slope, vec, ctx, low_rows, small, order,
+    info, cm0, cm1, co0, co1, x0, x1, o0, o1, o2, o3, i0, i1, i2, i3,
+    hidden_out, normed_out, inv_out, act, slope, vec,
+    ctx, low_rows, small, order, inner_weight, sems,
 ):
     step = pl.program_id(0)
     _, x, _, _, _, f = coords(info)
 
+    def copy(e, n):
+        return pltpu.make_async_copy(
+            (i0, i1, i2, i3)[n].at[:, pl.ds(pl.multiple_of(D * (f ^ e), 128), D)],
+            inner_weight.at[e, pl.ds(pl.multiple_of(192 * (f ^ n), 64), 192), :],
+            sems.at[e, n],
+        )
+
     @pl.when(step == 0)
     def _():
-        for n, piece in enumerate((s0, s1, s2, s3)):
-            small[f ^ n] = wide(piece[...])
-            order[n] = wide(piece[...])
+        for e in range(4):
+            for n in range(4):
+                copy(e, n).start()
+        for n, piece in enumerate((o0, o1, o2, o3)):
+            small[f ^ n] = wide(piece[192:, :])
+            order[n] = wide(piece[192:, :])
         for n in range(8):
             vec[n : n + 1, :] = jnp.concatenate(
                 [small[m][n : n + 1, :192] for m in range(4)], axis=1
@@ -743,14 +771,16 @@
                 ctx[2 * (x ^ side) + part] = rows[:, 192 * part : 192 * part + 192]
         total = wide(jnp.concatenate([x0[...], x1[...]], axis=0)) + vec[2:3, :]
         for n, piece in enumerate((o0, o1, o2, o3)):
-            total = total + matmul(ctx[f ^ n], piece[...])
+            total = total + matmul(ctx[f ^ n], piece[:192, :])
         hidden, normed, inv = layer_norm(total, vec[3:4, :], vec[4:5, :])
         hidden_out[...] = hidden
         normed_out[...] = normed
         inv_out[...] = inv
         low_rows[...] = low(hidden)
 
-    pre = matmul(low_rows[...], inner_weight[...]) + order[step][8:9, :]
+    for n in range(4):
+        copy(step, n).wait()
+    pre = matmul(low_rows[...], inner_weight[step]) + order[step][8:9, :]
     bell = 0.5 * (1.0 + lax.erf(pre * ROOT_HALF))
     act[0] = low(pre * bell)
     slope[0] = low(bell + pre * INV_ROOT_TAU * jnp.exp(-0.5 * pre * pre))
@@ -769,8 +799,24 @@
     return jnp.sum(value, axis=0, keepdims=True)
 
 
+def outer_copies(refs, held, sems):
+    w0, w1, y0, y1, ky0, ky1 = refs
+    half = D // 2
+    plan = [
+        [(w0, held.at[0], 0)],
+        [(w1, held.at[1], 1)],
+        [(y0, held.at[2, :half], 2), (y1, held.at[2, half:], 3)],
+        [(ky0, held.at[3, :half], 4), (ky1, held.at[3, half:], 5)],
+    ]
+    copies = [[pltpu.make_async_copy(a, b, sems.at[n]) for a, b, n in block] for block in plan]
+    for block in copies:
+        for copy in block:
+            copy.start()
+    return copies
+
+
 def middle_two_kernel(
-    info, lens, act, act_block, hidden, cot, vec, w0, w1, w2, w3,
+    info, lens, act, act_block, hidden, cot, vec, w0, w1, w2, w3, w4, w5,
     out, second_out, outer_out, sums, keep, send, w_all, w_sem,
 ):
     step = pl.program_id(0)
@@ -778,16 +824,12 @@
 
     @pl.when(step == 0)
     def _():
-        copies = [
-            pltpu.make_async_copy(ref, w_all.at[n], w_sem.at[n])
-            for n, ref in enumerate((w0, w1, w2, w3))
-        ]
-        for copy in copies:
-            copy.start()
+        copies = outer_copies((w0, w1, w2, w3, w4, w5), w_all, w_sem)
         b_2, g_2, s_2 = vec[5:6, :], vec[6:7, :], vec[7:8, :]
         total = hidden[...] + b_2
         for n in range(4):
-            copies[n].wait()
+            for copy in copies[n]:
+                copy.wait()
             total = total + matmul(act[n], w_all[n])
         result, normed, inv = layer_norm(total, g_2, s_2)
         zh = z >> 1
@@ -815,34 +857,41 @@
                     place[0, n ^ (2 * (z & 1) + x)] = grad[192 * n : 192 * n + 192]
 
 
+def inner_back_kernel(
+    info, outer, slope, w0, w1, w2, w3, w4, w5, inner_out, sums, w_all, sems
+):
+    f = info[0] & 3
+    copies = outer_copies((w0, w1, w2, w3, w4, w5), w_all, sems)
+    for e in range(4):
+        for copy in copies[e]:
+            copy.wait()
+        inner = low(dot_nt(outer[...], w_all[e]) * wide(slope[e]))
+        inner_out[e] = inner
+        sums[pl.ds(f ^ e, 1), :] = column_sum(wide(inner))
+
+
 def middle_three_kernel(
-    info, outer, second, slope, normed_one, inv_one, vec, inner_weight,
-    o0, o1, o2, o3, w0, w1, w2, w3,
-    first_out, gm0, gm1, go0, go1, inner_out, branch_out, sums,
-    o_all, i_all, w_all, gc, o_sem, i_sem, w_sem,
+    info, second, inner, normed_one, inv_one, vec, o0, o1, o2, o3, i0, i1, i2, i3,
+    first_out, gm0, gm1, go0, go1, branch_out, sums, o_all, i_all, gc, o_sem, i_sem,
 ):
     _, x, _, _, _, f = coords(info)
     copies = {}
     for e in range(4):
         columns = pl.ds(pl.multiple_of(D * (f ^ e), 128), D)
-        copies["w", e] = pltpu.make_async_copy((w0, w1, w2, w3)[e], w_all.at[e], w_sem.at[e])
-        copies["i", e] = pltpu.make_async_copy(
-            inner_weight.at[:, columns], i_all.at[e], i_sem.at[e]
-        )
-        copies["w", e].start()
-        copies["i", e].start()
+        for n, ref in enumerate((i0, i1, i2, i3)):
+            rows = pl.ds(pl.multiple_of(192 * (f ^ n), 64), 192)
+            copies["i", e, n] = pltpu.make_async_copy(
+                ref.at[:, columns], i_all.at[e, rows, :], i_sem.at[e, n]
+            )
+            copies["i", e, n].start()
     for n, ref in enumerate((o0, o1, o2, o3)):
-        copies["o", n] = pltpu.make_async_copy(ref, o_all.at[n], o_sem.at[n])
+        copies["o", n] = pltpu.make_async_copy(ref.at[:192, :D], o_all.at[n], o_sem.at[n])
         copies["o", n].start()
-    sums[...] = jnp.zeros_like(sums)
     grad_hidden = second[...]
     for e in range(4):
-        copies["w", e].wait()
-        inner = low(dot_nt(outer[...], w_all[e]) * wide(slope[e]))
-        inner_out[e] = inner
-        sums[pl.ds(8 + (f ^ e), 1), :] = column_sum(wide(inner))
-        copies["i", e].wait()
-        grad_hidden = grad_hidden + dot_nt(inner, i_all[e])
+        for n in range(4):
+            copies["i", e, n].wait()
+        grad_hidden = grad_hidden + dot_nt(inner[e], i_all[e])
     grad_first = norm_grad(grad_hidden, normed_one[...], inv_one[...], vec[3:4, :])
     first_out[...] = grad_first
     branch = low(grad_first)
@@ -859,7 +908,7 @@
 
 
 def middle_four_kernel(
-    info, inner, hidden, branch, cm0, cm1, co0, co1, sums_one, sums_two,
+    info, inner, hidden, branch, cm0, cm1, co0, co1, sums_two, sums_in, sums_one,
     keep, send, held, out_held, vec_held,
 ):
     step = pl.program_id(0)
@@ -877,12 +926,12 @@
         for n in range(4):
             cut = slice(192 * n, 192 * n + 192)
             lines = (
-                sums_two[8 + n : 9 + n, :],
+                sums_in[n : n + 1, :],
                 jnp.concatenate(
-                    [sums_two[m : m + 1, cut] for m in range(3)] + [sums_one[0:1, cut]], axis=1
+                    [sums_one[m : m + 1, cut] for m in range(3)] + [sums_two[0:1, cut]], axis=1
                 ),
                 jnp.concatenate(
-                    [sums_one[1:2, cut], sums_one[2:3, cut], jnp.zeros((1, HALF), jnp.float32)],
+                    [sums_two[1:2, cut], sums_two[2:3, cut], jnp.zeros((1, HALF), jnp.float32)],
                     axis=1,
                 ),
             )
@@ -926,7 +975,7 @@
             dimension_semantics=("arbitrary",), vmem_limit_bytes=VMEM_LIMIT
         ),
         cost_estimate=pl.CostEstimate(
-            flops=work[0] * 1_000_000_000, bytes_accessed=work[1] * 1_000_000, transcendentals=0
+            flops=1000, bytes_accessed=1000, transcendentals=0
         ),
         name=name,
     )(*scalars, *[array for array, _ in operands])
@@ -949,76 +998,88 @@
         pack_kernel, "pack", 1, (info, lens), plain([inputs, cotangent, *weights, *vectors]),
         [
             ((ROWS, D), BF, None), ((ROWS, D), BF, None), ((MIDDLE, D), BF, None),
-            ((192, 3 * HALF), BF, None), ((16, D), BF, None),
+            ((208, D + 3 * HALF), BF, None),
         ],
         [pltpu.VMEM((16, D), FP)], (1, 4),
     )
 
 
-def attend(info, blocks, pieces, small):
+def first_columns(pieces):
+    return [(piece, pl.BlockSpec((208, D), lambda *_: (0, 0))) for piece in pieces]
+
+
+def attend(info, blocks, pieces):
     return call(
-        attend_kernel, "attend", 3, (info,), plain([*blocks, *pieces, *small]),
+        attend_kernel, "attend", 3, (info,),
+        plain(blocks)
+        + [(piece, pl.BlockSpec((16, D), lambda *_: (12, 0))) for piece in pieces]
+        + anywhere(pieces),
         [
             ((8 * ROWS, D), BF, None), ((D, 3 * HALF), BF, None), ((4 * ROWS, HALF), BF, None),
             ((8 * ROWS, HALF), BF, None), ((8 * ROWS, HALF), BF, None),
             ((6, 4 * ROWS, 8 * ROWS), BF, probs_block()),
         ]
-        + [((ROWS, HALF), BF, lane_block(ROWS))] * 4,
-        [pltpu.VMEM((1, 8 * ROWS), FP), pltpu.VMEM((4, 16, D), FP)], (10, 15),
-    )
-
-
-def attend_back(queries, keys, values, probs, grads):
+        + [((ROWS, HALF), BF, lane_block(ROWS))] * 2
+        + [((2, ROWS, HALF), BF, pl.BlockSpec((2, ROWS, 128), lambda step, *_: (0, 0, step)))],
+        [
+            pltpu.VMEM((1, 8 * ROWS), FP), pltpu.VMEM((4, 16, D), FP),
+            pltpu.SemaphoreType.DMA((4,)),
+        ],
+        (10, 15),
+    )
+
+
+def attend_back(queries, keys, values, probs, grads, start, pairs):
     return call(
-        attend_back_kernel, "attend_back", 2, (),
+        attend_back_kernel, "attend_back", pairs, (),
         [
-            (queries, lane_block(4 * ROWS)), (keys, lane_block(8 * ROWS)),
-            (values, lane_block(8 * ROWS)), (probs, probs_block()),
+            (queries, lane_block(4 * ROWS, start)), (keys, lane_block(8 * ROWS, start)),
+            (values, lane_block(8 * ROWS, start)), (probs, probs_block(start)),
         ]
-        + [(grad, lane_block(ROWS)) for grad in grads],
+        + [(grad, lane_block(ROWS, start)) for grad in grads],
         [
-            ((4 * ROWS, 256), BF, lane_block(4 * ROWS)),
-            ((8 * ROWS, 256), BF, lane_block(8 * ROWS)),
-            ((8 * ROWS, 256), BF, lane_block(8 * ROWS)),
+            ((4 * ROWS, 128 * pairs), BF, lane_block(4 * ROWS)),
+            ((8 * ROWS, 128 * pairs), BF, lane_block(8 * ROWS)),
+            ((8 * ROWS, 128 * pairs), BF, lane_block(8 * ROWS)),
         ],
-        (), (8, 10),
-    )
-
-
-def attend_last(info, xs, ws, queries, keys, values, probs, grads, parts):
+        (), (4 * pairs, 5 * pairs),
+    )
+
+
+def by_name(pairs):
+    return [part for name in zip(*pairs) for part in name]
+
+
+def joint_grads(info, xs, pairs):
     joint = (2, 2, 112, 3 * HALF)
     return call(
-        attend_last_kernel, "attend_last", 1, (info,),
-        plain([xs, ws])
-        + [
-            (queries, lane_block(4 * ROWS, 2)), (keys, lane_block(8 * ROWS, 2)),
-            (values, lane_block(8 * ROWS, 2)), (probs, probs_block(2)),
-        ]
-        + [(grad, lane_block(ROWS, 2)) for grad in grads]
-        + plain(parts),
-        [((4 * ROWS, D), FP, None), ((4 * ROWS, D), BF, None), (joint, BF, None), (joint, BF, None)],
-        [
-            pltpu.VMEM((4 * ROWS, HALF), BF), pltpu.VMEM((8 * ROWS, HALF), BF),
-            pltpu.VMEM((8 * ROWS, HALF), BF), pltpu.VMEM((D, 3 * HALF), BF),
-        ],
-        (8, 10),
-    )
-
-
-def middle_one(info, ctx, rows, out_p, inner_weight, small):
+        joint_kernel, "joint_grads", 1, (info,), plain([xs, *by_name(pairs)]),
+        [(joint, BF, None), (joint, BF, None)],
+        [pltpu.VMEM((8 * ROWS, 3 * HALF), BF), pltpu.VMEM((D, 3 * HALF), BF)],
+    )
+
+
+def rows_back(ws, pairs):
+    return call(
+        rows_back_kernel, "rows_back", 1, (), plain([ws, *by_name(pairs)]),
+        [((4 * ROWS, D), FP, None), ((4 * ROWS, D), BF, None)],
+        [pltpu.VMEM((8 * ROWS, 3 * HALF), BF)],
+    )
+
+
+def middle_one(info, ctx, rows, out_p, inner_p):
     block = pl.BlockSpec((1, MIDDLE, D), lambda step, *_: (step, 0, 0))
     return call(
         middle_one_kernel, "middle_one", 4, (info,),
-        plain([*ctx, *rows, *out_p])
-        + [(inner_weight, pl.BlockSpec((D, D), lambda step, info: (0, (info[0] & 3) ^ step)))]
-        + plain(small),
+        plain([*ctx, *rows]) + first_columns(out_p) + anywhere(inner_p),
         [
             ((MIDDLE, D), FP, None), ((MIDDLE, D), FP, None), ((MIDDLE, 1), FP, None),
             ((4, MIDDLE, D), BF, block), ((4, MIDDLE, D), BF, block), ((8, D), FP, None),
         ],
         [
             pltpu.VMEM((4, MIDDLE, 192), BF), pltpu.VMEM((MIDDLE, D), BF),
-            pltpu.VMEM((4, 16, D), FP), pltpu.VMEM((4, 16, D), FP),
+            pltpu.VMEM((4, 16, D), FP), pltpu.VMEM((4, 16, D), FP), pltpu.VMEM((4, D, D), BF),
+            pltpu.SemaphoreType.DMA((4, 4)),
         ],
         (4, 10),
     )
@@ -1041,23 +1102,31 @@
             (blocks, BF, pl.BlockSpec((1, 4, 192, D), lambda s, *_: (jnp.maximum(s - 3, 0), 0, 0, 0))),
             (blocks, BF, pl.BlockSpec((1, 4, 192, D), lambda s, *_: (jnp.where(s < 2, 0, 1), 0, 0, 0))),
         ],
-        [pltpu.VMEM((4, D, D), BF), pltpu.SemaphoreType.DMA((4,))], (4, 10),
-    )
-
-
-def middle_three(info, outer, second, slope, normed, inv, vec, inner_weight, out_p, outer_p):
+        [pltpu.VMEM((4, D, D), BF), pltpu.SemaphoreType.DMA((6,))], (4, 10),
+    )
+
+
+def inner_back(info, outer, slope, outer_p):
+    return call(
+        inner_back_kernel, "inner_back", 1, (info,), plain([outer, slope]) + anywhere(outer_p),
+        [((4, MIDDLE, D), BF, None), ((4, D), FP, None)],
+        [pltpu.VMEM((4, D, D), BF), pltpu.SemaphoreType.DMA((6,))], (2, 7),
+    )
+
+
+def middle_three(info, second, inner, normed, inv, vec, out_p, inner_p):
     return call(
         middle_three_kernel, "middle_three", 1, (info,),
-        plain([outer, second, slope, normed, inv, vec]) + anywhere([inner_weight, *out_p, *outer_p]),
+        plain([second, inner, normed, inv, vec]) + anywhere([*out_p, *inner_p]),
         [((MIDDLE, D), FP, None)]
         + [((ROWS, HALF), BF, None)] * 4
-        + [((4, MIDDLE, D), BF, None), ((MIDDLE, D), BF, None), ((16, D), FP, None)],
+        + [((MIDDLE, D), BF, None), ((8, D), FP, None)],
         [
-            pltpu.VMEM((4, 192, D), BF), pltpu.VMEM((4, D, D), BF), pltpu.VMEM((4, D, D), BF),
+            pltpu.VMEM((4, 192, D), BF), pltpu.VMEM((4, D, D), BF),
             pltpu.VMEM((4, MIDDLE, 192), BF), pltpu.SemaphoreType.DMA((4,)),
-            pltpu.SemaphoreType.DMA((4,)), pltpu.SemaphoreType.DMA((4,)),
+            pltpu.SemaphoreType.DMA((4, 4)),
         ],
-        (4, 14),
+        (2, 7),
     )
 
 
@@ -1083,29 +1152,41 @@
         out[pl.ds(pl.multiple_of(192 * (n ^ (2 * (z & 1) + x)), 64), 192), :] = wide(piece[...])
 
 
-def place_inner_kernel(info, p0, p1, p2, p3, inner, out, vec):
+def place_inner_kernel(
+    info, p0, p1, p2, p3, inner, out, b_in, b_out, g_one, s_one, b_two, g_two, s_two, held
+):
     z, x, _, _, _, _ = coords(info)
     for n, piece in enumerate((p0, p1, p2, p3)):
         at = n ^ (2 * x + (z & 1))
         inner[:, pl.ds(pl.multiple_of(D * at, 128), D)] = wide(piece[:192, :])
         out[pl.ds(pl.multiple_of(48 * at, 16), 48), :] = wide(piece[192:240, :])
-        vec[at] = wide(piece[240:, :])
-
-
-def place_joint_kernel(info, p0, p1, p2, p3, query, key, value, vec):
-    z, x, _, _, _, _ = coords(info)
+        held[at] = wide(piece[240:, :])
+    b_in[...] = held[0][0:1, :].reshape(D)
+    for n, vector in enumerate((b_out, g_one, s_one, b_two, g_two, s_two)):
+        cut = 192 * (n % 4)
+        vector[...] = held[1 + n // 4][0:1, cut : cut + 192].reshape(192)
+
+
+def place_joint_kernel(info, p0, p1, p2, p3, query, key, value, b_query, b_value, held):
+    z, x, _, _, _, f = coords(info)
     z_bit = z & 1
     for n, piece in enumerate((p0, p1, p2, p3)):
         rows = pl.ds(pl.multiple_of(96 * (n % 2 ^ z_bit), 32), 96)
         columns = pl.ds(pl.multiple_of(HALF * (n // 2 ^ x), 128), HALF)
         for m, out in enumerate((query, key, value)):
             out[rows, columns] = wide(piece[:96, HALF * m : HALF * m + HALF])
-        vec[n // 2 ^ x, n % 2 ^ z_bit] = wide(piece[96:, :])
-
-
-def placed(kernel, name, info, pieces, shapes):
+        line = wide(piece[96:, :])
+        line = jnp.where(f & 1 == 0, line, jnp.concatenate([line[:, 192:], line[:, :192]], axis=1))
+        held[n // 2 ^ x, n % 2 ^ z_bit] = line
+    mine = held[f >> 1, 0][0:1, :]
+    b_query[...] = mine[:, :192].reshape(192)
+    b_value[...] = mine[:, 2 * HALF : 2 * HALF + 192].reshape(192)
+
+
+def placed(kernel, name, info, pieces, shapes, held=()):
     return call(
-        kernel, name, 1, (info,), plain(pieces), [(shape, FP, None) for shape in shapes], (), (1, 6)
+        kernel, name, 1, (info,), plain(pieces), [(shape, FP, None) for shape in shapes],
+        [pltpu.VMEM(shape, FP) for shape in held], (1, 6),
     )
 
 
@@ -1115,11 +1196,6 @@
 
 def tied(values, *events):
     return lax.optimization_barrier((values, events))[0]
-
-
-def z_level(low_half):
-    one = low(wide(low_half) + wide(swap_z2(low_half)))
-    return one
 
 
 def fast_body(
@@ -1127,136 +1203,133 @@
     gain_one, bias_one, w_inner, b_inner, w_outer, b_outer, gain_two, bias_two,
 ):
     info = lax.axis_index(("ctx", "fsdp")).astype(jnp.int32).reshape(1)
-    f = lax.axis_index("fsdp")
     zh = lax.axis_index("ctx") // 4
 
-    inner_weight = lax.all_gather(w_inner, "fsdp", axis=0, tiled=True)
-    t0, t1, cot, w_x, small = pack(
-        info, lengths, inputs, cotangent, (w_query, w_key, w_value),
+    t0, t1, cot, first = pack(
+        info, lengths, inputs, cotangent, (w_query, w_key, w_value, w_output),
         (b_query, b_value, b_output, gain_one, bias_one, b_outer, gain_two, bias_two, b_inner),
     )
 
     bu, bv = seq_send[0](t0), seq_send[1](t1)
-    w_y, small_y, out_y = swap_y(w_x), swap_y(small), swap_y(tied(w_output, t0))
-    bu, bv, small_y = tied((bu, bv, small_y))
-    bxu, bxv = swap_x(bu), swap_x(bv)
-    bku, bkv = swap_core(bu), swap_core(bv)
-    bku, bkv, bxu, bxv, w_y, out_y = tied((bku, bkv, bxu, bxv, w_y, out_y))
-    outer_y = swap_y(tied(w_outer, out_y))
-    rest = [swap_core(b) for b in (bxu, bxv)] + [swap_core(tied(w_x, w_y)), swap_core(w_y)]
-    rest, small_y = tied((rest, small_y))
-    small_k, small_ky = swap_core(tied(small, rest)), swap_core(small_y)
-    blocks = [bu, bv, bxu, bxv, bku, bkv, rest[0], rest[1]]
-    qkv_p = [w_x, rest[2], w_y, rest[3]]
-    smalls = [small, small_k, small_y, small_ky]
-
-    xs, ws, queries, keys, values, probs, cu, cv, cxu, cxv = attend(info, blocks, qkv_p, smalls)
+    first_y, first_k = swap_y(first), swap_core(first)
+    bu, bv, first_k = tied((bu, bv, first_k))
+    bxu, bxv, bku = swap_x(bu), swap_x(bv), swap_core(bu)
+    inner_y = swap_y(tied(w_inner, bu))
+    bxu, bxv, bku, first_y = tied((bxu, bxv, bku, first_y))
+    w_cut = w_outer.reshape(2, D // 2, D)
+    outer_y1 = swap_y(tied(w_cut[0], first_y))
+    bkv, *rest = [swap_core(b) for b in (bv, bxu, bxv, first_y)]
+    bkv, *rest = tied([bkv] + rest)
+    blocks = [bu, bv, bxu, bxv, bku, bkv, *rest[:2]]
+    first_p = [first, first_k, first_y, rest[2]]
+    xs, ws, queries, keys, values, probs, cu, cv, cx = attend(info, blocks, first_p)
 
     cu, cv = seq_return[0](cu), seq_return[1](cv)
-    cxu, cxv = swap_x(cxu), swap_x(cxv)
-    cu, cv, cxu, cxv = tied((cu, cv, cxu, cxv))
-    cxu, cxv = seq_return[0](cxu), seq_return[1](cxv)
-    out_k, out_ky = swap_core(tied(w_output, cu)), swap_core(tied(out_y, cu))
-    cxu, cxv, out_k, out_ky, outer_y = tied((cxu, cxv, out_k, out_ky, outer_y))
+    cx = swap_x(cx)
+    cu, cv, cx, inner_y, outer_y1 = tied((cu, cv, cx, inner_y, outer_y1))
+    outer_y2 = swap_y(tied(w_cut[1], outer_y1))
+    cxu, cxv = seq_return[0](cx[0]), seq_return[1](cx[1])
+    inner_k, inner_ky = swap_core(tied(w_inner, cx)), swap_core(inner_y)
+    cxu, cxv, inner_k, inner_ky, outer_y2 = tied((cxu, cxv, inner_k, inner_ky, outer_y2))
     ctx = [cu, cv, cxu, cxv]
-    out_p = [w_output, out_k, out_y, out_ky]
-    outer_k, outer_ky = swap_core(tied(w_outer, cxu)), swap_core(outer_y)
-
-    hidden, normed, inv, act, slope, vec = middle_one(
-        info, ctx, [t0, t1], out_p, inner_weight, smalls
-    )
-    outer_p = [w_outer, outer_k, outer_y, outer_ky]
-    outputs, second, outer, sums_two, o_keep, o_send = middle_two(
+    inner_p = [w_inner, inner_k, inner_y, inner_ky]
+    outer_k = swap_core(tied(w_outer, cxu))
+    outer_ky1, outer_ky2 = swap_core(tied(outer_y1, cxu)), swap_core(outer_y2)
+    hidden, normed, inv, act, slope, vec = middle_one(info, ctx, [t0, t1], first_p, inner_p)
+    act, outer_k, outer_ky1, outer_ky2 = tied((act, outer_k, outer_ky1, outer_ky2))
+    outer_p = [w_outer, outer_k, outer_y1, outer_y2, outer_ky1, outer_ky2]
+    outputs, second_grad, outer, sums_two, o_keep, o_send = middle_two(
         info, lengths, act, hidden, cot, vec, outer_p
     )
     o_came = swap_core(o_send)
-    grad_first, gm0, gm1, go0, go1, inner, branch, sums_one = middle_three(
-        info, outer, second, slope, normed, inv, vec, inner_weight, out_p, outer_p
+    inner, sums_in = inner_back(info, outer, slope, outer_p)
+    o_came, inner = tied((o_came, inner))
+    o_far = low(wide(o_keep[1]) + wide(o_came[1]))
+    o_near = wide(o_keep[0]) + wide(o_came[0])
+    inner, o_far, o_near = tied((inner, o_far, o_near))
+    o_came = swap_y(o_far[1:])
+    grad_first, gm0, gm1, go0, go1, branch, sums_one = middle_three(
+        info, second_grad, inner, normed, inv, vec, first_p, inner_p
     )
     go0, go1 = seq_send[0](go0), seq_send[1](go1)
     gm0, gm1 = seq_send[0](gm0), seq_send[1](gm1)
-    o_far = low(wide(o_keep[1]) + wide(o_came[1]))
-    o_near = wide(o_keep[0]) + wide(o_came[0])
-    o_came = swap_y(o_far[2:])
-    inner, o_far, o_near = tied((inner, o_far, o_near))
-    i_keep, i_send = middle_four(info, inner, hidden, branch, ctx, (sums_two, sums_one))
+    i_keep, i_send = middle_four(
+        info, inner, hidden, branch, ctx, (sums_two, sums_in, sums_one)
+    )
     go0, go1, gm0, gm1, i_send, o_came = tied((go0, go1, gm0, gm1, i_send, o_came))
     go0, go1 = swap_x(go0), swap_x(go1)
     i_came = swap_core(i_send)
-    o_zed = swap_z1(low(o_near[2:] + wide(o_came)))
-    o_came = swap_y(tied(o_far[:2], o_came))
-    go0, go1, i_came = tied((go0, go1, i_came))
+    o_zed = swap_z1(low(o_near[2:] + wide(o_came[1:])))
+    o_last = swap_y(tied(o_far[:1], o_came))
+    go0, go1, i_came, o_last = tied((go0, go1, i_came, o_last))
     i_far = low(wide(i_keep[1, 2:]) + wide(i_came[1, 2:]))
     i_far2 = low(wide(i_keep[1, :2]) + wide(i_came[1, :2]))
     i_near = wide(i_keep[0]) + wide(i_came[0])
     grads, i_far, i_far2, i_near = tied(([gm0, gm1, go0, go1], i_far, i_far2, i_near))
-    parts = attend_back(queries, keys, values, probs, grads)
     i_came = swap_y(i_far)
-    parts, o_came, o_zed = tied((parts, o_came, o_zed))
-    o_sum = o_near[:2] + wide(o_came) + wide(o_zed)
-    o_came = swap_x(low(o_sum[1]))
-    dx_own, dx_other, j_keep, j_send = attend_last(
-        info, xs, ws, queries, keys, values, probs, grads, tied(parts, o_sum)
-    )
-    dx_own, dx_other, j_keep, j_send, o_came, i_came = tied(
-        (dx_own, dx_other, j_keep, j_send, o_came, i_came)
-    )
-    dx_came, j_came = swap_core(dx_other), swap_core(j_send)
+    pair_0 = attend_back(queries, keys, values, probs, grads, 0, 1)
+    pair_0, o_zed = tied((pair_0, o_zed))
+    o_one = o_near[1] + wide(o_came[0]) + wide(o_zed[1])
+    o_sum = o_near[0] + wide(o_last[0]) + wide(o_zed[0])
+    o_came = swap_x(low(o_one))
+    pair_1 = attend_back(tied(queries, o_one), keys, values, probs, grads, 1, 1)
+    pair_1, o_came, i_came = tied((pair_1, o_came, i_came))
+    o_sum = low(o_sum + wide(o_came))
     i_sum = i_near[2:] + wide(i_came)
-    o_sum = low(o_sum[0] + wide(o_came))
+    o_came = swap_z2(o_sum)
     i_came = swap_x(low(i_sum))
     i_came2 = swap_y(tied(i_far2, i_sum))
-    o_came = swap_z2(o_sum)
-    dx_came, j_came = tied((dx_came, j_came))
-    dx = dx_own + wide(dx_came)
+    pair_2 = attend_back(tied(queries, o_sum, i_sum), keys, values, probs, grads, 2, 1)
+    pairs = (pair_0, pair_1, pair_2)
+    dx_own, dx_other = rows_back(ws, pairs)
+    j_keep, j_send = joint_grads(info, tied(xs, dx_other), pairs)
+    dx_own, dx_other, j_keep, j_send, i_came, i_came2, o_came = tied(
+        (dx_own, dx_other, j_keep, j_send, i_came, i_came2, o_came)
+    )
+    j_came, dx_came = swap_core(j_send), swap_core(dx_other)
+    o_sum = low(wide(o_sum) + wide(o_came))
+    i_sum = i_near[:2] + wide(i_came2) + wide(i_came)
+    j_came, dx_came, o_sum, i_sum = tied((j_came, dx_came, o_sum, i_sum))
     j_far = low(wide(j_keep[1]) + wide(j_came[1]))
     j_near = wide(j_keep[0]) + wide(j_came[0])
-    dx_came = swap_x(low(dx[2 * ROWS :]))
-    i_came, i_came2, dx_came, o_came = tied((i_came, i_came2, dx_came, o_came))
-    j_came = swap_y(tied(j_far, i_came2))
-    o_sum = low(wide(o_sum) + wide(o_came))
-    i_sum = i_near[:2] + wide(i_came2) + wide(i_came)
-    dx = low(dx[: 2 * ROWS] + wide(dx_came))
+    dx = dx_own[: 2 * ROWS] + wide(dx_came[: 2 * ROWS])
+    dx_send = low(dx_own[2 * ROWS :] + wide(dx_came[2 * ROWS :]))
+    j_came = swap_y(j_far)
     i_came = swap_z1(low(i_sum[1]))
-    dx0, dx1 = seq_return[0](dx[:ROWS]), seq_return[1](dx[ROWS:])
-    o_x = swap_x(o_sum)
-    i_came, dx0, dx1, j_came, o_x = tied((i_came, dx0, dx1, j_came, o_x))
+    dx_came = swap_x(dx_send)
+    j_came, i_came, dx_came = tied((j_came, i_came, dx_came))
+    j_sum = j_near + wide(j_came)
     i_sum = low(i_sum[0] + wide(i_came))
-    j_sum = j_near + wide(j_came)
+    dx = low(dx + wide(dx_came))
+    j_came = swap_z1(low(j_sum[1]))
+    i_came = swap_z2(i_sum)
+    o_x = swap_x(tied(o_sum, i_sum))
+    j_came, o_x = tied((j_came, o_x))
+    j_sum = low(j_sum[0] + wide(j_came))
+    j_came = swap_z2(j_sum)
+    o_z, o_zx = swap_z1(tied(o_sum, j_sum)), swap_z1(tied(o_x, j_sum))
+    i_came, o_z, o_zx = tied((i_came, o_z, o_zx))
+    i_sum = low(wide(i_sum) + wide(i_came))
+    i_z, i_x = swap_z1(i_sum), swap_x(i_sum)
+    j_came, i_sum = tied((j_came, i_sum))
+    j_sum = low(wide(j_sum) + wide(j_came))
+    j_x, j_z = swap_x(j_sum), swap_z1(j_sum)
+    (outer_grad,) = placed(
+        place_outer_kernel, "place_outer", info, tied([o_sum, o_x, o_z, o_zx], j_sum), [(D, D)]
+    )
+    i_z, i_x, j_x, j_z, outer_grad = tied((i_z, i_x, j_x, j_z, outer_grad))
+    i_zx, j_zx = swap_x(i_z), swap_z1(j_x)
+    dx0, dx1 = seq_return[0](tied(dx[:ROWS], i_z)), seq_return[1](tied(dx[ROWS:], i_z))
     input_grad = grad_first + wide(jnp.concatenate([dx0, dx1], axis=0))
     input_grad = unshuffle(input_grad.reshape(2, ROWS, D), zh)
-    i_came = swap_z2(i_sum)
-    j_came = swap_z1(low(j_sum[1]))
-    o_z, o_zx = swap_z1(o_sum), swap_z1(o_x)
-    j_came, i_came, o_z, o_zx = tied((j_came, i_came, o_z, o_zx))
-    j_sum = low(j_sum[0] + wide(j_came))
-    i_sum = low(wide(i_sum) + wide(i_came))
-    (outer_grad,) = placed(place_outer_kernel, "place_outer", info, [o_sum, o_x, o_z, o_zx], [(D, D)])
-    j_came = swap_z2(j_sum)
-    i_z, i_x = swap_z1(i_sum), swap_x(i_sum)
-    j_came, i_z, i_x = tied((j_came, i_z, i_x))
-    j_sum = low(wide(j_sum) + wide(j_came))
-    i_zx = swap_x(i_z)
-    j_z, j_x = swap_z1(j_sum), swap_x(j_sum)
-    j_z, j_x, i_zx = tied((j_z, j_x, i_zx))
-    j_zx = swap_x(j_z)
-    inner_grad, out_grad, lines = placed(
+    inner_grad, out_grad, grad_b1, grad_bo, grad_g1, grad_s1, grad_b2, grad_g2, grad_s2 = placed(
         place_inner_kernel, "place_inner", info, [i_sum, i_z, i_x, i_zx],
-        [(192, 4 * D), (192, D), (4, 16, D)],
-    )
-    q_grad, k_grad, v_grad, joint_lines = placed(
+        [(192, 4 * D), (192, D), (D,)] + [(192,)] * 6, [(4, 16, D)],
+    )
+    q_grad, k_grad, v_grad, grad_bq, grad_bv = placed(
         place_joint_kernel, "place_joint", info, [j_sum, j_z, j_x, j_zx],
-        [(192, D)] * 3 + [(2, 2, 16, 3 * HALF)],
-    )
-    grad_b1 = lines[0, 0]
-    grad_bo, grad_g1, grad_s1, grad_b2 = (lines[1, 0, 192 * n : 192 * n + 192] for n in range(4))
-    grad_g2, grad_s2 = (lines[2, 0, 192 * n : 192 * n + 192] for n in range(2))
-    joint_sums = joint_lines[:, 0, 0]
-
-    def own(vector):
-        return lax.dynamic_slice_in_dim(vector.reshape(D), f * 192, 192)
-
-    grad_bq, grad_bv = own(joint_sums[:, :HALF]), own(joint_sums[:, 2 * HALF :])
+        [(192, D)] * 3 + [(192,)] * 2, [(2, 2, 16, 3 * HALF)],
+    )
     return (
         outputs, input_grad, q_grad, grad_bq, k_grad, v_grad, grad_bv, out_grad, grad_bo,
         grad_g1, grad_s1, inner_grad, grad_b1, outer_grad, grad_b2, grad_g2, grad_s2,

time: 317 us -> 288 us (0.909)
  waiting for transfers between devices: 126 us -> 111 us
  between operations: 14.8 us -> 1.32 us
  Pallas kernels: 84.2 us -> 96 us
  starting transfers between devices: 70.8 us -> 59.9 us
  local copies, waits for them, and re-layouts: 11.1 us -> 6.96 us
  other arithmetic: 8.71 us -> 12.3 us
    pallas_call x11 -> x15, Pallas kernels: 84.2 us -> 96 us  [call(): pl.pallas_call(kernel, out_shape=[jax.ShapeDtypeStruct(shape, kind) for s...]
    ppermute x55 -> x53, starting transfers between devices: 60 us -> 48.4 us  [permute(): return lambda block: lax.ppermute(block, ('ctx', 'fsdp'), pairs)]
    ppermute x6, waiting for transfers between devices: 17.1 us -> 9.53 us  [permute_back(): return lambda block: lax.ppermute(block, ('ctx', 'fsdp'), pairs)]
    ppermute x55 -> x53, waiting for transfers between devices: 108 us -> 101 us  [permute(): return lambda block: lax.ppermute(block, ('ctx', 'fsdp'), pairs)]
    slice x8 -> x4, local copies, waits for them, and re-layouts: 4.63 us -> 0.18 us  [the longest x1 0.08 us: fast_body(): outer_y2 = swap_y(tied(w_cut[1], outer_y1))]
    convert_element_type x10 -> x11, other arithmetic: 1.95 us -> 5.54 us  [low(): return value.astype(jnp.bfloat16)]
    unnamed x97 -> x92, local copies, waits for them, and re-layouts: 5.12 us -> 6.68 us
  transfers between devices with their start and end apart: 62 -> 59, of which waited for: 22 -> 28; matrix products, arithmetic and copies ran while one was open for 3% -> 3% of each run, Pallas kernels for 22% -> 27%
where the time goes in v3:
time: 288 us; the launch traced here: 287 us
  waiting for transfers between devices  111 us (39%)
  Pallas kernels  96 us (33%)
  starting transfers between devices  59.9 us (21%)
  other arithmetic  12.3 us (4%)
  local copies, waits for them, and re-layouts  6.96 us (2%)
    ppermute x53, waiting for transfers between devices, permute(): return lambda block: lax.ppermute(block, ('ctx', 'fsdp'), pairs)  101 us
    pallas_call x15, Pallas kernels, call(): pl.pallas_call(kernel, out_shape=[jax.ShapeDtypeStruct(shape, kind) for s...  96 us
    ppermute x53, starting transfers between devices, permute(): return lambda block: lax.ppermute(block, ('ctx', 'fsdp'), pairs)  48.4 us
    ppermute x6, starting transfers between devices, permute_back(): return lambda block: lax.ppermute(block, ('ctx', 'fsdp'), pairs)  11.4 us
    ppermute x6, waiting for transfers between devices, permute_back(): return lambda block: lax.ppermute(block, ('ctx', 'fsdp'), pairs)  9.53 us
    unnamed x92, local copies, waits for them, and re-layouts  6.68 us
  transfers between devices with their start and end apart: 59, of which 28 were waited for; matrix products, arithmetic and copies ran while one was open for 3% of the time, Pallas kernels for 27%

profile of v3, /device:TPU:0, one launch (start us, length us, event | category | flops | bytes accessed | tf_op | source)
XLA Modules:
  0.0 287.3 jit_solution(5469918949082467750)
XLA Ops:
  0.7 3.5 %pack.1 = (bf16[128,768]{1,0:T(8,128)(2,1)}, bf16[128,768]{1,0:T(8,128)(2,1)}, bf16[256,768]{1,0:T(8,128)(2,1)}, bf16[208,1920]{1,0:T(8,128)(2,1)}) custom-call(s32[1]{0:T(128)} %bitcast.info, s32[2]{0:T(128)} %lens.3, bf16[2,128,768]{2,1,0:T(8,128)(2,1)} %rows.1, bf16[2,128,768]{2,1,0:T(8,128)(2,1)} %grads.1, bf16[192,768]{1,0:T(8,128)(2,1)} %w_q.1, ...), custom_call_target="tpu_custom_call" | custom-call | flops 1000 | bytes 1000 | tf_op jit(solution)/shard_map/pack/pallas_call | solution.py:964
  11.0 11.3 %collective-permute-done.1.b1 = bf16[128,768]{1,0:T(8,128)(2,1)S(1)} collective-permute-done((bf16[128,768]{1,0:T(8,128)(2,1)}, bf16[128,768]{1,0:T(8,128)(2,1)S(1)}, u32[]{:S(2)}, u32[]{:S(2)}) %collective-permute-start.1) | collective-permute-done | bytes 196640 | tf_op jit(solution)/shard_map/ppermute | solution.py:523
  37.9 14.7 %attend.1 = (bf16[1024,768]{1,0:T(8,128)(2,1)}, bf16[768,1152]{1,0:T(8,128)(2,1)}, bf16[512,384]{1,0:T(8,128)(2,1)}, bf16[1024,384]{1,0:T(8,128)(2,1)}, bf16[102...) custom-call(s32[1]{0:T(128)} %bitcast.info, ...), custom_call_target="tpu_custom_call" | custom-call | flops 1000 | bytes 1000 | tf_op jit(solution)/shard_map/attend/pallas_call | solution.py:964
  58.5 6.9 %collective-permute-done.15.w2 = bf16[384,768]{1,0:T(8,128)(2,1)S(1)} collective-permute-done((bf16[384,768]{1,0:T(8,128)(2,1)S(1)}, bf16[384,768]{1,0:T(8,128)(2,1)S(1)}, u32[]{:S(2)}, u32[]{:S(2)}) %collective-permute-start.15) | collective-permute-done | bytes 589856 | tf_op jit(solution)/shard_map/ppermute | solution.py:523
  72.3 9.7 %collective-permute-done.20.w3 = bf16[384,768]{1,0:T(8,128)(2,1)S(1)} collective-permute-done((bf16[384,768]{1,0:T(8,128)(2,1)S(1)}, bf16[384,768]{1,0:T(8,128)(2,1)S(1)}, u32[]{:S(2)}, u32[]{:S(2)}) %collective-permute-start.20) | collective-permute-done | bytes 589856 | tf_op jit(solution)/shard_map/ppermute | solution.py:523
  83.5 7.8 %middle_one.1 = (f32[256,768]{1,0:T(8,128)}, f32[256,768]{1,0:T(8,128)}, f32[256,1]{1,0:T(8,128)}, bf16[4,256,768]{2,1,0:T(8,128)(2,1)}, bf16[4,256,768]{2,1,0:T(8,128)(2,1)}, /*index=5*/f32[8,768]{1,0:T(8,128)}) custom-call(s32[1]{0:T(128)} %bitcast.info, bf16[128,384]{1,0:T(8,128)(2,1)} %copy-done.25, bf16[128,384]{1,0:T(8,128)(2,1)} %copy-done.26, ...), custom_call_target="tpu_custom_call" | custom-call | flops 1000 | bytes 1000 | tf_op jit(solution)/shard_map/middle_one/pallas_call | solution.py:964
  92.8 12.1 %middle_two.1 = (bf16[2,128,768]{2,1,0:T(8,128)(2,1)}, f32[256,768]{1,0:T(8,128)}, bf16[256,768]{1,0:T(8,128)(2,1)}, f32[8,768]{1,0:T(8,128)}, bf16[2,4,192,768]...) custom-call(s32[1]{0:T(128)} %bitcast.info, s32[2]{0:T(128)} %lens.3, ...), custom_call_target="tpu_custom_call" | custom-call | flops 1000 | bytes 1000 | tf_op jit(solution)/shard_map/middle_two/pallas_call | solution.py:964
  105.0 6.7 %inner_back.1 = (bf16[4,256,768]{2,1,0:T(8,128)(2,1)}, f32[4,768]{1,0:T(4,128)}) custom-call(s32[1]{0:T(128)} %bitcast.info, bf16[256,768]{1,0:T(8,128)(2,1)} %get-tuple-element.226.outer, bf16[4,256,768]{2,1,0:T(8,128)(2,1)} %get-tuple-element.227.slope, bf16[768,768]{1,0:T(8,128)(2,1)} %w0.3, bf16[768,768]{1,0:T(8,128)(2,1)} %copy-done.8, ...), custom_call_target="tpu_custom_call" | custom-call | flops 1000 | bytes 1000 | tf_op jit(solution)/shard_map/inner_back/pallas_call | solution.py:964
  112.9 7.9 %middle_three.1 = (f32[256,768]{1,0:T(8,128)}, bf16[128,384]{1,0:T(8,128)(2,1)}, bf16[128,384]{1,0:T(8,128)(2,1)}, bf16[128,384]{1,0:T(8,128)(2,1)}, bf16[128,38...) custom-call(s32[1]{0:T(128)} %bitcast.info, f32[256,768]{1,0:T(8,128)} %get-tuple-element.224.second, ...), custom_call_target="tpu_custom_call" | custom-call | flops 1000 | bytes 1000 | tf_op jit(solution)/shard_map/middle_three/pallas_call | solution.py:964
  126.2 3.7 %collective-permute-start.28 = (bf16[128,384]{1,0:T(8,128)(2,1)}, bf16[128,384]{1,0:T(8,128)(2,1)S(1)}, u32[]{:S(2)}, u32[]{:S(2)}) collective-permute-start(bf16[128,384]{1,0:T(8,128)(2,1)} %get-tuple-element.244), channel_id=1, source_target_pairs={{0,8},{1,24},{2,10},{3,26},{4,12},{5,28},{6,14},{7,30},{8,9},{9,25... | collective-permute-start | bytes 294920 | tf_op jit(solution)/shard_map/ppermute | solution.py:523
  129.9 6.8 %middle_four.1 = (bf16[2,4,256,768]{3,2,1,0:T(8,128)(2,1)}, bf16[2,4,256,768]{3,2,1,0:T(8,128)(2,1)}) custom-call(s32[1]{0:T(128)} %bitcast.info, bf16[4,256,768]{2,1,0:T(8,128)(2,1)} %get-tuple-element.232.inner, f32[256,768]{1,0:T(8,128)} %get-tuple-element.217.hidden, bf16[256,768]{1,0:T(8,128)(2,1)} %get-tuple-element.245.branch, ...), custom_call_target="tpu_custom_call" | custom-call | flops 1000 | bytes 1000 | tf_op jit(solution)/shard_map/middle_four/pallas_call | solution.py:964
  150.5 5.7 %attend_back.3 = (bf16[512,128]{1,0:T(8,128)(2,1)}, bf16[1024,128]{1,0:T(8,128)(2,1)}, bf16[1024,128]{1,0:T(8,128)(2,1)}) custom-call(bf16[512,384]{1,0:T(8,128)(2,1)} %get-tuple-element.282.queries, bf16[1024,384]{1,0:T(8,128)(2,1)} %get-tuple-element.238.keys, bf16[1024,384]{1,0:T(8,128)(2,1)} %get-tuple-element.239.values, ...), custom_call_target="tpu_custom_call" | custom-call | flops 1000 | bytes 1000 | tf_op jit(solution)/shard_map/attend_back/pallas_call | solution.py:964
  158.8 5.7 %attend_back.4 = (bf16[512,128]{1,0:T(8,128)(2,1)}, bf16[1024,128]{1,0:T(8,128)(2,1)}, bf16[1024,128]{1,0:T(8,128)(2,1)}) custom-call(bf16[512,384]{1,0:T(8,128)(2,1)} %get-tuple-element.282.queries, bf16[1024,384]{1,0:T(8,128)(2,1)} %get-tuple-element.238.keys, bf16[1024,384]{1,0:T(8,128)(2,1)} %get-tuple-element.239.values, ...), custom_call_target="tpu_custom_call" | custom-call | flops 1000 | bytes 1000 | tf_op jit(solution)/shard_map/attend_back/pallas_call | solution.py:964
  165.1 3.8 %collective-permute-done.36 = bf16[2,256,768]{2,1,0:T(8,128)(2,1)} collective-permute-done((bf16[2,256,768]{2,1,0:T(8,128)(2,1)}, bf16[2,256,768]{2,1,0:T(8,128)(2,1)}, u32[]{:S(2)}, u32[]{:S(2)}) %collective-permute-start.36) | collective-permute-done | bytes 786464 | tf_op jit(solution)/shard_map/ppermute | solution.py:523
  174.9 5.7 %attend_back.5 = (bf16[512,128]{1,0:T(8,128)(2,1)}, bf16[1024,128]{1,0:T(8,128)(2,1)}, bf16[1024,128]{1,0:T(8,128)(2,1)}) custom-call(bf16[512,384]{1,0:T(8,128)(2,1)} %get-tuple-element.282.queries, bf16[1024,384]{1,0:T(8,128)(2,1)} %get-tuple-element.238.keys, bf16[1024,384]{1,0:T(8,128)(2,1)} %get-tuple-element.239.values, ...), custom_call_target="tpu_custom_call" | custom-call | flops 1000 | bytes 1000 | tf_op jit(solution)/shard_map/attend_back/pallas_call | solution.py:964
  180.6 5.3 %rows_back.1 = (f32[512,768]{1,0:T(8,128)}, bf16[512,768]{1,0:T(8,128)(2,1)}) custom-call(bf16[768,1152]{1,0:T(8,128)(2,1)} %get-tuple-element.236.ws, bf16[512,128]{1,0:T(8,128)(2,1)} %get-tuple-element.270.dq0, bf16[512,128]{1,0:T(8,128)(2,1)} %get-tuple-element.277.dq1, bf16[512,128]{1,0:T(8,128)(2,1)} %get-tuple-element.283.dq2, ...), custom_call_target="tpu_custom_call" | custom-call | flops 1000 | bytes 1000 | tf_op jit(solution)/shard_map/rows_back/pallas_call | solution.py:964
  185.9 5.5 %joint_grads.1 = (bf16[2,2,112,1152]{3,2,1,0:T(8,128)(2,1)}, bf16[2,2,112,1152]{3,2,1,0:T(8,128)(2,1)}) custom-call(s32[1]{0:T(128)} %bitcast.info, bf16[1024,768]{1,0:T(8,128)(2,1)} %get-tuple-element.293.xs, bf16[512,128]{1,0:T(8,128)(2,1)} %get-tuple-element.270.dq0, bf16[512,128]{1,0:T(8,128)(2,1)} %get-tuple-element.277.dq1, ...), custom_call_target="tpu_custom_call" | custom-call | flops 1000 | bytes 1000 | tf_op jit(solution)/shard_map/joint_grads/pallas_call | solution.py:964
  199.7 7.0 %collective-permute-done.43 = bf16[256,768]{1,0:T(8,128)(2,1)S(1)} collective-permute-done((bf16[256,768]{1,0:T(8,128)(2,1)S(1)}, bf16[256,768]{1,0:T(8,128)(2,1)S(1)}, u32[]{:S(2)}, u32[]{:S(2)}) %collective-permute-start.43) | collective-permute-done | bytes 393248 | tf_op jit(solution)/shard_map/ppermute | solution.py:523
  214.6 9.2 %collective-permute-done.46 = bf16[112,1152]{1,0:T(8,128)(2,1)S(1)} collective-permute-done((bf16[112,1152]{1,0:T(8,128)(2,1)S(1)}, bf16[112,1152]{1,0:T(8,128)(2,1)S(1)}, u32[]{:S(2)}, u32[]{:S(2)}) %collective-permute-start.46) | collective-permute-done | bytes 258080 | tf_op jit(solution)/shard_map/ppermute | solution.py:523
  226.2 7.1 %collective-permute-done.45 = bf16[256,768]{1,0:T(8,128)(2,1)S(1)} collective-permute-done((bf16[256,768]{1,0:T(8,128)(2,1)S(1)}, bf16[256,768]{1,0:T(8,128)(2,1)S(1)}, u32[]{:S(2)}, u32[]{:S(2)}) %collective-permute-start.45) | collective-permute-done | bytes 393248 | tf_op jit(solution)/shard_map/ppermute | solution.py:523
  233.3 8.5 %collective-permute-done.48.p2 = bf16[192,768]{1,0:T(8,128)(2,1)S(1)} collective-permute-done((bf16[192,768]{1,0:T(8,128)(2,1)S(1)}, bf16[192,768]{1,0:T(8,128)(2,1)S(1)}, u32[]{:S(2)}, u32[]{:S(2)}) %collective-permute-start.48) | collective-permute-done | bytes 294944 | tf_op jit(solution)/shard_map/ppermute | solution.py:523
  241.8 5.2 %collective-permute-done.49.p3 = bf16[192,768]{1,0:T(8,128)(2,1)S(1)} collective-permute-done((bf16[192,768]{1,0:T(8,128)(2,1)S(1)}, bf16[192,768]{1,0:T(8,128)(2,1)S(1)}, u32[]{:S(2)}, u32[]{:S(2)}) %collective-permute-start.49) | collective-permute-done | bytes 294944 | tf_op jit(solution)/shard_map/ppermute | solution.py:523
  256.5 6.4 %collective-permute-done.51.p2 = bf16[256,768]{1,0:T(8,128)(2,1)S(1)} collective-permute-done((bf16[256,768]{1,0:T(8,128)(2,1)S(1)}, bf16[256,768]{1,0:T(8,128)(2,1)S(1)}, u32[]{:S(2)}, u32[]{:S(2)}) %collective-permute-start.51) | collective-permute-done | bytes 393248 | tf_op jit(solution)/shard_map/ppermute | solution.py:523
  269.0 7.5 %collective-permute-done.56 = bf16[128,768]{1,0:T(8,128)(2,1)S(1)} collective-permute-done((bf16[128,768]{1,0:T(8,128)(2,1)S(1)}, bf16[128,768]{1,0:T(8,128)(2,1)S(1)}, u32[]{:S(2)}, u32[]{:S(2)}) %collective-permute-start.56) | collective-permute-done | bytes 196640 | tf_op jit(solution)/shard_map/ppermute | solution.py:528
  (227 shorter events, 112.2 us)
Async XLA Ops:
  4.2 18.1 %collective-permute-start.2 = (bf16[208,1920]{1,0:T(8,128)(2,1)}, bf16[208,1920]{1,0:T(8,128)(2,1)S(1)}, u32[]{:S(2)}, u32[]{:S(2)}) collective-permute-start(bf16[208,1920]{1,0:T(8,128)(2,1)} %get-tuple-element.184.s0.w0.o0), channel_id=1, source_target_pairs={{0,1},{1,0},{2,3},{3,2},{4,5},{5,4},{6,7},{7,6},{8,9},{9,8},{10,11... | collective-permute-start | bytes 2396168 | tf_op jit(solution)/shard_map/ppermute | solution.py:523
  4.7 21.2 %collective-permute-start.6 = (bf16[208,1920]{1,0:T(8,128)(2,1)}, bf16[208,1920]{1,0:T(8,128)(2,1)S(1)}, u32[]{:S(2)}, u32[]{:S(2)}) collective-permute-start(bf16[208,1920]{1,0:T(8,128)(2,1)} %get-tuple-element.184.s0.w0.o0), channel_id=1, source_target_pairs={{0,2},{1,3},{2,0},{3,1},{4,6},{5,7},{6,4},{7,5},{8,10},{9,11},{10,... | collective-permute-start | bytes 2396168 | tf_op jit(solution)/shard_map/ppermute | solution.py:523
  8.8 13.5 %collective-permute-start.1 = (bf16[128,768]{1,0:T(8,128)(2,1)}, bf16[128,768]{1,0:T(8,128)(2,1)S(1)}, u32[]{:S(2)}, u32[]{:S(2)}) collective-permute-start(bf16[128,768]{1,0:T(8,128)(2,1)} %get-tuple-element.183.x1), channel_id=1, source_target_pairs={{0,8},{1,24},{2,10},{3,26},{4,12},{5,28},{6,14},{7,30},{8,9},{9,25... | collective-permute-start | bytes 589832 | tf_op jit(solution)/shard_map/ppermute | solution.py:523
  24.4 41.0 %collective-permute-start.14 = (bf16[192,3072]{1,0:T(8,128)(2,1)}, bf16[192,3072]{1,0:T(8,128)(2,1)S(1)}, u32[]{:S(2)}, u32[]{:S(2)}) collective-permute-start(bf16[192,3072]{1,0:T(8,128)(2,1)} %i0.3), channel_id=1, source_target_pairs={{0,2},{1,3},{2,0},{3,1},{4,6},{5,7},{6,4},{7,5},{8,10},{9,11},{10,... | collective-permute-start | bytes 3538952 | tf_op jit(solution)/shard_map/ppermute | solution.py:523
  32.9 32.5 %collective-permute-start.15 = (bf16[384,768]{1,0:T(8,128)(2,1)S(1)}, bf16[384,768]{1,0:T(8,128)(2,1)S(1)}, u32[]{:S(2)}, u32[]{:S(2)}) collective-permute-start(bf16[384,768]{1,0:T(8,128)(2,1)S(1)} %get-tuple-element.200), channel_id=1, source_target_pairs={{0,2},{1,3},{2,0},{3,1},{4,6},{5,7},{6,4},{7,5},{8,10},{9,11},{10,... | collective-permute-start | bytes 1769480 | tf_op jit(solution)/shard_map/ppermute | solution.py:523
  66.1 15.9 %collective-permute-start.18 = (bf16[192,3072]{1,0:T(8,128)(2,1)S(1)}, bf16[192,3072]{1,0:T(8,128)(2,1)S(1)}, u32[]{:S(2)}, u32[]{:S(2)}) collective-permute-start(bf16[192,3072]{1,0:T(8,128)(2,1)S(1)} %copy-done.4), channel_id=1, source_target_pairs={{0,1},{1,0},{2,3},{3,2},{4,5},{5,4},{6,7},{7,6},{8,9},{9,8},{10,11... | collective-permute-start | bytes 3538952 | tf_op jit(solution)/shard_map/ppermute | solution.py:523
  66.2 15.8 %collective-permute-start.19 = (bf16[192,3072]{1,0:T(8,128)(2,1)S(1)}, bf16[192,3072]{1,0:T(8,128)(2,1)S(1)}, u32[]{:S(2)}, u32[]{:S(2)}) collective-permute-start(bf16[192,3072]{1,0:T(8,128)(2,1)S(1)} %collective-permute-done.14.i2), channel_id=1, source_target_pairs={{0,1},{1,0},{2,3},{3,2},{4,5},{5,4},{6,7},{7,6},{8,9},{9,8},{10,11... | collective-permute-start | bytes 3538952 | tf_op jit(solution)/shard_map/ppermute | solution.py:523
  66.7 15.3 %collective-permute-start.20 = (bf16[384,768]{1,0:T(8,128)(2,1)S(1)}, bf16[384,768]{1,0:T(8,128)(2,1)S(1)}, u32[]{:S(2)}, u32[]{:S(2)}) collective-permute-start(bf16[384,768]{1,0:T(8,128)(2,1)S(1)} %get-tuple-element.207), channel_id=1, source_target_pairs={{0,2},{1,3},{2,0},{3,1},{4,6},{5,7},{6,4},{7,5},{8,10},{9,11},{10,... | collective-permute-start | bytes 1769480 | tf_op jit(solution)/shard_map/ppermute | solution.py:523
  112.3 24.4 %collective-permute-start.29 = (bf16[3,192,768]{2,1,0:T(8,128)(2,1)S(1)}, bf16[3,192,768]{2,1,0:T(8,128)(2,1)S(1)}, u32[]{:S(2)}, u32[]{:S(2)}) collective-permute-start(bf16[3,192,768]{2,1,0:T(8,128)(2,1)S(1)} %slice.129), channel_id=1, source_target_pairs={{0,2},{1,3},{2,0},{3,1},{4,6},{5,7},{6,4},{7,5},{8,10},{9,11},{10,... | collective-permute-start | bytes 2654216 | tf_op jit(solution)/shard_map/ppermute | solution.py:523
  120.8 15.9 %collective-permute-start.25 = (bf16[128,384]{1,0:T(8,128)(2,1)}, bf16[128,384]{1,0:T(8,128)(2,1)S(1)}, u32[]{:S(2)}, u32[]{:S(2)}) collective-permute-start(bf16[128,384]{1,0:T(8,128)(2,1)} %get-tuple-element.241), channel_id=1, source_target_pairs={{0,0},{1,16},{2,2},{3,18},{4,4},{5,20},{6,6},{7,22},{8,1},{9,17},{... | collective-permute-start | bytes 294920 | tf_op jit(solution)/shard_map/ppermute | solution.py:523
  122.4 14.3 %collective-permute-start.26 = (bf16[128,384]{1,0:T(8,128)(2,1)}, bf16[128,384]{1,0:T(8,128)(2,1)S(1)}, u32[]{:S(2)}, u32[]{:S(2)}) collective-permute-start(bf16[128,384]{1,0:T(8,128)(2,1)} %get-tuple-element.242), channel_id=1, source_target_pairs={{0,8},{1,24},{2,10},{3,26},{4,12},{5,28},{6,14},{7,30},{8,9},{9,25... | collective-permute-start | bytes 294920 | tf_op jit(solution)/shard_map/ppermute | solution.py:523
  141.2 15.0 %collective-permute-start.34 = (bf16[2,192,768]{2,1,0:T(8,128)(2,1)}, bf16[2,192,768]{2,1,0:T(8,128)(2,1)}, u32[]{:S(2)}, u32[]{:S(2)}) collective-permute-start(bf16[2,192,768]{2,1,0:T(8,128)(2,1)} %add_convert_fusion.3), channel_id=1, source_target_pairs={{0,8},{1,9},{2,10},{3,11},{4,12},{5,13},{6,14},{7,15},{8,0},{9,1},... | collective-permute-start | bytes 1769480 | tf_op jit(solution)/shard_map/ppermute | solution.py:523
  149.8 19.1 %collective-permute-start.36 = (bf16[2,256,768]{2,1,0:T(8,128)(2,1)}, bf16[2,256,768]{2,1,0:T(8,128)(2,1)}, u32[]{:S(2)}, u32[]{:S(2)}) collective-permute-start(bf16[2,256,768]{2,1,0:T(8,128)(2,1)} %get-tuple-element.276), channel_id=1, source_target_pairs={{0,2},{1,3},{2,0},{3,1},{4,6},{5,7},{6,4},{7,5},{8,10},{9,11},{10,... | collective-permute-start | bytes 2359304 | tf_op jit(solution)/shard_map/ppermute | solution.py:523
  171.1 20.3 %collective-permute-start.38 = (bf16[2,256,768]{2,1,0:T(8,128)(2,1)S(1)}, bf16[2,256,768]{2,1,0:T(8,128)(2,1)S(1)}, u32[]{:S(2)}, u32[]{:S(2)}) collective-permute-start(bf16[2,256,768]{2,1,0:T(8,128)(2,1)S(1)} %get-tuple-element.297), channel_id=1, source_target_pairs={{0,2},{1,3},{2,0},{3,1},{4,6},{5,7},{6,4},{7,5},{8,10},{9,11},{10,... | collective-permute-start | bytes 2359304 | tf_op jit(solution)/shard_map/ppermute | solution.py:523
  171.6 19.8 %collective-permute-start.37 = (bf16[2,256,768]{2,1,0:T(8,128)(2,1)}, bf16[2,256,768]{2,1,0:T(8,128)(2,1)}, u32[]{:S(2)}, u32[]{:S(2)}) collective-permute-start(bf16[2,256,768]{2,1,0:T(8,128)(2,1)} %convert_add_fusion.1), channel_id=1, source_target_pairs={{0,4},{1,5},{2,6},{3,7},{4,0},{5,1},{6,2},{7,3},{8,12},{9,13},{10,... | collective-permute-start | bytes 2359304 | tf_op jit(solution)/shard_map/ppermute | solution.py:523
  174.2 17.2 %collective-permute-start.39 = (bf16[192,768]{1,0:T(8,128)(2,1)S(1)}, bf16[192,768]{1,0:T(8,128)(2,1)S(1)}, u32[]{:S(2)}, u32[]{:S(2)}) collective-permute-start(bf16[192,768]{1,0:T(8,128)(2,1)S(1)} %fusion.4), channel_id=1, source_target_pairs={{0,16},{1,17},{2,18},{3,19},{4,20},{5,21},{6,22},{7,23},{8,24},{9,... | collective-permute-start | bytes 884744 | tf_op jit(solution)/shard_map/ppermute | solution.py:523
  197.4 13.6 %collective-permute-start.42 = (bf16[2,112,1152]{2,1,0:T(8,128)(2,1)S(1)}, bf16[2,112,1152]{2,1,0:T(8,128)(2,1)S(1)}, u32[]{:S(2)}, u32[]{:S(2)}) collective-permute-start(bf16[2,112,1152]{2,1,0:T(8,128)(2,1)S(1)} %fusion.5), channel_id=1, source_target_pairs={{0,2},{1,3},{2,0},{3,1},{4,6},{5,7},{6,4},{7,5},{8,10},{9,11},{10,... | collective-permute-start | bytes 1548296 | tf_op jit(solution)/shard_map/ppermute | solution.py:523
  212.2 21.1 %collective-permute-start.45 = (bf16[256,768]{1,0:T(8,128)(2,1)S(1)}, bf16[256,768]{1,0:T(8,128)(2,1)S(1)}, u32[]{:S(2)}, u32[]{:S(2)}) collective-permute-start(bf16[256,768]{1,0:T(8,128)(2,1)S(1)} %fusion.3), channel_id=1, source_target_pairs={{0,16},{1,17},{2,18},{3,19},{4,20},{5,21},{6,22},{7,23},{8,24},{9,... | collective-permute-start | bytes 1179656 | tf_op jit(solution)/shard_map/ppermute | solution.py:523
  223.8 17.9 %collective-permute-start.48 = (bf16[192,768]{1,0:T(8,128)(2,1)S(1)}, bf16[192,768]{1,0:T(8,128)(2,1)S(1)}, u32[]{:S(2)}, u32[]{:S(2)}) collective-permute-start(bf16[192,768]{1,0:T(8,128)(2,1)S(1)} %add_convert_fusion.8.p0), channel_id=1, source_target_pairs={{0,8},{1,9},{2,10},{3,11},{4,12},{5,13},{6,14},{7,15},{8,0},{9,1},... | collective-permute-start | bytes 884744 | tf_op jit(solution)/shard_map/ppermute | solution.py:523
  223.9 23.1 %collective-permute-start.49 = (bf16[192,768]{1,0:T(8,128)(2,1)S(1)}, bf16[192,768]{1,0:T(8,128)(2,1)S(1)}, u32[]{:S(2)}, u32[]{:S(2)}) collective-permute-start(bf16[192,768]{1,0:T(8,128)(2,1)S(1)} %collective-permute-done.47.p1), channel_id=1, source_target_pairs={{0,8},{1,9},{2,10},{3,11},{4,12},{5,13},{6,14},{7,15},{8,0},{9,1},... | collective-permute-start | bytes 884744 | tf_op jit(solution)/shard_map/ppermute | solution.py:523
  225.9 21.2 %collective-permute-start.52 = (bf16[112,1152]{1,0:T(8,128)(2,1)S(1)}, bf16[112,1152]{1,0:T(8,128)(2,1)S(1)}, u32[]{:S(2)}, u32[]{:S(2)}) collective-permute-start(bf16[112,1152]{1,0:T(8,128)(2,1)S(1)} %fusion.7), channel_id=1, source_target_pairs={{0,16},{1,17},{2,18},{3,19},{4,20},{5,21},{6,22},{7,23},{8,24},{9,... | collective-permute-start | bytes 774152 | tf_op jit(solution)/shard_map/ppermute | solution.py:523
  248.9 14.0 %collective-permute-start.51 = (bf16[256,768]{1,0:T(8,128)(2,1)S(1)}, bf16[256,768]{1,0:T(8,128)(2,1)S(1)}, u32[]{:S(2)}, u32[]{:S(2)}) collective-permute-start(bf16[256,768]{1,0:T(8,128)(2,1)S(1)} %add_convert_fusion.5.p0), channel_id=1, source_target_pairs={{0,4},{1,5},{2,6},{3,7},{4,0},{5,1},{6,2},{7,3},{8,12},{9,13},{10,... | collective-permute-start | bytes 1179656 | tf_op jit(solution)/shard_map/ppermute | solution.py:523
  249.4 13.5 %collective-permute-start.50 = (bf16[256,768]{1,0:T(8,128)(2,1)S(1)}, bf16[256,768]{1,0:T(8,128)(2,1)S(1)}, u32[]{:S(2)}, u32[]{:S(2)}) collective-permute-start(bf16[256,768]{1,0:T(8,128)(2,1)S(1)} %add_convert_fusion.5.p0), channel_id=1, source_target_pairs={{0,8},{1,9},{2,10},{3,11},{4,12},{5,13},{6,14},{7,15},{8,0},{9,1},... | collective-permute-start | bytes 1179656 | tf_op jit(solution)/shard_map/ppermute | solution.py:523
  266.9 16.7 %collective-permute-start.58 = (bf16[256,768]{1,0:T(8,128)(2,1)S(1)}, bf16[256,768]{1,0:T(8,128)(2,1)S(1)}, u32[]{:S(2)}, u32[]{:S(2)}) collective-permute-start(bf16[256,768]{1,0:T(8,128)(2,1)S(1)} %collective-permute-done.50.p1), channel_id=1, source_target_pairs={{0,4},{1,5},{2,6},{3,7},{4,0},{5,1},{6,2},{7,3},{8,12},{9,13},{10,... | collective-permute-start | bytes 1179656 | tf_op jit(solution)/shard_map/ppermute | solution.py:523
  (81 other events, 742.3 us)
